TPU v7x, 32 devices: a whole 2x2x4 slice. The times are simulated.
32 devices in a mesh: cuts: 2 (over y), inter: 16 (over z, x, core).
Axes of the slice: x: 2, y: 2, z: 4, core: 2. Of those that a mesh axis runs over, the one named last changes fastest.
Arguments:
- stem_tensor: bfloat16 [2, 1024, 512, 1, 256], P(None, ('cuts', 'inter')), parts along dimension 1, may hold values from -6 to 6
- branch_one: bfloat16 [2, 512, 512], replicated, may hold values from -0.1875 to 0.1875
- branch_two: bfloat16 [2, 256, 256], replicated, may hold values from -0.25 to 0.25
- mode_order: int32 [256], replicated, may hold values from 0 to 255, each once
- branch_three: bfloat16 [2, 512, 512], replicated, may hold values from -0.1875 to 0.1875
- closing: bfloat16 [2, 512, 512], replicated, may hold values from -4 to 4
Outputs:
- amplitudes: float32 [1024, 512, 2, 1, 256], P(('cuts', 'inter')), parts along dimension 0
There are 2 independent parts, one for each index of `cuts`. A program takes and returns all parts, laid end to end along the dimension named above; an argument that names none is the same for every part. Nothing has to cross between parts.
All inputs are finite; a program needn't handle non-finite values.
Results may differ from a plain program's by a relative error of at most 0.0041.
Values may be sent and summed in bfloat16 or wider, within the bound.
No kernel may reach another device: no remote copies, remote signals or barrier semaphores. Data moves between devices by JAX's collectives and lax.ppermute only.
A program may use at most 192 MiB of HBM per device.

v0:
```python
import functools

import jax
import jax.numpy as jnp
import numpy as np
from jax import lax
from jax.experimental import pallas as pl
from jax.experimental.pallas import tpu as pltpu
from jax.sharding import PartitionSpec as P


B_CHUNKS = 2

ROWS = 8
STEP_ROWS = 2


def complex_mix(input_real, input_imag, weight_real, weight_imag, pattern):

    def product(first_op, second_op):
        return jnp.einsum(pattern, first_op, second_op, preferred_element_type=jnp.float32)

    return (
        product(input_real, weight_real) - product(input_imag, weight_imag),
        product(input_real, weight_imag) + product(input_imag, weight_real),
    )


def small_blocks(stem_tensor, branch_one, branch_two, mode_order, branch_three, closing):
    group_size = lax.axis_size("inter")
    my_index = lax.axis_index("inter")
    local_b = branch_three.shape[1] // group_size
    permuted = jnp.zeros_like(branch_two).at[:, mode_order, :].set(branch_two)
    close_cols = lax.dynamic_slice_in_dim(closing, my_index * local_b, local_b, 2).astype(
        jnp.float32
    )
    close_real = close_cols[0][:, :, None, None]
    close_imag = close_cols[1][:, :, None, None]
    received = lax.all_to_all(stem_tensor, "inter", split_axis=2, concat_axis=1, tiled=True)
    real_part, imag_part = complex_mix(
        received[0], received[1], branch_one[0], branch_one[1], "abkr,ac->cbkr"
    )
    phased = jnp.stack(
        [
            close_real * real_part - close_imag * imag_part,
            close_real * imag_part + close_imag * real_part,
        ]
    ).astype(jnp.bfloat16)
    real_two, imag_two = complex_mix(
        phased[0], phased[1], permuted[0], permuted[1], "abkr,rq->abkq"
    )
    second = jnp.stack([real_two, imag_two]).astype(jnp.bfloat16)
    returned = lax.all_to_all(second, "inter", split_axis=1, concat_axis=2, tiled=True)
    out_real, out_imag = complex_mix(
        returned[0], returned[1], branch_three[0], branch_three[1], "abkr,bc->ackr"
    )
    return jnp.stack([out_real, out_imag], axis=2)


MOVES = ((3, 2, 1, 0), (2, 0, 3, 1), (1, 3, 0, 2))


def rounds_of(group):
    quarters = 4 if group % 4 == 0 else 1
    turns = range(group // quarters)
    moves = MOVES if quarters == 4 else ()
    stay = tuple(range(quarters))
    near = [(stay, t) for t in turns]
    far = [(move, t) for move in moves for t in turns]
    return near[:1] + far[:1] + near[1:] + far[1:]


def inverse_of(rounds, group):
    return [
        (tuple(int(q) for q in np.argsort(move)), -turn % (group // len(move)))
        for move, turn in rounds
    ]


def pairs_of(move, turn, group):
    inner = group // len(move)
    return [
        (i, move[i // inner] * inner + (i % inner + turn) % inner) for i in range(group)
    ]


def partners(index, rounds, group):
    inner = group // len(rounds[0][0])
    quarter, place = index // inner, index % inner
    moved, turned = {}, {}
    for move, turn in rounds:
        if move not in moved:
            steps = [
                jnp.where(quarter == q, jnp.uint32(m * inner), jnp.uint32(0))
                for q, m in enumerate(move)
                if m
            ]
            moved[move] = functools.reduce(jnp.add, steps) if steps else jnp.uint32(0)
        if turn not in turned:
            turned[turn] = (place + jnp.uint32(turn)) % inner
    return [moved[move] + turned[turn] for move, turn in rounds]


def front_kernel(group, *refs):
    pieces, (w1, w2, close), outs = refs[:group], refs[group : group + 3], refs[group + 3 : -2]
    x, acc = refs[-2:]
    step = pl.program_id(0)
    local_a, width = pieces[0].shape[2:]
    total = group * local_a
    for i, piece in enumerate(pieces):
        for c in range(2):
            x[c * total + i * local_a : c * total + (i + 1) * local_a, :] = piece[c, 0]
    y = jnp.dot(w1[...], x[...], preferred_element_type=jnp.float32)
    lane = lax.broadcasted_iota(jnp.int32, close.shape[1:], 1)

    def column(c):
        return jnp.sum(jnp.where(lane == step, close[c], 0.0), axis=1, keepdims=True)

    cr, ci = column(0), column(1)
    yr, yi = y[:total], y[total:]
    phased = jnp.concatenate(
        [(cr * yr - ci * yi).astype(jnp.bfloat16), (cr * yi + ci * yr).astype(jnp.bfloat16)],
        axis=1,
    )
    both = jnp.dot(phased, w2[...], preferred_element_type=jnp.float32)
    row = lax.rem(step, ROWS)
    for h in range(acc.shape[0]):
        acc[h, pl.ds(row, total, stride=ROWS), :] = both[:, h * 128 : (h + 1) * 128]

    @pl.when(row == ROWS - 1)
    def _():
        for i, out in enumerate(outs):
            for h in range(acc.shape[0]):
                c, lanes = divmod(h * 128, width)
                out[c, :, :, lanes : lanes + 128] = (
                    acc[h, i * local_a * ROWS : (i + 1) * local_a * ROWS, :]
                    .reshape(local_a, ROWS, 128)
                    .astype(jnp.bfloat16)
                )


def front(pieces, w1, w2, close):
    group = len(pieces)
    _, chunk, local_a, width = pieces[0].shape
    total = group * local_a
    return pl.pallas_call(
        functools.partial(front_kernel, group),
        grid=(chunk,),
        in_specs=[pl.BlockSpec((2, 1, local_a, width), lambda b: (0, b, 0, 0))] * group
        + [
            pl.BlockSpec(w1.shape, lambda b: (0, 0)),
            pl.BlockSpec(w2.shape, lambda b: (0, 0)),
            pl.BlockSpec(close.shape, lambda b: (0, 0, 0)),
        ],
        out_specs=[pl.BlockSpec((2, local_a, ROWS, width), lambda b: (0, 0, b // ROWS, 0))]
        * group,
        out_shape=[jax.ShapeDtypeStruct((2, local_a, chunk, width), jnp.bfloat16)] * group,
        scratch_shapes=[
            pltpu.VMEM((2 * total, width), jnp.bfloat16),
            pltpu.VMEM((2 * width // 128, total * ROWS, 128), jnp.float32),
        ],
        compiler_params=pltpu.CompilerParams(vmem_limit_bytes=40 << 20),
        name="front",
    )(*pieces, w1, w2, close)


def mix_rows(pieces, w3, x, t):
    chunk, _ = pieces[0].shape[2:]
    total = len(pieces) * chunk
    for i, piece in enumerate(pieces):
        for c in range(2):
            x[c * total + i * chunk : c * total + (i + 1) * chunk, :] = piece[c, t]
    return jnp.dot(w3[...], x[...], preferred_element_type=jnp.float32)


def partial_kernel(n, *refs):
    pieces, w3, out, buffers, x, sems = refs[:n], refs[n], *refs[n + 1 :]
    steps = out.shape[0] // STEP_ROWS

    def copies(step, slot):
        rows = pl.ds(step * STEP_ROWS, STEP_ROWS)
        return [
            pltpu.make_async_copy(piece.at[:, rows], buffers.at[slot, i], sems.at[slot, i])
            for i, piece in enumerate(pieces)
        ]

    for copy in copies(0, 0):
        copy.start()

    @pl.loop(0, steps)
    def _(step):
        slot = lax.rem(step, 2)

        @pl.when(step + 1 < steps)
        def _():
            for copy in copies(step + 1, 1 - slot):
                copy.start()

        for copy in copies(step, slot):
            copy.wait()
        held = [buffers.at[slot, i] for i in range(n)]
        for t in range(STEP_ROWS):
            out[step * STEP_ROWS + t] = mix_rows(held, w3, x.at[t], t)


def partial_b(pieces, w3):
    _, local_a, chunk, width = pieces[0].shape
    n = len(pieces)
    return pl.pallas_call(
        functools.partial(partial_kernel, n),
        in_specs=[pl.BlockSpec(memory_space=pl.ANY)] * n
        + [pl.BlockSpec(memory_space=pltpu.VMEM)],
        out_specs=pl.BlockSpec(memory_space=pltpu.VMEM),
        out_shape=jax.ShapeDtypeStruct((local_a, w3.shape[0], width), jnp.float32),
        scratch_shapes=[
            pltpu.VMEM((2, n, 2, STEP_ROWS, chunk, width), jnp.bfloat16),
            pltpu.VMEM((STEP_ROWS, 2 * n * chunk, width), jnp.bfloat16),
            pltpu.SemaphoreType.DMA((2, n)),
        ],
        compiler_params=pltpu.CompilerParams(vmem_limit_bytes=12 << 20),
        name="partial",
    )(*pieces, w3)


def last_kernel(n, *refs):
    pieces, w3, base, out, x = refs[:n], *refs[n:]
    for t in range(out.shape[0]):
        y = base[t] + mix_rows(pieces, w3, x.at[t], t)
        split = y.shape[1] // 128
        for h in range(split):
            out[t, pl.ds(h, y.shape[0], stride=split), :] = y[:, h * 128 : (h + 1) * 128]


def last_b(pieces, w3, base):
    _, local_a, chunk, width = pieces[0].shape
    n = len(pieces)
    lines = w3.shape[0] * (width // 128)
    return pl.pallas_call(
        functools.partial(last_kernel, n),
        grid=(local_a // STEP_ROWS,),
        in_specs=[pl.BlockSpec((2, STEP_ROWS, chunk, width), lambda a: (0, a, 0, 0))] * n
        + [
            pl.BlockSpec(w3.shape, lambda a: (0, 0)),
            pl.BlockSpec((STEP_ROWS,) + base.shape[1:], lambda a: (a, 0, 0)),
        ],
        out_specs=pl.BlockSpec((STEP_ROWS, lines, 128), lambda a: (a, 0, 0)),
        out_shape=jax.ShapeDtypeStruct((local_a, lines, 128), jnp.float32),
        scratch_shapes=[pltpu.VMEM((STEP_ROWS, 2 * n * chunk, width), jnp.bfloat16)],
        compiler_params=pltpu.CompilerParams(vmem_limit_bytes=20 << 20),
        name="last",
    )(*pieces, w3, base)


def on_device(stem_tensor, branch_one, branch_two, mode_order, branch_three, closing):
    group = lax.axis_size("inter")
    me = lax.axis_index("inter")
    local_a, width = stem_tensor.shape[1], stem_tensor.shape[4]
    size_b = branch_three.shape[1]
    local_b = size_b // group
    chunk = local_b // B_CHUNKS
    size_a = group * local_a
    if (
        local_b % (B_CHUNKS * 2 * ROWS)
        or local_a % ROWS
        or width % 128
        or stem_tensor.shape[3] != 1
    ):
        return small_blocks(stem_tensor, branch_one, branch_two, mode_order, branch_three, closing)

    rounds = rounds_of(group)
    n_rounds = len(rounds)
    place = me.astype(jnp.uint32)
    zero = jnp.uint32(0)
    target = partners(place, rounds, group)
    pairs = [pairs_of(move, turn, group) for move, turn in rounds]

    def send(block, k):
        if k == 0:
            return block
        return lax.ppermute(block, "inter", pairs[k])

    stem = stem_tensor[:, :, :, 0, :]
    arrived = []
    for j in range(B_CHUNKS):
        got = []
        for k in range(n_rounds):
            block = lax.dynamic_slice(
                stem,
                (zero, zero, target[k] * jnp.uint32(local_b) + jnp.uint32(j * chunk), zero),
                (2, local_a, chunk, width),
                allow_negative_indices=False,
            )
            got.append(send(jnp.transpose(block, (0, 2, 1, 3)), k))
        arrived.append(got)

    where_to = jnp.stack(target).astype(jnp.int32)
    where_from = jnp.stack(partners(place, inverse_of(rounds, group), group)).astype(jnp.int32)
    one = branch_one.reshape(2, group, local_a, group, local_a)
    one = one[:, where_from][:, :, :, where_to].reshape(2, size_a, size_a)
    one = jnp.transpose(one, (0, 2, 1))
    w1 = jnp.concatenate(
        [
            jnp.concatenate([one[0], -one[1]], axis=1),
            jnp.concatenate([one[1], one[0]], axis=1),
        ],
        axis=0,
    )
    permuted = jnp.zeros_like(branch_two).at[:, mode_order, :].set(branch_two)
    w2 = jnp.concatenate(
        [
            jnp.concatenate([permuted[0], permuted[1]], axis=1),
            jnp.concatenate([-permuted[1], permuted[0]], axis=1),
        ],
        axis=0,
    )
    close = lax.dynamic_slice_in_dim(closing, me * local_b, local_b, 2).astype(jnp.float32)
    close = close.reshape(2, group, local_a, local_b)[:, where_to].reshape(2, size_a, local_b)
    three = branch_three.reshape(2, group, B_CHUNKS, chunk, size_b)[:, where_from]
    three = jnp.transpose(three, (2, 0, 4, 1, 3)).reshape(B_CHUNKS, 2, size_b, group * chunk)
    w3 = [
        jnp.stack(
            [
                jnp.concatenate([part[0], -part[1]], axis=1),
                jnp.concatenate([part[1], part[0]], axis=1),
            ],
            axis=1,
        ).reshape(2 * size_b, 2 * group * chunk)
        for part in three
    ]
    w1, w2, w3 = lax.optimization_barrier((w1, w2, w3))

    returned = []
    for j in range(B_CHUNKS):
        pieces = front(arrived[j], w1, w2, close[:, :, j * chunk : (j + 1) * chunk])
        returned.append([send(piece, k) for k, piece in enumerate(pieces)])

    base = partial_b(returned[0], w3[0])
    out = last_b(returned[1], w3[1], base)
    return out.reshape(local_a, size_b, 2, 1, width)


def solution(mesh):
    in_specs = (P(None, ("cuts", "inter"), None, None, None), P(), P(), P(), P(), P())
    out_specs = P(("cuts", "inter"), None, None, None, None)
    return jax.shard_map(
        on_device, mesh=mesh, in_specs=in_specs, out_specs=out_specs, check_vma=False
    )
```

profile of v0, /device:TPU:1, one launch (start us, length us, event | category | flops | bytes accessed | tf_op | source)
XLA Modules:
  0.0 775.5 jit_solution(13408427783282597883)
XLA Ops:
  30.9 7.5 constant_dynamic-slice_fusion
  42.9 29.8 %collective-permute-start.7 = (bf16[2,16,32,256]{3,2,1,0:T(8,128)(2,1)}, bf16[2,16,32,256]{3,2,1,0:T(8,128)(2,1)}, u32[]{:S(2)}, u32[]{:S(2)}) collective-permute-start(bf16[2,16,32,256]{3,2,1,0:T(8,128)(2,1)} %bitcast.211), channel_id=1, source_target_pairs={{0,8},{1,9},{2,10},{3,11},{4,0},{5,1},{6,2},{7,3},{8,12},{9,13},{1... | collective-permute-start | bytes 1572872 | tf_op jit(solution)/shard_map/ppermute | solution.py:280
  72.7 31.6 %collective-permute-start.9 = (bf16[2,16,32,256]{3,2,1,0:T(8,128)(2,1)}, bf16[2,16,32,256]{3,2,1,0:T(8,128)(2,1)}, u32[]{:S(2)}, u32[]{:S(2)}) collective-permute-start(bf16[2,16,32,256]{3,2,1,0:T(8,128)(2,1)} %bitcast.209), channel_id=1, source_target_pairs={{0,10},{1,11},{2,8},{3,9},{4,2},{5,3},{6,0},{7,1},{8,14},{9,15},{1... | collective-permute-start | bytes 1572872 | tf_op jit(solution)/shard_map/ppermute | solution.py:280
  127.1 19.7 %collective-permute-start.11 = (bf16[2,16,32,256]{3,2,1,0:T(8,128)(2,1)}, bf16[2,16,32,256]{3,2,1,0:T(8,128)(2,1)S(1)}, u32[]{:S(2)}, u32[]{:S(2)}) collective-permute-start(bf16[2,16,32,256]{3,2,1,0:T(8,128)(2,1)} %bitcast.250), channel_id=1, source_target_pairs={{0,4},{1,5},{2,6},{3,7},{4,12},{5,13},{6,14},{7,15},{8,0},{9,1},{1... | collective-permute-start | bytes 1572872 | tf_op jit(solution)/shard_map/ppermute | solution.py:280
  153.3 7.2 collective-permute-done.11.refs_12_
  161.4 10.1 %collective-permute-done.43.refs_14_ = bf16[2,16,32,256]{3,2,1,0:T(8,128)(2,1)S(1)} collective-permute-done((bf16[2,16,32,256]{3,2,1,0:T(8,128)(2,1)}, bf16[2,16,32,256]{3,2,1,0:T(8,128)(2,1)S(1)}, u32[]{:S(2)}, u32[]{:S(2)}) %collective-permute-start.43) | collective-permute-done | bytes 524320 | tf_op jit(solution)/shard_map/ppermute | solution.py:280
  171.5 9.8 %collective-permute-done.12.refs_13_ = bf16[2,16,32,256]{3,2,1,0:T(8,128)(2,1)S(1)} collective-permute-done((bf16[2,16,32,256]{3,2,1,0:T(8,128)(2,1)S(1)}, bf16[2,16,32,256]{3,2,1,0:T(8,128)(2,1)S(1)}, u32[]{:S(2)}, u32[]{:S(2)}) %collective-permute-start.12) | collective-permute-done | bytes 524320 | tf_op jit(solution)/shard_map/ppermute | solution.py:280
  182.8 11.2 %collective-permute-done.13.refs_14_ = bf16[2,16,32,256]{3,2,1,0:T(8,128)(2,1)S(1)} collective-permute-done((bf16[2,16,32,256]{3,2,1,0:T(8,128)(2,1)S(1)}, bf16[2,16,32,256]{3,2,1,0:T(8,128)(2,1)S(1)}, u32[]{:S(2)}, u32[]{:S(2)}) %collective-permute-start.13) | collective-permute-done | bytes 524320 | tf_op jit(solution)/shard_map/ppermute | solution.py:280
  202.1 18.2 %scatter_fusion = bf16[2,256,256]{2,0,1:T(2,128)(2,1)S(1)} fusion(bf16[2,256,256]{2,0,1:T(2,128)(2,1)S(1)} %broadcast_in_dim.4, s32[256]{0:T(256)S(1)} %compare_select_fusion, bf16[256,2,256]{2,1,0:T(2,128)(2,1)} %copy.111), kind=kCustom, calls=%fused_computation.4 | custom fusion | bytes 787456 | tf_op jit(solution)/shard_map/scatter | solution.py:308
  227.3 36.7 %collective-permute-start.37 = (bf16[2,16,32,256]{3,2,1,0:T(8,128)(2,1)}, bf16[2,16,32,256]{3,2,1,0:T(8,128)(2,1)}, u32[]{:S(2)}, u32[]{:S(2)}) collective-permute-start(bf16[2,16,32,256]{3,2,1,0:T(8,128)(2,1)} %bitcast.240), channel_id=1, source_target_pairs={{0,8},{1,9},{2,10},{3,11},{4,0},{5,1},{6,2},{7,3},{8,12},{9,13},{1... | collective-permute-start | bytes 1572872 | tf_op jit(solution)/shard_map/ppermute | solution.py:280
  302.3 7.1 copy.110
  330.9 32.2 %front.2 = (bf16[2,32,16,256]{3,2,1,0:T(8,128)(2,1)S(1)}, bf16[2,32,16,256]{3,2,1,0:T(8,128)(2,1)S(1)}, bf16[2,32,16,256]{3,2,1,0:T(8,128)(2,1)S(1)}, bf16[2,32,...) custom-call(bf16[2,16,32,256]{3,2,1,0:T(8,128)(2,1)S(1)} %bitcast.22, ...), custom_call_target="tpu_custom_call" | custom-call | tf_op jit(solution)/shard_map/front/pallas_call | solution.py:146
  373.3 10.3 %collective-permute-done.44.refs_15_ = bf16[2,16,32,256]{3,2,1,0:T(8,128)(2,1)S(1)} collective-permute-done((bf16[2,16,32,256]{3,2,1,0:T(8,128)(2,1)S(1)}, bf16[2,16,32,256]{3,2,1,0:T(8,128)(2,1)S(1)}, u32[]{:S(2)}, u32[]{:S(2)}) %collective-permute-start.44) | collective-permute-done | bytes 524320 | tf_op jit(solution)/shard_map/ppermute | solution.py:280
  386.1 7.7 collective-permute-done.15.refs_1_
  402.6 38.6 %collective-permute-start.22 = (bf16[2,32,16,256]{3,2,1,0:T(8,128)(2,1)}, bf16[2,32,16,256]{3,2,1,0:T(8,128)(2,1)S(1)}, u32[]{:S(2)}, u32[]{:S(2)}) collective-permute-start(bf16[2,32,16,256]{3,2,1,0:T(8,128)(2,1)} %get-tuple-element.51), channel_id=1, source_target_pairs={{0,8},{1,9},{2,10},{3,11},{4,0},{5,1},{6,2},{7,3},{8,12},{9,13},{1... | collective-permute-start | bytes 1572872 | tf_op jit(solution)/shard_map/ppermute | solution.py:280
  441.7 31.2 %collective-permute-start.24 = (bf16[2,32,16,256]{3,2,1,0:T(8,128)(2,1)}, bf16[2,32,16,256]{3,2,1,0:T(8,128)(2,1)S(1)}, u32[]{:S(2)}, u32[]{:S(2)}) collective-permute-start(bf16[2,32,16,256]{3,2,1,0:T(8,128)(2,1)} %get-tuple-element.53), channel_id=1, source_target_pairs={{0,10},{1,11},{2,8},{3,9},{4,2},{5,3},{6,0},{7,1},{8,14},{9,15},{1... | collective-permute-start | bytes 1572872 | tf_op jit(solution)/shard_map/ppermute | solution.py:280
  473.1 31.3 %front.3 = (bf16[2,32,16,256]{3,2,1,0:T(8,128)(2,1)S(1)}, bf16[2,32,16,256]{3,2,1,0:T(8,128)(2,1)S(1)}, bf16[2,32,16,256]{3,2,1,0:T(8,128)(2,1)S(1)}, bf16[2,32,...) custom-call(bf16[2,16,32,256]{3,2,1,0:T(8,128)(2,1)S(1)} %bitcast.22, ...), custom_call_target="tpu_custom_call" | custom-call | tf_op jit(solution)/shard_map/front/pallas_call | solution.py:146
  511.7 7.3 collective-permute-done.45.refs_1_
  526.0 28.3 %collective-permute-done.47.refs_3_ = bf16[2,32,16,256]{3,2,1,0:T(8,128)(2,1)S(1)} collective-permute-done((bf16[2,32,16,256]{3,2,1,0:T(8,128)(2,1)S(1)}, bf16[2,32,16,256]{3,2,1,0:T(8,128)(2,1)S(1)}, u32[]{:S(2)}, u32[]{:S(2)}) %collective-permute-start.47) | collective-permute-done | bytes 524320 | tf_op jit(solution)/shard_map/ppermute | solution.py:280
  554.3 12.2 %collective-permute-start.52 = (bf16[2,32,16,256]{3,2,1,0:T(8,128)(2,1)S(1)}, bf16[2,32,16,256]{3,2,1,0:T(8,128)(2,1)S(1)}, u32[]{:S(2)}, u32[]{:S(2)}) collective-permute-start(bf16[2,32,16,256]{3,2,1,0:T(8,128)(2,1)S(1)} %get-tuple-element.68), channel_id=1, source_target_pairs={{0,8},{1,9},{2,10},{3,11},{4,0},{5,1},{6,2},{7,3},{8,12},{9,13},{1... | collective-permute-start | bytes 1572872 | tf_op jit(solution)/shard_map/ppermute | solution.py:280
  567.7 30.2 %collective-permute-start.54 = (bf16[2,32,16,256]{3,2,1,0:T(8,128)(2,1)S(1)}, bf16[2,32,16,256]{3,2,1,0:T(8,128)(2,1)S(1)}, u32[]{:S(2)}, u32[]{:S(2)}) collective-permute-start(bf16[2,32,16,256]{3,2,1,0:T(8,128)(2,1)S(1)} %get-tuple-element.70), channel_id=1, source_target_pairs={{0,10},{1,11},{2,8},{3,9},{4,2},{5,3},{6,0},{7,1},{8,14},{9,15},{1... | collective-permute-start | bytes 1572872 | tf_op jit(solution)/shard_map/ppermute | solution.py:280
  597.8 23.0 %collective-permute-start.55 = (bf16[2,32,16,256]{3,2,1,0:T(8,128)(2,1)S(1)}, bf16[2,32,16,256]{3,2,1,0:T(8,128)(2,1)S(1)}, u32[]{:S(2)}, u32[]{:S(2)}) collective-permute-start(bf16[2,32,16,256]{3,2,1,0:T(8,128)(2,1)S(1)} %get-tuple-element.71), channel_id=1, source_target_pairs={{0,11},{1,8},{2,9},{3,10},{4,3},{5,0},{6,1},{7,2},{8,15},{9,12},{1... | collective-permute-start | bytes 1572872 | tf_op jit(solution)/shard_map/ppermute | solution.py:280
  620.9 21.7 %collective-permute-start.56 = (bf16[2,32,16,256]{3,2,1,0:T(8,128)(2,1)S(1)}, bf16[2,32,16,256]{3,2,1,0:T(8,128)(2,1)S(1)}, u32[]{:S(2)}, u32[]{:S(2)}) collective-permute-start(bf16[2,32,16,256]{3,2,1,0:T(8,128)(2,1)S(1)} %get-tuple-element.72), channel_id=1, source_target_pairs={{0,4},{1,5},{2,6},{3,7},{4,12},{5,13},{6,14},{7,15},{8,0},{9,1},{1... | collective-permute-start | bytes 1572872 | tf_op jit(solution)/shard_map/ppermute | solution.py:280
  647.7 7.1 collective-permute-done.56.refs_12_
  656.5 9.0 %collective-permute-done.57.refs_13_ = bf16[2,32,16,256]{3,2,1,0:T(8,128)(2,1)S(1)} collective-permute-done((bf16[2,32,16,256]{3,2,1,0:T(8,128)(2,1)S(1)}, bf16[2,32,16,256]{3,2,1,0:T(8,128)(2,1)S(1)}, u32[]{:S(2)}, u32[]{:S(2)}) %collective-permute-start.57) | collective-permute-done | bytes 524320 | tf_op jit(solution)/shard_map/ppermute | solution.py:280
  668.9 7.9 %collective-permute-done.58.refs_14_ = bf16[2,32,16,256]{3,2,1,0:T(8,128)(2,1)S(1)} collective-permute-done((bf16[2,32,16,256]{3,2,1,0:T(8,128)(2,1)S(1)}, bf16[2,32,16,256]{3,2,1,0:T(8,128)(2,1)S(1)}, u32[]{:S(2)}, u32[]{:S(2)}) %collective-permute-start.58) | collective-permute-done | bytes 524320 | tf_op jit(solution)/shard_map/ppermute | solution.py:280
  679.6 9.2 %collective-permute-done.59.refs_15_ = bf16[2,32,16,256]{3,2,1,0:T(8,128)(2,1)S(1)} collective-permute-done((bf16[2,32,16,256]{3,2,1,0:T(8,128)(2,1)S(1)}, bf16[2,32,16,256]{3,2,1,0:T(8,128)(2,1)S(1)}, u32[]{:S(2)}, u32[]{:S(2)}) %collective-permute-start.59) | collective-permute-done | bytes 524320 | tf_op jit(solution)/shard_map/ppermute | solution.py:280
  690.5 17.7 %partial.1.refs_17_ = f32[32,1024,256]{2,1,0:T(8,128)S(1)} custom-call(bf16[2,32,16,256]{3,2,1,0:T(8,128)(2,1)S(1)} %get-tuple-element.60.refs_0_, bf16[2,32,16,256]{3,2,1,0:T(8,128)(2,1)S(1)} %collective-permute-done.45.refs_1_, bf16[2,32,16,256]{3,2,1,0:T(8,128)(2,1)S(1)} %collective-permute-done.46.refs_2_, ...), custom_call_target="tpu_custom_call" | custom-call | tf_op jit(solution)/shard_map/partial/pallas_call | solution.py:209
  708.2 11.1 %copy-done.2 = f32[32,1024,256]{2,1,0:T(8,128)} copy-done((f32[32,1024,256]{2,1,0:T(8,128)}, f32[32,1024,256]{2,1,0:T(8,128)S(1)}, u32[]{:S(2)}) %copy-start.2) | copy-done | bytes 33554456
  721.9 11.1 %collective-permute-done.28.refs_14_ = bf16[2,32,16,256]{3,2,1,0:T(8,128)(2,1)S(1)} collective-permute-done((bf16[2,32,16,256]{3,2,1,0:T(8,128)(2,1)S(1)}, bf16[2,32,16,256]{3,2,1,0:T(8,128)(2,1)S(1)}, u32[]{:S(2)}, u32[]{:S(2)}) %collective-permute-start.28) | collective-permute-done | bytes 524320 | tf_op jit(solution)/shard_map/ppermute | solution.py:280
  733.0 11.2 %collective-permute-done.29.refs_15_ = bf16[2,32,16,256]{3,2,1,0:T(8,128)(2,1)S(1)} collective-permute-done((bf16[2,32,16,256]{3,2,1,0:T(8,128)(2,1)S(1)}, bf16[2,32,16,256]{3,2,1,0:T(8,128)(2,1)S(1)}, u32[]{:S(2)}, u32[]{:S(2)}) %collective-permute-start.29) | collective-permute-done | bytes 524320 | tf_op jit(solution)/shard_map/ppermute | solution.py:280
  744.2 31.3 %last.1 = f32[32,2048,128]{2,1,0:T(8,128)} custom-call(bf16[2,32,16,256]{3,2,1,0:T(8,128)(2,1)S(1)} %get-tuple-element.43.refs_0_, bf16[2,32,16,256]{3,2,1,0:T(8,128)(2,1)S(1)} %collective-permute-done.15.refs_1_, bf16[2,32,16,256]{3,2,1,0:T(8,128)(2,1)S(1)} %collective-permute-done.16.refs_2_, bf16[2,32,16,256]{3,2,1,0:T(8,128)(2,1)S(1)} %collective-permute-done.17.refs_3_, ...), custom_call_target="tpu_custom_call" | custom-call | tf_op jit(solution)/shard_map/last/pallas_call | solution.py:238
  (267 shorter events, 196.2 us)
Async XLA Ops:
  15.8 56.9 %collective-permute-start.3 = (bf16[2,16,32,256]{3,2,1,0:T(8,128)(2,1)}, bf16[2,16,32,256]{3,2,1,0:T(8,128)(2,1)S(1)}, u32[]{:S(2)}, u32[]{:S(2)}) collective-permute-start(bf16[2,16,32,256]{3,2,1,0:T(8,128)(2,1)} %bitcast.215), channel_id=1, source_target_pairs={{0,3},{1,0},{2,1},{3,2},{4,7},{5,4},{6,5},{7,6},{8,11},{9,8},{10,9... | collective-permute-start | bytes 1572872 | tf_op jit(solution)/shard_map/ppermute | solution.py:280
  38.4 84.8 %collective-permute-start.5 = (bf16[2,16,32,256]{3,2,1,0:T(8,128)(2,1)}, bf16[2,16,32,256]{3,2,1,0:T(8,128)(2,1)S(1)}, u32[]{:S(2)}, u32[]{:S(2)}) collective-permute-start(bf16[2,16,32,256]{3,2,1,0:T(8,128)(2,1)} %bitcast.213), channel_id=1, source_target_pairs={{0,14},{1,15},{2,12},{3,13},{4,10},{5,11},{6,8},{7,9},{8,6},{9,7},... | collective-permute-start | bytes 1572872 | tf_op jit(solution)/shard_map/ppermute | solution.py:280
  42.9 84.2 %collective-permute-start.6 = (bf16[2,16,32,256]{3,2,1,0:T(8,128)(2,1)}, bf16[2,16,32,256]{3,2,1,0:T(8,128)(2,1)S(1)}, u32[]{:S(2)}, u32[]{:S(2)}) collective-permute-start(bf16[2,16,32,256]{3,2,1,0:T(8,128)(2,1)} %bitcast.212), channel_id=1, source_target_pairs={{0,15},{1,12},{2,13},{3,14},{4,11},{5,8},{6,9},{7,10},{8,7},{9,4},... | collective-permute-start | bytes 1572872 | tf_op jit(solution)/shard_map/ppermute | solution.py:280
  42.9 104.0 %collective-permute-start.7 = (bf16[2,16,32,256]{3,2,1,0:T(8,128)(2,1)}, bf16[2,16,32,256]{3,2,1,0:T(8,128)(2,1)}, u32[]{:S(2)}, u32[]{:S(2)}) collective-permute-start(bf16[2,16,32,256]{3,2,1,0:T(8,128)(2,1)} %bitcast.211), channel_id=1, source_target_pairs={{0,8},{1,9},{2,10},{3,11},{4,0},{5,1},{6,2},{7,3},{8,12},{9,13},{1... | collective-permute-start | bytes 1572872 | tf_op jit(solution)/shard_map/ppermute | solution.py:280
  72.7 74.2 %collective-permute-start.8 = (bf16[2,16,32,256]{3,2,1,0:T(8,128)(2,1)}, bf16[2,16,32,256]{3,2,1,0:T(8,128)(2,1)}, u32[]{:S(2)}, u32[]{:S(2)}) collective-permute-start(bf16[2,16,32,256]{3,2,1,0:T(8,128)(2,1)} %bitcast.210), channel_id=1, source_target_pairs={{0,9},{1,10},{2,11},{3,8},{4,1},{5,2},{6,3},{7,0},{8,13},{9,14},{1... | collective-permute-start | bytes 1572872 | tf_op jit(solution)/shard_map/ppermute | solution.py:280
  72.7 76.6 %collective-permute-start.9 = (bf16[2,16,32,256]{3,2,1,0:T(8,128)(2,1)}, bf16[2,16,32,256]{3,2,1,0:T(8,128)(2,1)}, u32[]{:S(2)}, u32[]{:S(2)}) collective-permute-start(bf16[2,16,32,256]{3,2,1,0:T(8,128)(2,1)} %bitcast.209), channel_id=1, source_target_pairs={{0,10},{1,11},{2,8},{3,9},{4,2},{5,3},{6,0},{7,1},{8,14},{9,15},{1... | collective-permute-start | bytes 1572872 | tf_op jit(solution)/shard_map/ppermute | solution.py:280
  151.5 69.9 %collective-permute-start.14 = (bf16[2,16,32,256]{3,2,1,0:T(8,128)(2,1)}, bf16[2,16,32,256]{3,2,1,0:T(8,128)(2,1)}, u32[]{:S(2)}, u32[]{:S(2)}) collective-permute-start(bf16[2,16,32,256]{3,2,1,0:T(8,128)(2,1)} %bitcast.204), channel_id=1, source_target_pairs={{0,7},{1,4},{2,5},{3,6},{4,15},{5,12},{6,13},{7,14},{8,3},{9,0},{1... | collective-permute-start | bytes 1572872 | tf_op jit(solution)/shard_map/ppermute | solution.py:280
  160.6 63.4 %collective-permute-start.30 = (bf16[2,16,32,256]{3,2,1,0:T(8,128)(2,1)}, bf16[2,16,32,256]{3,2,1,0:T(8,128)(2,1)S(1)}, u32[]{:S(2)}, u32[]{:S(2)}) collective-permute-start(bf16[2,16,32,256]{3,2,1,0:T(8,128)(2,1)} %bitcast.202), channel_id=1, source_target_pairs={{0,12},{1,13},{2,14},{3,15},{4,8},{5,9},{6,10},{7,11},{8,4},{9,5},... | collective-permute-start | bytes 1572872 | tf_op jit(solution)/shard_map/ppermute | solution.py:280
  194.1 69.9 %collective-permute-start.33 = (bf16[2,16,32,256]{3,2,1,0:T(8,128)(2,1)}, bf16[2,16,32,256]{3,2,1,0:T(8,128)(2,1)}, u32[]{:S(2)}, u32[]{:S(2)}) collective-permute-start(bf16[2,16,32,256]{3,2,1,0:T(8,128)(2,1)} %bitcast.199), channel_id=1, source_target_pairs={{0,3},{1,0},{2,1},{3,2},{4,7},{5,4},{6,5},{7,6},{8,11},{9,8},{10,9... | collective-permute-start | bytes 1572872 | tf_op jit(solution)/shard_map/ppermute | solution.py:280
  221.4 100.1 %collective-permute-start.34 = (bf16[2,16,32,256]{3,2,1,0:T(8,128)(2,1)}, bf16[2,16,32,256]{3,2,1,0:T(8,128)(2,1)}, u32[]{:S(2)}, u32[]{:S(2)}) collective-permute-start(bf16[2,16,32,256]{3,2,1,0:T(8,128)(2,1)} %bitcast.248), channel_id=1, source_target_pairs={{0,13},{1,14},{2,15},{3,12},{4,9},{5,10},{6,11},{7,8},{8,5},{9,6},... | collective-permute-start | bytes 1572872 | tf_op jit(solution)/shard_map/ppermute | solution.py:280
  224.0 100.4 %collective-permute-start.35 = (bf16[2,16,32,256]{3,2,1,0:T(8,128)(2,1)}, bf16[2,16,32,256]{3,2,1,0:T(8,128)(2,1)}, u32[]{:S(2)}, u32[]{:S(2)}) collective-permute-start(bf16[2,16,32,256]{3,2,1,0:T(8,128)(2,1)} %bitcast.244), channel_id=1, source_target_pairs={{0,14},{1,15},{2,12},{3,13},{4,10},{5,11},{6,8},{7,9},{8,6},{9,7},... | collective-permute-start | bytes 1572872 | tf_op jit(solution)/shard_map/ppermute | solution.py:280
  226.9 97.4 %collective-permute-start.36 = (bf16[2,16,32,256]{3,2,1,0:T(8,128)(2,1)}, bf16[2,16,32,256]{3,2,1,0:T(8,128)(2,1)}, u32[]{:S(2)}, u32[]{:S(2)}) collective-permute-start(bf16[2,16,32,256]{3,2,1,0:T(8,128)(2,1)} %bitcast.242), channel_id=1, source_target_pairs={{0,15},{1,12},{2,13},{3,14},{4,11},{5,8},{6,9},{7,10},{8,7},{9,4},... | collective-permute-start | bytes 1572872 | tf_op jit(solution)/shard_map/ppermute | solution.py:280
  227.3 97.2 %collective-permute-start.37 = (bf16[2,16,32,256]{3,2,1,0:T(8,128)(2,1)}, bf16[2,16,32,256]{3,2,1,0:T(8,128)(2,1)}, u32[]{:S(2)}, u32[]{:S(2)}) collective-permute-start(bf16[2,16,32,256]{3,2,1,0:T(8,128)(2,1)} %bitcast.240), channel_id=1, source_target_pairs={{0,8},{1,9},{2,10},{3,11},{4,0},{5,1},{6,2},{7,3},{8,12},{9,13},{1... | collective-permute-start | bytes 1572872 | tf_op jit(solution)/shard_map/ppermute | solution.py:280
  264.0 63.1 %collective-permute-start.38 = (bf16[2,16,32,256]{3,2,1,0:T(8,128)(2,1)}, bf16[2,16,32,256]{3,2,1,0:T(8,128)(2,1)}, u32[]{:S(2)}, u32[]{:S(2)}) collective-permute-start(bf16[2,16,32,256]{3,2,1,0:T(8,128)(2,1)} %bitcast.238), channel_id=1, source_target_pairs={{0,9},{1,10},{2,11},{3,8},{4,1},{5,2},{6,3},{7,0},{8,13},{9,14},{1... | collective-permute-start | bytes 1572872 | tf_op jit(solution)/shard_map/ppermute | solution.py:280
  327.1 56.5 %collective-permute-start.44 = (bf16[2,16,32,256]{3,2,1,0:T(8,128)(2,1)S(1)}, bf16[2,16,32,256]{3,2,1,0:T(8,128)(2,1)S(1)}, u32[]{:S(2)}, u32[]{:S(2)}) collective-permute-start(bf16[2,16,32,256]{3,2,1,0:T(8,128)(2,1)S(1)} %bitcast.239), channel_id=1, source_target_pairs={{0,7},{1,4},{2,5},{3,6},{4,15},{5,12},{6,13},{7,14},{8,3},{9,0},{1... | collective-permute-start | bytes 1572872 | tf_op jit(solution)/shard_map/ppermute | solution.py:280
  371.8 69.4 %collective-permute-start.18 = (bf16[2,32,16,256]{3,2,1,0:T(8,128)(2,1)S(1)}, bf16[2,32,16,256]{3,2,1,0:T(8,128)(2,1)S(1)}, u32[]{:S(2)}, u32[]{:S(2)}) collective-permute-start(bf16[2,32,16,256]{3,2,1,0:T(8,128)(2,1)S(1)} %get-tuple-element.47), channel_id=1, source_target_pairs={{0,3},{1,0},{2,1},{3,2},{4,7},{5,4},{6,5},{7,6},{8,11},{9,8},{10,9... | collective-permute-start | bytes 1572872 | tf_op jit(solution)/shard_map/ppermute | solution.py:280
  384.4 57.3 %collective-permute-start.19 = (bf16[2,32,16,256]{3,2,1,0:T(8,128)(2,1)S(1)}, bf16[2,32,16,256]{3,2,1,0:T(8,128)(2,1)S(1)}, u32[]{:S(2)}, u32[]{:S(2)}) collective-permute-start(bf16[2,32,16,256]{3,2,1,0:T(8,128)(2,1)S(1)} %get-tuple-element.48), channel_id=1, source_target_pairs={{0,13},{1,14},{2,15},{3,12},{4,9},{5,10},{6,11},{7,8},{8,5},{9,6},... | collective-permute-start | bytes 1572872 | tf_op jit(solution)/shard_map/ppermute | solution.py:280
  393.9 110.6 %collective-permute-start.20 = (bf16[2,32,16,256]{3,2,1,0:T(8,128)(2,1)}, bf16[2,32,16,256]{3,2,1,0:T(8,128)(2,1)S(1)}, u32[]{:S(2)}, u32[]{:S(2)}) collective-permute-start(bf16[2,32,16,256]{3,2,1,0:T(8,128)(2,1)} %get-tuple-element.49), channel_id=1, source_target_pairs={{0,14},{1,15},{2,12},{3,13},{4,10},{5,11},{6,8},{7,9},{8,6},{9,7},... | collective-permute-start | bytes 1572872 | tf_op jit(solution)/shard_map/ppermute | solution.py:280
  396.5 110.9 %collective-permute-start.21 = (bf16[2,32,16,256]{3,2,1,0:T(8,128)(2,1)}, bf16[2,32,16,256]{3,2,1,0:T(8,128)(2,1)S(1)}, u32[]{:S(2)}, u32[]{:S(2)}) collective-permute-start(bf16[2,32,16,256]{3,2,1,0:T(8,128)(2,1)} %get-tuple-element.50), channel_id=1, source_target_pairs={{0,15},{1,12},{2,13},{3,14},{4,11},{5,8},{6,9},{7,10},{8,7},{9,4},... | collective-permute-start | bytes 1572872 | tf_op jit(solution)/shard_map/ppermute | solution.py:280
  402.6 106.6 %collective-permute-start.22 = (bf16[2,32,16,256]{3,2,1,0:T(8,128)(2,1)}, bf16[2,32,16,256]{3,2,1,0:T(8,128)(2,1)S(1)}, u32[]{:S(2)}, u32[]{:S(2)}) collective-permute-start(bf16[2,32,16,256]{3,2,1,0:T(8,128)(2,1)} %get-tuple-element.51), channel_id=1, source_target_pairs={{0,8},{1,9},{2,10},{3,11},{4,0},{5,1},{6,2},{7,3},{8,12},{9,13},{1... | collective-permute-start | bytes 1572872 | tf_op jit(solution)/shard_map/ppermute | solution.py:280
  441.2 68.0 %collective-permute-start.23 = (bf16[2,32,16,256]{3,2,1,0:T(8,128)(2,1)}, bf16[2,32,16,256]{3,2,1,0:T(8,128)(2,1)S(1)}, u32[]{:S(2)}, u32[]{:S(2)}) collective-permute-start(bf16[2,32,16,256]{3,2,1,0:T(8,128)(2,1)} %get-tuple-element.52), channel_id=1, source_target_pairs={{0,9},{1,10},{2,11},{3,8},{4,1},{5,2},{6,3},{7,0},{8,13},{9,14},{1... | collective-permute-start | bytes 1572872 | tf_op jit(solution)/shard_map/ppermute | solution.py:280
  441.7 68.0 %collective-permute-start.24 = (bf16[2,32,16,256]{3,2,1,0:T(8,128)(2,1)}, bf16[2,32,16,256]{3,2,1,0:T(8,128)(2,1)S(1)}, u32[]{:S(2)}, u32[]{:S(2)}) collective-permute-start(bf16[2,32,16,256]{3,2,1,0:T(8,128)(2,1)} %get-tuple-element.53), channel_id=1, source_target_pairs={{0,10},{1,11},{2,8},{3,9},{4,2},{5,3},{6,0},{7,1},{8,14},{9,15},{1... | collective-permute-start | bytes 1572872 | tf_op jit(solution)/shard_map/ppermute | solution.py:280
  509.2 57.2 %collective-permute-start.48 = (bf16[2,32,16,256]{3,2,1,0:T(8,128)(2,1)S(1)}, bf16[2,32,16,256]{3,2,1,0:T(8,128)(2,1)S(1)}, u32[]{:S(2)}, u32[]{:S(2)}) collective-permute-start(bf16[2,32,16,256]{3,2,1,0:T(8,128)(2,1)S(1)} %get-tuple-element.64), channel_id=1, source_target_pairs={{0,3},{1,0},{2,1},{3,2},{4,7},{5,4},{6,5},{7,6},{8,11},{9,8},{10,9... | collective-permute-start | bytes 1572872 | tf_op jit(solution)/shard_map/ppermute | solution.py:280
  509.7 57.9 %collective-permute-start.49 = (bf16[2,32,16,256]{3,2,1,0:T(8,128)(2,1)S(1)}, bf16[2,32,16,256]{3,2,1,0:T(8,128)(2,1)S(1)}, u32[]{:S(2)}, u32[]{:S(2)}) collective-permute-start(bf16[2,32,16,256]{3,2,1,0:T(8,128)(2,1)S(1)} %get-tuple-element.65), channel_id=1, source_target_pairs={{0,13},{1,14},{2,15},{3,12},{4,9},{5,10},{6,11},{7,8},{8,5},{9,6},... | collective-permute-start | bytes 1572872 | tf_op jit(solution)/shard_map/ppermute | solution.py:280
  519.0 78.9 %collective-permute-start.50 = (bf16[2,32,16,256]{3,2,1,0:T(8,128)(2,1)S(1)}, bf16[2,32,16,256]{3,2,1,0:T(8,128)(2,1)S(1)}, u32[]{:S(2)}, u32[]{:S(2)}) collective-permute-start(bf16[2,32,16,256]{3,2,1,0:T(8,128)(2,1)S(1)} %get-tuple-element.66), channel_id=1, source_target_pairs={{0,14},{1,15},{2,12},{3,13},{4,10},{5,11},{6,8},{7,9},{8,6},{9,7},... | collective-permute-start | bytes 1572872 | tf_op jit(solution)/shard_map/ppermute | solution.py:280
  522.1 98.8 %collective-permute-start.51 = (bf16[2,32,16,256]{3,2,1,0:T(8,128)(2,1)S(1)}, bf16[2,32,16,256]{3,2,1,0:T(8,128)(2,1)S(1)}, u32[]{:S(2)}, u32[]{:S(2)}) collective-permute-start(bf16[2,32,16,256]{3,2,1,0:T(8,128)(2,1)S(1)} %get-tuple-element.67), channel_id=1, source_target_pairs={{0,15},{1,12},{2,13},{3,14},{4,11},{5,8},{6,9},{7,10},{8,7},{9,4},... | collective-permute-start | bytes 1572872 | tf_op jit(solution)/shard_map/ppermute | solution.py:280
  554.3 88.3 %collective-permute-start.52 = (bf16[2,32,16,256]{3,2,1,0:T(8,128)(2,1)S(1)}, bf16[2,32,16,256]{3,2,1,0:T(8,128)(2,1)S(1)}, u32[]{:S(2)}, u32[]{:S(2)}) collective-permute-start(bf16[2,32,16,256]{3,2,1,0:T(8,128)(2,1)S(1)} %get-tuple-element.68), channel_id=1, source_target_pairs={{0,8},{1,9},{2,10},{3,11},{4,0},{5,1},{6,2},{7,3},{8,12},{9,13},{1... | collective-permute-start | bytes 1572872 | tf_op jit(solution)/shard_map/ppermute | solution.py:280
  566.5 76.4 %collective-permute-start.53 = (bf16[2,32,16,256]{3,2,1,0:T(8,128)(2,1)S(1)}, bf16[2,32,16,256]{3,2,1,0:T(8,128)(2,1)S(1)}, u32[]{:S(2)}, u32[]{:S(2)}) collective-permute-start(bf16[2,32,16,256]{3,2,1,0:T(8,128)(2,1)S(1)} %get-tuple-element.69), channel_id=1, source_target_pairs={{0,9},{1,10},{2,11},{3,8},{4,1},{5,2},{6,3},{7,0},{8,13},{9,14},{1... | collective-permute-start | bytes 1572872 | tf_op jit(solution)/shard_map/ppermute | solution.py:280
  567.7 75.8 %collective-permute-start.54 = (bf16[2,32,16,256]{3,2,1,0:T(8,128)(2,1)S(1)}, bf16[2,32,16,256]{3,2,1,0:T(8,128)(2,1)S(1)}, u32[]{:S(2)}, u32[]{:S(2)}) collective-permute-start(bf16[2,32,16,256]{3,2,1,0:T(8,128)(2,1)S(1)} %get-tuple-element.70), channel_id=1, source_target_pairs={{0,10},{1,11},{2,8},{3,9},{4,2},{5,3},{6,0},{7,1},{8,14},{9,15},{1... | collective-permute-start | bytes 1572872 | tf_op jit(solution)/shard_map/ppermute | solution.py:280
  644.5 74.8 %collective-permute-start.25 = (bf16[2,32,16,256]{3,2,1,0:T(8,128)(2,1)}, bf16[2,32,16,256]{3,2,1,0:T(8,128)(2,1)S(1)}, u32[]{:S(2)}, u32[]{:S(2)}) collective-permute-start(bf16[2,32,16,256]{3,2,1,0:T(8,128)(2,1)} %get-tuple-element.54), channel_id=1, source_target_pairs={{0,11},{1,8},{2,9},{3,10},{4,3},{5,0},{6,1},{7,2},{8,15},{9,12},{1... | collective-permute-start | bytes 1572872 | tf_op jit(solution)/shard_map/ppermute | solution.py:280
  654.8 64.5 %collective-permute-start.26 = (bf16[2,32,16,256]{3,2,1,0:T(8,128)(2,1)}, bf16[2,32,16,256]{3,2,1,0:T(8,128)(2,1)S(1)}, u32[]{:S(2)}, u32[]{:S(2)}) collective-permute-start(bf16[2,32,16,256]{3,2,1,0:T(8,128)(2,1)} %get-tuple-element.55), channel_id=1, source_target_pairs={{0,4},{1,5},{2,6},{3,7},{4,12},{5,13},{6,14},{7,15},{8,0},{9,1},{1... | collective-permute-start | bytes 1572872 | tf_op jit(solution)/shard_map/ppermute | solution.py:280
  665.5 56.3 %collective-permute-start.27 = (bf16[2,32,16,256]{3,2,1,0:T(8,128)(2,1)}, bf16[2,32,16,256]{3,2,1,0:T(8,128)(2,1)S(1)}, u32[]{:S(2)}, u32[]{:S(2)}) collective-permute-start(bf16[2,32,16,256]{3,2,1,0:T(8,128)(2,1)} %get-tuple-element.56), channel_id=1, source_target_pairs={{0,5},{1,6},{2,7},{3,4},{4,13},{5,14},{6,15},{7,12},{8,1},{9,2},{1... | collective-permute-start | bytes 1572872 | tf_op jit(solution)/shard_map/ppermute | solution.py:280
  (79 other events, 3630.8 us)
where the time goes:
time: 778 us; the launch traced here: 776 us
  starting transfers between devices  354 us (46%)
  waiting for transfers between devices  157 us (20%)
  local copies, waits for them, and re-layouts  142 us (18%)
  Pallas kernels  112 us (14%)
  other arithmetic  10 us (1%)
    ppermute x60, starting transfers between devices, send(): return lax.ppermute(block, 'inter', pairs[k])  354 us
    ppermute x60, waiting for transfers between devices, send(): return lax.ppermute(block, 'inter', pairs[k])  157 us
    pallas_call x2, Pallas kernels, front(): pl.pallas_call(functools.partial(front_kernel, group), grid=(chunk,), in_...  63.5 us
    dynamic_slice x34, local copies, waits for them, and re-layouts, on_device(): lax.dynamic_slice(stem, (zero, zero, target[k] * jnp.uint32(local_b) + jn...  51 us
    pallas_call x1, Pallas kernels, last_b(): pl.pallas_call(functools.partial(last_kernel, n), grid=(local_a // STEP_R...  31.3 us
    gather x4, local copies, waits for them, and re-layouts, on_device(): one = one[:, where_from][:, :, :, where_to].reshape(2, size_a, size_a)  23 us
    scatter x1, local copies, waits for them, and re-layouts, on_device(): permuted = jnp.zeros_like(branch_two).at[:, mode_order, :].set(branch_two)  18.2 us
    pallas_call x1, Pallas kernels, partial_b(): pl.pallas_call(functools.partial(partial_kernel, n), in_specs=[pl.BlockSp...  17.7 us
  transfers between devices with their start and end apart: 60, of which 18 were waited for; matrix products, arithmetic and copies ran while one was open for 17% of the time, Pallas kernels for 10%

commit v1 on v0

--- a/solution.py
+++ b/solution.py
@@ -13,6 +13,7 @@
 
 ROWS = 8
 STEP_ROWS = 2
+SUMS = 4
 
 
 def complex_mix(input_real, input_imag, weight_real, weight_imag, pattern):
@@ -154,7 +155,7 @@
         ],
         out_specs=[pl.BlockSpec((2, local_a, ROWS, width), lambda b: (0, 0, b // ROWS, 0))]
         * group,
-        out_shape=[jax.ShapeDtypeStruct((2, local_a, chunk, width), jnp.bfloat16)] * group,
+        out_shape=[pltpu.HBM((2, local_a, chunk, width), jnp.bfloat16)] * group,
         scratch_shapes=[
             pltpu.VMEM((2 * total, width), jnp.bfloat16),
             pltpu.VMEM((2 * width // 128, total * ROWS, 128), jnp.float32),
@@ -173,10 +174,7 @@
     return jnp.dot(w3[...], x[...], preferred_element_type=jnp.float32)
 
 
-def partial_kernel(n, *refs):
-    pieces, w3, out, buffers, x, sems = refs[:n], refs[n], *refs[n + 1 :]
-    steps = out.shape[0] // STEP_ROWS
-
+def in_steps(pieces, buffers, sems, steps, body):
     def copies(step, slot):
         rows = pl.ds(step * STEP_ROWS, STEP_ROWS)
         return [
@@ -198,57 +196,100 @@
 
         for copy in copies(step, slot):
             copy.wait()
-        held = [buffers.at[slot, i] for i in range(n)]
+        body(step, [buffers.at[slot, i] for i in range(len(pieces))])
+
+
+def by_part(row, rows, parts, body):
+    for part in range(parts):
+
+        @pl.when((row >= part * rows) & (row < (part + 1) * rows))
+        def _():
+            body(part, row - part * rows)
+
+
+def partial_kernel(n, *refs):
+    pieces, w3, outs, (buffers, x, sems) = refs[:n], refs[n], refs[n + 1 : -3], refs[-3:]
+    rows = outs[0].shape[0]
+
+    def body(step, held):
         for t in range(STEP_ROWS):
-            out[step * STEP_ROWS + t] = mix_rows(held, w3, x.at[t], t)
-
-
-def partial_b(pieces, w3):
-    _, local_a, chunk, width = pieces[0].shape
-    n = len(pieces)
-    return pl.pallas_call(
-        functools.partial(partial_kernel, n),
-        in_specs=[pl.BlockSpec(memory_space=pl.ANY)] * n
-        + [pl.BlockSpec(memory_space=pltpu.VMEM)],
-        out_specs=pl.BlockSpec(memory_space=pltpu.VMEM),
-        out_shape=jax.ShapeDtypeStruct((local_a, w3.shape[0], width), jnp.float32),
-        scratch_shapes=[
-            pltpu.VMEM((2, n, 2, STEP_ROWS, chunk, width), jnp.bfloat16),
-            pltpu.VMEM((STEP_ROWS, 2 * n * chunk, width), jnp.bfloat16),
-            pltpu.SemaphoreType.DMA((2, n)),
-        ],
-        compiler_params=pltpu.CompilerParams(vmem_limit_bytes=12 << 20),
-        name="partial",
-    )(*pieces, w3)
+            y = mix_rows(held, w3, x.at[t], t)
+
+            def store(part, row):
+                outs[part][row] = y
+
+            by_part(step * STEP_ROWS + t, rows, len(outs), store)
+
+    in_steps(pieces, buffers, sems, rows * len(outs) // STEP_ROWS, body)
 
 
 def last_kernel(n, *refs):
-    pieces, w3, base, out, x = refs[:n], *refs[n:]
-    for t in range(out.shape[0]):
-        y = base[t] + mix_rows(pieces, w3, x.at[t], t)
-        split = y.shape[1] // 128
-        for h in range(split):
-            out[t, pl.ds(h, y.shape[0], stride=split), :] = y[:, h * 128 : (h + 1) * 128]
-
-
-def last_b(pieces, w3, base):
+    pieces, w3, bases = refs[:n], refs[n], refs[n + 1 : -6]
+    out, buffers, x, held_out, sems, out_sems = refs[-6:]
+    rows = bases[0].shape[0]
+    steps = rows * len(bases) // STEP_ROWS
+
+    def copy_out(step, slot):
+        lines = pl.ds(step * STEP_ROWS, STEP_ROWS)
+        return pltpu.make_async_copy(held_out.at[slot], out.at[lines], out_sems.at[slot])
+
+    def body(step, held):
+        slot = lax.rem(step, 2)
+
+        @pl.when(step >= 2)
+        def _():
+            copy_out(step - 2, slot).wait()
+
+        for t in range(STEP_ROWS):
+            y = mix_rows(held, w3, x.at[t], t)
+
+            def store(part, row):
+                total = bases[part][row] + y
+                split = y.shape[1] // 128
+                for h in range(split):
+                    lines = pl.ds(h, y.shape[0], stride=split)
+                    held_out[slot, t, lines, :] = total[:, h * 128 : (h + 1) * 128]
+
+            by_part(step * STEP_ROWS + t, rows, len(bases), store)
+        copy_out(step, slot).start()
+
+    in_steps(pieces, buffers, sems, steps, body)
+    for step in range(max(steps - 2, 0), steps):
+        copy_out(step, step % 2).wait()
+
+
+def mix_b(pieces, w3, bases=()):
     _, local_a, chunk, width = pieces[0].shape
     n = len(pieces)
     lines = w3.shape[0] * (width // 128)
+    scratch = [
+        pltpu.VMEM((2, n, 2, STEP_ROWS, chunk, width), jnp.bfloat16),
+        pltpu.VMEM((STEP_ROWS, 2 * n * chunk, width), jnp.bfloat16),
+    ]
+    sems = [pltpu.SemaphoreType.DMA((2, n))]
+    vmem = pl.BlockSpec(memory_space=pltpu.VMEM)
+    hbm = pl.BlockSpec(memory_space=pl.ANY)
+    if bases:
+        scratch += [pltpu.VMEM((2, STEP_ROWS, lines, 128), jnp.float32)]
+        sems += [pltpu.SemaphoreType.DMA((2,))]
+        bases = [pltpu.with_memory_space_constraint(base, pltpu.VMEM) for base in bases]
+        shape, out_specs = jax.ShapeDtypeStruct((local_a, lines, 128), jnp.float32), hbm
+    else:
+        part = pltpu.VMEM((local_a // SUMS, w3.shape[0], width), jnp.float32)
+        shape, out_specs = [part] * SUMS, [vmem] * SUMS
     return pl.pallas_call(
-        functools.partial(last_kernel, n),
-        grid=(local_a // STEP_ROWS,),
-        in_specs=[pl.BlockSpec((2, STEP_ROWS, chunk, width), lambda a: (0, a, 0, 0))] * n
-        + [
-            pl.BlockSpec(w3.shape, lambda a: (0, 0)),
-            pl.BlockSpec((STEP_ROWS,) + base.shape[1:], lambda a: (a, 0, 0)),
-        ],
-        out_specs=pl.BlockSpec((STEP_ROWS, lines, 128), lambda a: (a, 0, 0)),
-        out_shape=jax.ShapeDtypeStruct((local_a, lines, 128), jnp.float32),
-        scratch_shapes=[pltpu.VMEM((STEP_ROWS, 2 * n * chunk, width), jnp.bfloat16)],
-        compiler_params=pltpu.CompilerParams(vmem_limit_bytes=20 << 20),
-        name="last",
-    )(*pieces, w3, base)
+        functools.partial(last_kernel if bases else partial_kernel, n),
+        in_specs=[hbm] * n + [vmem] * (1 + len(bases)),
+        out_specs=out_specs,
+        out_shape=shape,
+        scratch_shapes=scratch + sems,
+        compiler_params=pltpu.CompilerParams(vmem_limit_bytes=12 << 20),
+        name="last" if bases else "partial",
+    )(
+        *[pltpu.with_memory_space_constraint(piece, pltpu.HBM) for piece in pieces],
+        w3,
+        *bases,
+    )
 
 
 def on_device(stem_tensor, branch_one, branch_two, mode_order, branch_three, closing):
@@ -262,6 +303,7 @@
     if (
         local_b % (B_CHUNKS * 2 * ROWS)
         or local_a % ROWS
+        or local_a % (SUMS * STEP_ROWS)
         or width % 128
         or stem_tensor.shape[3] != 1
     ):
@@ -334,8 +376,8 @@
         pieces = front(arrived[j], w1, w2, close[:, :, j * chunk : (j + 1) * chunk])
         returned.append([send(piece, k) for k, piece in enumerate(pieces)])
 
-    base = partial_b(returned[0], w3[0])
-    out = last_b(returned[1], w3[1], base)
+    sums = mix_b(returned[0], w3[0])
+    out = mix_b(returned[1], w3[1], sums)
     return out.reshape(local_a, size_b, 2, 1, width)
 
 

time: 778 us -> 775 us (level)
  waiting for transfers between devices: 157 us -> 173 us
  starting transfers between devices: 354 us -> 341 us
  local copies, waits for them, and re-layouts: 142 us -> 131 us
    ppermute x60, waiting for transfers between devices: 157 us -> 173 us  [send(): return lax.ppermute(block, 'inter', pairs[k])]
    ppermute x60, starting transfers between devices: 354 us -> 341 us  [send(): return lax.ppermute(block, 'inter', pairs[k])]
    unnamed x104 -> x152, local copies, waits for them, and re-layouts: 15.6 us -> 6.84 us
    pallas_call x2, Pallas kernels: 49 us -> 56.8 us  [mix_b(): pl.pallas_call(functools.partial(last_kernel if bases else partial_kernel...]
  transfers between devices with their start and end apart: 60 -> 60, of which waited for: 18 -> 16; matrix products, arithmetic and copies ran while one was open for 17% -> 16% of each run, Pallas kernels for 10% -> 12%
where the time goes in v1:
time: 775 us; the launch traced here: 772 us
  starting transfers between devices  341 us (44%)
  waiting for transfers between devices  173 us (22%)
  local copies, waits for them, and re-layouts  131 us (17%)
  Pallas kernels  119 us (15%)
    ppermute x60, starting transfers between devices, send(): return lax.ppermute(block, 'inter', pairs[k])  341 us
    ppermute x60, waiting for transfers between devices, send(): return lax.ppermute(block, 'inter', pairs[k])  173 us
    pallas_call x2, Pallas kernels, front(): pl.pallas_call(functools.partial(front_kernel, group), grid=(chunk,), in_...  62.4 us
    pallas_call x2, Pallas kernels, mix_b(): pl.pallas_call(functools.partial(last_kernel if bases else partial_kernel...  56.8 us
    dynamic_slice x34, local copies, waits for them, and re-layouts, on_device(): lax.dynamic_slice(stem, (zero, zero, target[k] * jnp.uint32(local_b) + jn...  51.3 us
    gather x4, local copies, waits for them, and re-layouts, on_device(): one = one[:, where_from][:, :, :, where_to].reshape(2, size_a, size_a)  23 us
    scatter x1, local copies, waits for them, and re-layouts, on_device(): permuted = jnp.zeros_like(branch_two).at[:, mode_order, :].set(branch_two)  18.2 us
  transfers between devices with their start and end apart: 60, of which 16 were waited for; matrix products, arithmetic and copies ran while one was open for 16% of the time, Pallas kernels for 12%

profile of v1, /device:TPU:1, one launch (start us, length us, event | category | flops | bytes accessed | tf_op | source)
XLA Modules:
  0.0 771.8 jit_solution(18122738418602188260)
XLA Ops:
  30.9 7.5 constant_dynamic-slice_fusion
  43.1 29.7 %collective-permute-start.7 = (bf16[2,16,32,256]{3,2,1,0:T(8,128)(2,1)}, bf16[2,16,32,256]{3,2,1,0:T(8,128)(2,1)}, u32[]{:S(2)}, u32[]{:S(2)}) collective-permute-start(bf16[2,16,32,256]{3,2,1,0:T(8,128)(2,1)} %bitcast.211), channel_id=1, source_target_pairs={{0,8},{1,9},{2,10},{3,11},{4,0},{5,1},{6,2},{7,3},{8,12},{9,13},{1... | collective-permute-start | bytes 1572872 | tf_op jit(solution)/shard_map/ppermute | solution.py:322
  72.8 31.6 %collective-permute-start.9 = (bf16[2,16,32,256]{3,2,1,0:T(8,128)(2,1)}, bf16[2,16,32,256]{3,2,1,0:T(8,128)(2,1)}, u32[]{:S(2)}, u32[]{:S(2)}) collective-permute-start(bf16[2,16,32,256]{3,2,1,0:T(8,128)(2,1)} %bitcast.209), channel_id=1, source_target_pairs={{0,10},{1,11},{2,8},{3,9},{4,2},{5,3},{6,0},{7,1},{8,14},{9,15},{1... | collective-permute-start | bytes 1572872 | tf_op jit(solution)/shard_map/ppermute | solution.py:322
  127.2 19.8 %collective-permute-start.11 = (bf16[2,16,32,256]{3,2,1,0:T(8,128)(2,1)S(1)}, bf16[2,16,32,256]{3,2,1,0:T(8,128)(2,1)S(1)}, u32[]{:S(2)}, u32[]{:S(2)}) collective-permute-start(bf16[2,16,32,256]{3,2,1,0:T(8,128)(2,1)S(1)} %bitcast.248), channel_id=1, source_target_pairs={{0,4},{1,5},{2,6},{3,7},{4,12},{5,13},{6,14},{7,15},{8,0},{9,1},{1... | collective-permute-start | bytes 1572872 | tf_op jit(solution)/shard_map/ppermute | solution.py:322
  162.0 9.3 %collective-permute-done.43.refs_14_ = bf16[2,16,32,256]{3,2,1,0:T(8,128)(2,1)S(1)} collective-permute-done((bf16[2,16,32,256]{3,2,1,0:T(8,128)(2,1)}, bf16[2,16,32,256]{3,2,1,0:T(8,128)(2,1)S(1)}, u32[]{:S(2)}, u32[]{:S(2)}) %collective-permute-start.43) | collective-permute-done | bytes 524320 | tf_op jit(solution)/shard_map/ppermute | solution.py:322
  171.4 9.9 %collective-permute-done.12.refs_13_ = bf16[2,16,32,256]{3,2,1,0:T(8,128)(2,1)S(1)} collective-permute-done((bf16[2,16,32,256]{3,2,1,0:T(8,128)(2,1)S(1)}, bf16[2,16,32,256]{3,2,1,0:T(8,128)(2,1)S(1)}, u32[]{:S(2)}, u32[]{:S(2)}) %collective-permute-start.12) | collective-permute-done | bytes 524320 | tf_op jit(solution)/shard_map/ppermute | solution.py:322
  183.5 10.4 %collective-permute-done.13.refs_14_ = bf16[2,16,32,256]{3,2,1,0:T(8,128)(2,1)S(1)} collective-permute-done((bf16[2,16,32,256]{3,2,1,0:T(8,128)(2,1)}, bf16[2,16,32,256]{3,2,1,0:T(8,128)(2,1)S(1)}, u32[]{:S(2)}, u32[]{:S(2)}) %collective-permute-start.13) | collective-permute-done | bytes 524320 | tf_op jit(solution)/shard_map/ppermute | solution.py:322
  202.7 18.2 %scatter_fusion = bf16[2,256,256]{2,0,1:T(2,128)(2,1)S(1)} fusion(bf16[2,256,256]{2,0,1:T(2,128)(2,1)S(1)} %broadcast_in_dim.4, s32[256]{0:T(256)S(1)} %compare_select_fusion, bf16[256,2,256]{2,1,0:T(2,128)(2,1)} %copy.111), kind=kCustom, calls=%fused_computation.4 | custom fusion | bytes 787456 | tf_op jit(solution)/shard_map/scatter | solution.py:350
  268.4 7.1 copy.110
  275.5 6.8 reshape.545
  287.6 7.5 collective-permute-start.39
  295.1 22.7 %collective-permute-start.40 = (bf16[2,16,32,256]{3,2,1,0:T(8,128)(2,1)S(1)}, bf16[2,16,32,256]{3,2,1,0:T(8,128)(2,1)S(1)}, u32[]{:S(2)}, u32[]{:S(2)}) collective-permute-start(bf16[2,16,32,256]{3,2,1,0:T(8,128)(2,1)S(1)} %bitcast.245), channel_id=1, source_target_pairs={{0,11},{1,8},{2,9},{3,10},{4,3},{5,0},{6,1},{7,2},{8,15},{9,12},{1... | collective-permute-start | bytes 1572872 | tf_op jit(solution)/shard_map/ppermute | solution.py:322
  317.9 21.9 %collective-permute-start.41 = (bf16[2,16,32,256]{3,2,1,0:T(8,128)(2,1)S(1)}, bf16[2,16,32,256]{3,2,1,0:T(8,128)(2,1)S(1)}, u32[]{:S(2)}, u32[]{:S(2)}) collective-permute-start(bf16[2,16,32,256]{3,2,1,0:T(8,128)(2,1)S(1)} %bitcast.243), channel_id=1, source_target_pairs={{0,4},{1,5},{2,6},{3,7},{4,12},{5,13},{6,14},{7,15},{8,0},{9,1},{1... | collective-permute-start | bytes 1572872 | tf_op jit(solution)/shard_map/ppermute | solution.py:322
  342.3 31.2 %front.2 = (bf16[2,32,16,256]{3,2,1,0:T(8,128)(2,1)}, bf16[2,32,16,256]{3,2,1,0:T(8,128)(2,1)}, bf16[2,32,16,256]{3,2,1,0:T(8,128)(2,1)}, bf16[2,32,16,256]{3,2,...) custom-call(bf16[2,16,32,256]{3,2,1,0:T(8,128)(2,1)S(1)} %bitcast.22, ...), custom_call_target="tpu_custom_call" | custom-call | tf_op jit(solution)/shard_map/front/pallas_call | solution.py:147
  396.3 27.8 %collective-permute-done.17.refs_3_ = bf16[2,32,16,256]{3,2,1,0:T(8,128)(2,1)S(1)} collective-permute-done((bf16[2,32,16,256]{3,2,1,0:T(8,128)(2,1)}, bf16[2,32,16,256]{3,2,1,0:T(8,128)(2,1)S(1)}, u32[]{:S(2)}, u32[]{:S(2)}) %collective-permute-start.17) | collective-permute-done | bytes 524320 | tf_op jit(solution)/shard_map/ppermute | solution.py:322
  424.1 14.0 %collective-permute-start.22 = (bf16[2,32,16,256]{3,2,1,0:T(8,128)(2,1)}, bf16[2,32,16,256]{3,2,1,0:T(8,128)(2,1)S(1)}, u32[]{:S(2)}, u32[]{:S(2)}) collective-permute-start(bf16[2,32,16,256]{3,2,1,0:T(8,128)(2,1)} %get-tuple-element.55), channel_id=1, source_target_pairs={{0,8},{1,9},{2,10},{3,11},{4,0},{5,1},{6,2},{7,3},{8,12},{9,13},{1... | collective-permute-start | bytes 1572872 | tf_op jit(solution)/shard_map/ppermute | solution.py:322
  438.1 31.6 %collective-permute-start.24 = (bf16[2,32,16,256]{3,2,1,0:T(8,128)(2,1)}, bf16[2,32,16,256]{3,2,1,0:T(8,128)(2,1)S(1)}, u32[]{:S(2)}, u32[]{:S(2)}) collective-permute-start(bf16[2,32,16,256]{3,2,1,0:T(8,128)(2,1)} %get-tuple-element.57), channel_id=1, source_target_pairs={{0,10},{1,11},{2,8},{3,9},{4,2},{5,3},{6,0},{7,1},{8,14},{9,15},{1... | collective-permute-start | bytes 1572872 | tf_op jit(solution)/shard_map/ppermute | solution.py:322
  469.9 31.1 %front.3 = (bf16[2,32,16,256]{3,2,1,0:T(8,128)(2,1)}, bf16[2,32,16,256]{3,2,1,0:T(8,128)(2,1)}, bf16[2,32,16,256]{3,2,1,0:T(8,128)(2,1)}, bf16[2,32,16,256]{3,2,...) custom-call(bf16[2,16,32,256]{3,2,1,0:T(8,128)(2,1)S(1)} %bitcast.22, ...), custom_call_target="tpu_custom_call" | custom-call | tf_op jit(solution)/shard_map/front/pallas_call | solution.py:147
  507.1 10.0 %collective-permute-done.45.refs_1_ = bf16[2,32,16,256]{3,2,1,0:T(8,128)(2,1)S(1)} collective-permute-done((bf16[2,32,16,256]{3,2,1,0:T(8,128)(2,1)}, bf16[2,32,16,256]{3,2,1,0:T(8,128)(2,1)S(1)}, u32[]{:S(2)}, u32[]{:S(2)}) %collective-permute-start.45) | collective-permute-done | bytes 524320 | tf_op jit(solution)/shard_map/ppermute | solution.py:322
  521.0 26.6 %collective-permute-done.47.refs_3_ = bf16[2,32,16,256]{3,2,1,0:T(8,128)(2,1)S(1)} collective-permute-done((bf16[2,32,16,256]{3,2,1,0:T(8,128)(2,1)}, bf16[2,32,16,256]{3,2,1,0:T(8,128)(2,1)S(1)}, u32[]{:S(2)}, u32[]{:S(2)}) %collective-permute-start.47) | collective-permute-done | bytes 524320 | tf_op jit(solution)/shard_map/ppermute | solution.py:322
  547.5 14.2 %collective-permute-start.52 = (bf16[2,32,16,256]{3,2,1,0:T(8,128)(2,1)}, bf16[2,32,16,256]{3,2,1,0:T(8,128)(2,1)S(1)}, u32[]{:S(2)}, u32[]{:S(2)}) collective-permute-start(bf16[2,32,16,256]{3,2,1,0:T(8,128)(2,1)} %get-tuple-element.72), channel_id=1, source_target_pairs={{0,8},{1,9},{2,10},{3,11},{4,0},{5,1},{6,2},{7,3},{8,12},{9,13},{1... | collective-permute-start | bytes 1572872 | tf_op jit(solution)/shard_map/ppermute | solution.py:322
  563.0 30.5 %collective-permute-start.54 = (bf16[2,32,16,256]{3,2,1,0:T(8,128)(2,1)}, bf16[2,32,16,256]{3,2,1,0:T(8,128)(2,1)S(1)}, u32[]{:S(2)}, u32[]{:S(2)}) collective-permute-start(bf16[2,32,16,256]{3,2,1,0:T(8,128)(2,1)} %get-tuple-element.74), channel_id=1, source_target_pairs={{0,10},{1,11},{2,8},{3,9},{4,2},{5,3},{6,0},{7,1},{8,14},{9,15},{1... | collective-permute-start | bytes 1572872 | tf_op jit(solution)/shard_map/ppermute | solution.py:322
  593.5 22.7 %collective-permute-start.55 = (bf16[2,32,16,256]{3,2,1,0:T(8,128)(2,1)}, bf16[2,32,16,256]{3,2,1,0:T(8,128)(2,1)S(1)}, u32[]{:S(2)}, u32[]{:S(2)}) collective-permute-start(bf16[2,32,16,256]{3,2,1,0:T(8,128)(2,1)} %get-tuple-element.75), channel_id=1, source_target_pairs={{0,11},{1,8},{2,9},{3,10},{4,3},{5,0},{6,1},{7,2},{8,15},{9,12},{1... | collective-permute-start | bytes 1572872 | tf_op jit(solution)/shard_map/ppermute | solution.py:322
  616.2 21.4 %collective-permute-start.56 = (bf16[2,32,16,256]{3,2,1,0:T(8,128)(2,1)}, bf16[2,32,16,256]{3,2,1,0:T(8,128)(2,1)S(1)}, u32[]{:S(2)}, u32[]{:S(2)}) collective-permute-start(bf16[2,32,16,256]{3,2,1,0:T(8,128)(2,1)} %get-tuple-element.76), channel_id=1, source_target_pairs={{0,4},{1,5},{2,6},{3,7},{4,12},{5,13},{6,14},{7,15},{8,0},{9,1},{1... | collective-permute-start | bytes 1572872 | tf_op jit(solution)/shard_map/ppermute | solution.py:322
  644.2 6.5 collective-permute-done.56.refs_12_
  651.4 10.6 %collective-permute-done.57.refs_13_ = bf16[2,32,16,256]{3,2,1,0:T(8,128)(2,1)S(1)} collective-permute-done((bf16[2,32,16,256]{3,2,1,0:T(8,128)(2,1)}, bf16[2,32,16,256]{3,2,1,0:T(8,128)(2,1)S(1)}, u32[]{:S(2)}, u32[]{:S(2)}) %collective-permute-start.57) | collective-permute-done | bytes 524320 | tf_op jit(solution)/shard_map/ppermute | solution.py:322
  663.8 8.6 %collective-permute-done.58.refs_14_ = bf16[2,32,16,256]{3,2,1,0:T(8,128)(2,1)S(1)} collective-permute-done((bf16[2,32,16,256]{3,2,1,0:T(8,128)(2,1)}, bf16[2,32,16,256]{3,2,1,0:T(8,128)(2,1)S(1)}, u32[]{:S(2)}, u32[]{:S(2)}) %collective-permute-start.58) | collective-permute-done | bytes 524320 | tf_op jit(solution)/shard_map/ppermute | solution.py:322
  674.8 11.7 %collective-permute-done.59.refs_15_ = bf16[2,32,16,256]{3,2,1,0:T(8,128)(2,1)S(1)} collective-permute-done((bf16[2,32,16,256]{3,2,1,0:T(8,128)(2,1)}, bf16[2,32,16,256]{3,2,1,0:T(8,128)(2,1)S(1)}, u32[]{:S(2)}, u32[]{:S(2)}) %collective-permute-start.59) | collective-permute-done | bytes 524320 | tf_op jit(solution)/shard_map/ppermute | solution.py:322
  687.3 26.5 %partial.1 = (f32[8,1024,256]{2,1,0:T(8,128)S(1)}, f32[8,1024,256]{2,1,0:T(8,128)S(1)}, f32[8,1024,256]{2,1,0:T(8,128)S(1)}, f32[8,1024,256]{2,1,0:T(8,128)S(1)}) custom-call(bf16[2,32,16,256]{3,2,1,0:T(8,128)(2,1)} %get-tuple-element.64.refs_0_, bf16[2,32,16,256]{3,2,1,0:T(8,128)(2,1)} %copy-done.56, bf16[2,32,16,256]{3,2,1,0:T(8,128)(2,1)} %copy-done.57, ...), custom_call_target="tpu_custom_call" | custom-call | tf_op jit(solution)/shard_map/partial/pallas_call | solution.py:280
  718.1 10.5 %collective-permute-done.28.refs_14_ = bf16[2,32,16,256]{3,2,1,0:T(8,128)(2,1)S(1)} collective-permute-done((bf16[2,32,16,256]{3,2,1,0:T(8,128)(2,1)}, bf16[2,32,16,256]{3,2,1,0:T(8,128)(2,1)S(1)}, u32[]{:S(2)}, u32[]{:S(2)}) %collective-permute-start.28) | collective-permute-done | bytes 524320 | tf_op jit(solution)/shard_map/ppermute | solution.py:322
  728.6 11.9 %collective-permute-done.29.refs_15_ = bf16[2,32,16,256]{3,2,1,0:T(8,128)(2,1)S(1)} collective-permute-done((bf16[2,32,16,256]{3,2,1,0:T(8,128)(2,1)}, bf16[2,32,16,256]{3,2,1,0:T(8,128)(2,1)S(1)}, u32[]{:S(2)}, u32[]{:S(2)}) %collective-permute-start.29) | collective-permute-done | bytes 524320 | tf_op jit(solution)/shard_map/ppermute | solution.py:322
  741.4 30.3 %last.1 = f32[32,2048,128]{2,1,0:T(8,128)} custom-call(bf16[2,32,16,256]{3,2,1,0:T(8,128)(2,1)} %get-tuple-element.47.refs_0_, bf16[2,32,16,256]{3,2,1,0:T(8,128)(2,1)} %copy-done.41, bf16[2,32,16,256]{3,2,1,0:T(8,128)(2,1)} %copy-done.42, bf16[2,32,16,256]{3,2,1,0:T(8,128)(2,1)} %copy-done.43, bf16[2,32,16,256]{3,2,1,0:T(8,128)(2,1)} %copy-done.44, ...), custom_call_target="tpu_custom_call" | custom-call | tf_op jit(solution)/shard_map/last/pallas_call | solution.py:280
  (315 shorter events, 190.5 us)
Async XLA Ops:
  15.9 56.9 %collective-permute-start.3 = (bf16[2,16,32,256]{3,2,1,0:T(8,128)(2,1)}, bf16[2,16,32,256]{3,2,1,0:T(8,128)(2,1)S(1)}, u32[]{:S(2)}, u32[]{:S(2)}) collective-permute-start(bf16[2,16,32,256]{3,2,1,0:T(8,128)(2,1)} %bitcast.215), channel_id=1, source_target_pairs={{0,3},{1,0},{2,1},{3,2},{4,7},{5,4},{6,5},{7,6},{8,11},{9,8},{10,9... | collective-permute-start | bytes 1572872 | tf_op jit(solution)/shard_map/ppermute | solution.py:322
  38.5 84.9 %collective-permute-start.5 = (bf16[2,16,32,256]{3,2,1,0:T(8,128)(2,1)}, bf16[2,16,32,256]{3,2,1,0:T(8,128)(2,1)S(1)}, u32[]{:S(2)}, u32[]{:S(2)}) collective-permute-start(bf16[2,16,32,256]{3,2,1,0:T(8,128)(2,1)} %bitcast.213), channel_id=1, source_target_pairs={{0,14},{1,15},{2,12},{3,13},{4,10},{5,11},{6,8},{7,9},{8,6},{9,7},... | collective-permute-start | bytes 1572872 | tf_op jit(solution)/shard_map/ppermute | solution.py:322
  43.0 84.2 %collective-permute-start.6 = (bf16[2,16,32,256]{3,2,1,0:T(8,128)(2,1)}, bf16[2,16,32,256]{3,2,1,0:T(8,128)(2,1)S(1)}, u32[]{:S(2)}, u32[]{:S(2)}) collective-permute-start(bf16[2,16,32,256]{3,2,1,0:T(8,128)(2,1)} %bitcast.212), channel_id=1, source_target_pairs={{0,15},{1,12},{2,13},{3,14},{4,11},{5,8},{6,9},{7,10},{8,7},{9,4},... | collective-permute-start | bytes 1572872 | tf_op jit(solution)/shard_map/ppermute | solution.py:322
  43.1 103.9 %collective-permute-start.7 = (bf16[2,16,32,256]{3,2,1,0:T(8,128)(2,1)}, bf16[2,16,32,256]{3,2,1,0:T(8,128)(2,1)}, u32[]{:S(2)}, u32[]{:S(2)}) collective-permute-start(bf16[2,16,32,256]{3,2,1,0:T(8,128)(2,1)} %bitcast.211), channel_id=1, source_target_pairs={{0,8},{1,9},{2,10},{3,11},{4,0},{5,1},{6,2},{7,3},{8,12},{9,13},{1... | collective-permute-start | bytes 1572872 | tf_op jit(solution)/shard_map/ppermute | solution.py:322
  72.8 74.2 %collective-permute-start.8 = (bf16[2,16,32,256]{3,2,1,0:T(8,128)(2,1)}, bf16[2,16,32,256]{3,2,1,0:T(8,128)(2,1)}, u32[]{:S(2)}, u32[]{:S(2)}) collective-permute-start(bf16[2,16,32,256]{3,2,1,0:T(8,128)(2,1)} %bitcast.210), channel_id=1, source_target_pairs={{0,9},{1,10},{2,11},{3,8},{4,1},{5,2},{6,3},{7,0},{8,13},{9,14},{1... | collective-permute-start | bytes 1572872 | tf_op jit(solution)/shard_map/ppermute | solution.py:322
  72.8 76.6 %collective-permute-start.9 = (bf16[2,16,32,256]{3,2,1,0:T(8,128)(2,1)}, bf16[2,16,32,256]{3,2,1,0:T(8,128)(2,1)}, u32[]{:S(2)}, u32[]{:S(2)}) collective-permute-start(bf16[2,16,32,256]{3,2,1,0:T(8,128)(2,1)} %bitcast.209), channel_id=1, source_target_pairs={{0,10},{1,11},{2,8},{3,9},{4,2},{5,3},{6,0},{7,1},{8,14},{9,15},{1... | collective-permute-start | bytes 1572872 | tf_op jit(solution)/shard_map/ppermute | solution.py:322
  152.3 69.8 %collective-permute-start.14 = (bf16[2,16,32,256]{3,2,1,0:T(8,128)(2,1)}, bf16[2,16,32,256]{3,2,1,0:T(8,128)(2,1)}, u32[]{:S(2)}, u32[]{:S(2)}) collective-permute-start(bf16[2,16,32,256]{3,2,1,0:T(8,128)(2,1)} %bitcast.204), channel_id=1, source_target_pairs={{0,7},{1,4},{2,5},{3,6},{4,15},{5,12},{6,13},{7,14},{8,3},{9,0},{1... | collective-permute-start | bytes 1572872 | tf_op jit(solution)/shard_map/ppermute | solution.py:322
  161.2 63.3 %collective-permute-start.30 = (bf16[2,16,32,256]{3,2,1,0:T(8,128)(2,1)}, bf16[2,16,32,256]{3,2,1,0:T(8,128)(2,1)S(1)}, u32[]{:S(2)}, u32[]{:S(2)}) collective-permute-start(bf16[2,16,32,256]{3,2,1,0:T(8,128)(2,1)} %bitcast.202), channel_id=1, source_target_pairs={{0,12},{1,13},{2,14},{3,15},{4,8},{5,9},{6,10},{7,11},{8,4},{9,5},... | collective-permute-start | bytes 1572872 | tf_op jit(solution)/shard_map/ppermute | solution.py:322
  222.1 65.5 %collective-permute-start.34 = (bf16[2,16,32,256]{3,2,1,0:T(8,128)(2,1)}, bf16[2,16,32,256]{3,2,1,0:T(8,128)(2,1)}, u32[]{:S(2)}, u32[]{:S(2)}) collective-permute-start(bf16[2,16,32,256]{3,2,1,0:T(8,128)(2,1)} %bitcast.246), channel_id=1, source_target_pairs={{0,13},{1,14},{2,15},{3,12},{4,9},{5,10},{6,11},{7,8},{8,5},{9,6},... | collective-permute-start | bytes 1572872 | tf_op jit(solution)/shard_map/ppermute | solution.py:322
  224.6 70.5 %collective-permute-start.35 = (bf16[2,16,32,256]{3,2,1,0:T(8,128)(2,1)}, bf16[2,16,32,256]{3,2,1,0:T(8,128)(2,1)}, u32[]{:S(2)}, u32[]{:S(2)}) collective-permute-start(bf16[2,16,32,256]{3,2,1,0:T(8,128)(2,1)} %bitcast.244), channel_id=1, source_target_pairs={{0,14},{1,15},{2,12},{3,13},{4,10},{5,11},{6,8},{7,9},{8,6},{9,7},... | collective-permute-start | bytes 1572872 | tf_op jit(solution)/shard_map/ppermute | solution.py:322
  227.6 90.3 %collective-permute-start.36 = (bf16[2,16,32,256]{3,2,1,0:T(8,128)(2,1)}, bf16[2,16,32,256]{3,2,1,0:T(8,128)(2,1)}, u32[]{:S(2)}, u32[]{:S(2)}) collective-permute-start(bf16[2,16,32,256]{3,2,1,0:T(8,128)(2,1)} %bitcast.242), channel_id=1, source_target_pairs={{0,15},{1,12},{2,13},{3,14},{4,11},{5,8},{6,9},{7,10},{8,7},{9,4},... | collective-permute-start | bytes 1572872 | tf_op jit(solution)/shard_map/ppermute | solution.py:322
  227.8 112.0 %collective-permute-start.37 = (bf16[2,16,32,256]{3,2,1,0:T(8,128)(2,1)}, bf16[2,16,32,256]{3,2,1,0:T(8,128)(2,1)}, u32[]{:S(2)}, u32[]{:S(2)}) collective-permute-start(bf16[2,16,32,256]{3,2,1,0:T(8,128)(2,1)} %bitcast.240), channel_id=1, source_target_pairs={{0,8},{1,9},{2,10},{3,11},{4,0},{5,1},{6,2},{7,3},{8,12},{9,13},{1... | collective-permute-start | bytes 1572872 | tf_op jit(solution)/shard_map/ppermute | solution.py:322
  230.0 110.6 %collective-permute-start.38 = (bf16[2,16,32,256]{3,2,1,0:T(8,128)(2,1)}, bf16[2,16,32,256]{3,2,1,0:T(8,128)(2,1)}, u32[]{:S(2)}, u32[]{:S(2)}) collective-permute-start(bf16[2,16,32,256]{3,2,1,0:T(8,128)(2,1)} %bitcast.238), channel_id=1, source_target_pairs={{0,9},{1,10},{2,11},{3,8},{4,1},{5,2},{6,3},{7,0},{8,13},{9,14},{1... | collective-permute-start | bytes 1572872 | tf_op jit(solution)/shard_map/ppermute | solution.py:322
  287.6 86.0 %collective-permute-start.39 = (bf16[2,16,32,256]{3,2,1,0:T(8,128)(2,1)S(1)}, bf16[2,16,32,256]{3,2,1,0:T(8,128)(2,1)S(1)}, u32[]{:S(2)}, u32[]{:S(2)}) collective-permute-start(bf16[2,16,32,256]{3,2,1,0:T(8,128)(2,1)S(1)} %bitcast.247), channel_id=1, source_target_pairs={{0,10},{1,11},{2,8},{3,9},{4,2},{5,3},{6,0},{7,1},{8,14},{9,15},{1... | collective-permute-start | bytes 1572872 | tf_op jit(solution)/shard_map/ppermute | solution.py:322
  295.1 80.7 %collective-permute-start.40 = (bf16[2,16,32,256]{3,2,1,0:T(8,128)(2,1)S(1)}, bf16[2,16,32,256]{3,2,1,0:T(8,128)(2,1)S(1)}, u32[]{:S(2)}, u32[]{:S(2)}) collective-permute-start(bf16[2,16,32,256]{3,2,1,0:T(8,128)(2,1)S(1)} %bitcast.245), channel_id=1, source_target_pairs={{0,11},{1,8},{2,9},{3,10},{4,3},{5,0},{6,1},{7,2},{8,15},{9,12},{1... | collective-permute-start | bytes 1572872 | tf_op jit(solution)/shard_map/ppermute | solution.py:322
  317.9 60.5 %collective-permute-start.41 = (bf16[2,16,32,256]{3,2,1,0:T(8,128)(2,1)S(1)}, bf16[2,16,32,256]{3,2,1,0:T(8,128)(2,1)S(1)}, u32[]{:S(2)}, u32[]{:S(2)}) collective-permute-start(bf16[2,16,32,256]{3,2,1,0:T(8,128)(2,1)S(1)} %bitcast.243), channel_id=1, source_target_pairs={{0,4},{1,5},{2,6},{3,7},{4,12},{5,13},{6,14},{7,15},{8,0},{9,1},{1... | collective-permute-start | bytes 1572872 | tf_op jit(solution)/shard_map/ppermute | solution.py:322
  378.6 59.4 %collective-permute-start.18 = (bf16[2,32,16,256]{3,2,1,0:T(8,128)(2,1)}, bf16[2,32,16,256]{3,2,1,0:T(8,128)(2,1)S(1)}, u32[]{:S(2)}, u32[]{:S(2)}) collective-permute-start(bf16[2,32,16,256]{3,2,1,0:T(8,128)(2,1)} %get-tuple-element.51), channel_id=1, source_target_pairs={{0,3},{1,0},{2,1},{3,2},{4,7},{5,4},{6,5},{7,6},{8,11},{9,8},{10,9... | collective-permute-start | bytes 1572872 | tf_op jit(solution)/shard_map/ppermute | solution.py:322
  378.9 59.2 %collective-permute-start.19 = (bf16[2,32,16,256]{3,2,1,0:T(8,128)(2,1)}, bf16[2,32,16,256]{3,2,1,0:T(8,128)(2,1)S(1)}, u32[]{:S(2)}, u32[]{:S(2)}) collective-permute-start(bf16[2,32,16,256]{3,2,1,0:T(8,128)(2,1)} %get-tuple-element.52), channel_id=1, source_target_pairs={{0,13},{1,14},{2,15},{3,12},{4,9},{5,10},{6,11},{7,8},{8,5},{9,6},... | collective-permute-start | bytes 1572872 | tf_op jit(solution)/shard_map/ppermute | solution.py:322
  387.4 113.7 %collective-permute-start.20 = (bf16[2,32,16,256]{3,2,1,0:T(8,128)(2,1)}, bf16[2,32,16,256]{3,2,1,0:T(8,128)(2,1)S(1)}, u32[]{:S(2)}, u32[]{:S(2)}) collective-permute-start(bf16[2,32,16,256]{3,2,1,0:T(8,128)(2,1)} %get-tuple-element.53), channel_id=1, source_target_pairs={{0,14},{1,15},{2,12},{3,13},{4,10},{5,11},{6,8},{7,9},{8,6},{9,7},... | collective-permute-start | bytes 1572872 | tf_op jit(solution)/shard_map/ppermute | solution.py:322
  392.5 109.6 %collective-permute-start.21 = (bf16[2,32,16,256]{3,2,1,0:T(8,128)(2,1)}, bf16[2,32,16,256]{3,2,1,0:T(8,128)(2,1)S(1)}, u32[]{:S(2)}, u32[]{:S(2)}) collective-permute-start(bf16[2,32,16,256]{3,2,1,0:T(8,128)(2,1)} %get-tuple-element.54), channel_id=1, source_target_pairs={{0,15},{1,12},{2,13},{3,14},{4,11},{5,8},{6,9},{7,10},{8,7},{9,4},... | collective-permute-start | bytes 1572872 | tf_op jit(solution)/shard_map/ppermute | solution.py:322
  424.1 78.5 %collective-permute-start.22 = (bf16[2,32,16,256]{3,2,1,0:T(8,128)(2,1)}, bf16[2,32,16,256]{3,2,1,0:T(8,128)(2,1)S(1)}, u32[]{:S(2)}, u32[]{:S(2)}) collective-permute-start(bf16[2,32,16,256]{3,2,1,0:T(8,128)(2,1)} %get-tuple-element.55), channel_id=1, source_target_pairs={{0,8},{1,9},{2,10},{3,11},{4,0},{5,1},{6,2},{7,3},{8,12},{9,13},{1... | collective-permute-start | bytes 1572872 | tf_op jit(solution)/shard_map/ppermute | solution.py:322
  438.0 65.7 %collective-permute-start.23 = (bf16[2,32,16,256]{3,2,1,0:T(8,128)(2,1)}, bf16[2,32,16,256]{3,2,1,0:T(8,128)(2,1)S(1)}, u32[]{:S(2)}, u32[]{:S(2)}) collective-permute-start(bf16[2,32,16,256]{3,2,1,0:T(8,128)(2,1)} %get-tuple-element.56), channel_id=1, source_target_pairs={{0,9},{1,10},{2,11},{3,8},{4,1},{5,2},{6,3},{7,0},{8,13},{9,14},{1... | collective-permute-start | bytes 1572872 | tf_op jit(solution)/shard_map/ppermute | solution.py:322
  438.1 65.7 %collective-permute-start.24 = (bf16[2,32,16,256]{3,2,1,0:T(8,128)(2,1)}, bf16[2,32,16,256]{3,2,1,0:T(8,128)(2,1)S(1)}, u32[]{:S(2)}, u32[]{:S(2)}) collective-permute-start(bf16[2,32,16,256]{3,2,1,0:T(8,128)(2,1)} %get-tuple-element.57), channel_id=1, source_target_pairs={{0,10},{1,11},{2,8},{3,9},{4,2},{5,3},{6,0},{7,1},{8,14},{9,15},{1... | collective-permute-start | bytes 1572872 | tf_op jit(solution)/shard_map/ppermute | solution.py:322
  503.7 58.0 %collective-permute-start.48 = (bf16[2,32,16,256]{3,2,1,0:T(8,128)(2,1)}, bf16[2,32,16,256]{3,2,1,0:T(8,128)(2,1)S(1)}, u32[]{:S(2)}, u32[]{:S(2)}) collective-permute-start(bf16[2,32,16,256]{3,2,1,0:T(8,128)(2,1)} %get-tuple-element.68), channel_id=1, source_target_pairs={{0,3},{1,0},{2,1},{3,2},{4,7},{5,4},{6,5},{7,6},{8,11},{9,8},{10,9... | collective-permute-start | bytes 1572872 | tf_op jit(solution)/shard_map/ppermute | solution.py:322
  503.8 59.2 %collective-permute-start.49 = (bf16[2,32,16,256]{3,2,1,0:T(8,128)(2,1)}, bf16[2,32,16,256]{3,2,1,0:T(8,128)(2,1)S(1)}, u32[]{:S(2)}, u32[]{:S(2)}) collective-permute-start(bf16[2,32,16,256]{3,2,1,0:T(8,128)(2,1)} %get-tuple-element.69), channel_id=1, source_target_pairs={{0,13},{1,14},{2,15},{3,12},{4,9},{5,10},{6,11},{7,8},{8,5},{9,6},... | collective-permute-start | bytes 1572872 | tf_op jit(solution)/shard_map/ppermute | solution.py:322
  517.1 76.3 %collective-permute-start.50 = (bf16[2,32,16,256]{3,2,1,0:T(8,128)(2,1)}, bf16[2,32,16,256]{3,2,1,0:T(8,128)(2,1)S(1)}, u32[]{:S(2)}, u32[]{:S(2)}) collective-permute-start(bf16[2,32,16,256]{3,2,1,0:T(8,128)(2,1)} %get-tuple-element.70), channel_id=1, source_target_pairs={{0,14},{1,15},{2,12},{3,13},{4,10},{5,11},{6,8},{7,9},{8,6},{9,7},... | collective-permute-start | bytes 1572872 | tf_op jit(solution)/shard_map/ppermute | solution.py:322
  518.4 97.8 %collective-permute-start.51 = (bf16[2,32,16,256]{3,2,1,0:T(8,128)(2,1)}, bf16[2,32,16,256]{3,2,1,0:T(8,128)(2,1)S(1)}, u32[]{:S(2)}, u32[]{:S(2)}) collective-permute-start(bf16[2,32,16,256]{3,2,1,0:T(8,128)(2,1)} %get-tuple-element.71), channel_id=1, source_target_pairs={{0,15},{1,12},{2,13},{3,14},{4,11},{5,8},{6,9},{7,10},{8,7},{9,4},... | collective-permute-start | bytes 1572872 | tf_op jit(solution)/shard_map/ppermute | solution.py:322
  547.5 90.0 %collective-permute-start.52 = (bf16[2,32,16,256]{3,2,1,0:T(8,128)(2,1)}, bf16[2,32,16,256]{3,2,1,0:T(8,128)(2,1)S(1)}, u32[]{:S(2)}, u32[]{:S(2)}) collective-permute-start(bf16[2,32,16,256]{3,2,1,0:T(8,128)(2,1)} %get-tuple-element.72), channel_id=1, source_target_pairs={{0,8},{1,9},{2,10},{3,11},{4,0},{5,1},{6,2},{7,3},{8,12},{9,13},{1... | collective-permute-start | bytes 1572872 | tf_op jit(solution)/shard_map/ppermute | solution.py:322
  561.8 76.3 %collective-permute-start.53 = (bf16[2,32,16,256]{3,2,1,0:T(8,128)(2,1)}, bf16[2,32,16,256]{3,2,1,0:T(8,128)(2,1)S(1)}, u32[]{:S(2)}, u32[]{:S(2)}) collective-permute-start(bf16[2,32,16,256]{3,2,1,0:T(8,128)(2,1)} %get-tuple-element.73), channel_id=1, source_target_pairs={{0,9},{1,10},{2,11},{3,8},{4,1},{5,2},{6,3},{7,0},{8,13},{9,14},{1... | collective-permute-start | bytes 1572872 | tf_op jit(solution)/shard_map/ppermute | solution.py:322
  563.0 77.6 %collective-permute-start.54 = (bf16[2,32,16,256]{3,2,1,0:T(8,128)(2,1)}, bf16[2,32,16,256]{3,2,1,0:T(8,128)(2,1)S(1)}, u32[]{:S(2)}, u32[]{:S(2)}) collective-permute-start(bf16[2,32,16,256]{3,2,1,0:T(8,128)(2,1)} %get-tuple-element.74), channel_id=1, source_target_pairs={{0,10},{1,11},{2,8},{3,9},{4,2},{5,3},{6,0},{7,1},{8,14},{9,15},{1... | collective-permute-start | bytes 1572872 | tf_op jit(solution)/shard_map/ppermute | solution.py:322
  641.1 72.8 %collective-permute-start.25 = (bf16[2,32,16,256]{3,2,1,0:T(8,128)(2,1)}, bf16[2,32,16,256]{3,2,1,0:T(8,128)(2,1)S(1)}, u32[]{:S(2)}, u32[]{:S(2)}) collective-permute-start(bf16[2,32,16,256]{3,2,1,0:T(8,128)(2,1)} %get-tuple-element.58), channel_id=1, source_target_pairs={{0,11},{1,8},{2,9},{3,10},{4,3},{5,0},{6,1},{7,2},{8,15},{9,12},{1... | collective-permute-start | bytes 1572872 | tf_op jit(solution)/shard_map/ppermute | solution.py:322
  650.7 63.2 %collective-permute-start.26 = (bf16[2,32,16,256]{3,2,1,0:T(8,128)(2,1)}, bf16[2,32,16,256]{3,2,1,0:T(8,128)(2,1)S(1)}, u32[]{:S(2)}, u32[]{:S(2)}) collective-permute-start(bf16[2,32,16,256]{3,2,1,0:T(8,128)(2,1)} %get-tuple-element.59), channel_id=1, source_target_pairs={{0,4},{1,5},{2,6},{3,7},{4,12},{5,13},{6,14},{7,15},{8,0},{9,1},{1... | collective-permute-start | bytes 1572872 | tf_op jit(solution)/shard_map/ppermute | solution.py:322
  (103 other events, 5795.2 us)

commit v2 on v0

--- a/solution.py
+++ b/solution.py
@@ -13,6 +13,8 @@
 
 ROWS = 8
 STEP_ROWS = 2
+SUM_ROWS = 8
+LAST_ROWS = 8
 
 
 def complex_mix(input_real, input_imag, weight_real, weight_imag, pattern):
@@ -101,7 +103,7 @@
     return [moved[move] + turned[turn] for move, turn in rounds]
 
 
-def front_kernel(group, *refs):
+def front_kernel(group, splits, *refs):
     pieces, (w1, w2, close), outs = refs[:group], refs[group : group + 3], refs[group + 3 : -2]
     x, acc = refs[-2:]
     step = pl.program_id(0)
@@ -129,22 +131,25 @@
 
     @pl.when(row == ROWS - 1)
     def _():
+        first = 0
         for i, out in enumerate(outs):
+            count = splits[i % len(splits)]
             for h in range(acc.shape[0]):
                 c, lanes = divmod(h * 128, width)
                 out[c, :, :, lanes : lanes + 128] = (
-                    acc[h, i * local_a * ROWS : (i + 1) * local_a * ROWS, :]
-                    .reshape(local_a, ROWS, 128)
+                    acc[h, first * ROWS : (first + count) * ROWS, :]
+                    .reshape(count, ROWS, 128)
                     .astype(jnp.bfloat16)
                 )
-
-
-def front(pieces, w1, w2, close):
+            first += count
+
+
+def front(pieces, w1, w2, close, splits):
     group = len(pieces)
     _, chunk, local_a, width = pieces[0].shape
     total = group * local_a
     return pl.pallas_call(
-        functools.partial(front_kernel, group),
+        functools.partial(front_kernel, group, splits),
         grid=(chunk,),
         in_specs=[pl.BlockSpec((2, 1, local_a, width), lambda b: (0, b, 0, 0))] * group
         + [
@@ -152,9 +157,12 @@
             pl.BlockSpec(w2.shape, lambda b: (0, 0)),
             pl.BlockSpec(close.shape, lambda b: (0, 0, 0)),
         ],
-        out_specs=[pl.BlockSpec((2, local_a, ROWS, width), lambda b: (0, 0, b // ROWS, 0))]
+        out_specs=[
+            pl.BlockSpec((2, count, ROWS, width), lambda b: (0, 0, b // ROWS, 0))
+            for count in splits
+        ]
         * group,
-        out_shape=[jax.ShapeDtypeStruct((2, local_a, chunk, width), jnp.bfloat16)] * group,
+        out_shape=[pltpu.HBM((2, count, chunk, width), jnp.bfloat16) for count in splits] * group,
         scratch_shapes=[
             pltpu.VMEM((2 * total, width), jnp.bfloat16),
             pltpu.VMEM((2 * width // 128, total * ROWS, 128), jnp.float32),
@@ -173,10 +181,7 @@
     return jnp.dot(w3[...], x[...], preferred_element_type=jnp.float32)
 
 
-def partial_kernel(n, *refs):
-    pieces, w3, out, buffers, x, sems = refs[:n], refs[n], *refs[n + 1 :]
-    steps = out.shape[0] // STEP_ROWS
-
+def in_steps(pieces, buffers, sems, parts, steps, body):
     def copies(step, slot):
         rows = pl.ds(step * STEP_ROWS, STEP_ROWS)
         return [
@@ -186,69 +191,116 @@
 
     for copy in copies(0, 0):
         copy.start()
-
-    @pl.loop(0, steps)
-    def _(step):
+    for part in range(parts):
+
+        @pl.loop(0, steps)
+        def _(own):
+            step = part * steps + own
+            slot = lax.rem(step, 2)
+
+            @pl.when(step + 1 < parts * steps)
+            def _():
+                for copy in copies(step + 1, 1 - slot):
+                    copy.start()
+
+            for copy in copies(step, slot):
+                copy.wait()
+            body(part, own, step, [buffers.at[slot, i] for i in range(len(pieces))])
+
+
+def partial_kernel(n, *refs):
+    pieces, w3, outs, (buffers, x, sems) = refs[:n], refs[n], refs[n + 1 : -3], refs[-3:]
+
+    def body(part, own, step, held):
+        for t in range(STEP_ROWS):
+            outs[part][own * STEP_ROWS + t] = mix_rows(held, w3, x.at[t], t)
+
+    in_steps(pieces, buffers, sems, len(outs), outs[0].shape[0] // STEP_ROWS, body)
+
+
+def last_kernel(n, n_bases, start, *refs):
+    pieces, w3, bases = refs[:n], refs[n], refs[n + 1 : n + 1 + n_bases]
+    out, buffers, x, held_out, sems, out_sems = refs[-6:]
+    part_steps = bases[0].shape[0] // STEP_ROWS
+    steps = part_steps * n_bases
+
+    def copy_out(step, slot):
+        rows = pl.ds(start + step * STEP_ROWS, STEP_ROWS)
+        return pltpu.make_async_copy(held_out.at[slot], out.at[rows], out_sems.at[slot])
+
+    def body(part, own, step, held):
         slot = lax.rem(step, 2)
 
-        @pl.when(step + 1 < steps)
+        @pl.when(step >= 2)
         def _():
-            for copy in copies(step + 1, 1 - slot):
-                copy.start()
-
-        for copy in copies(step, slot):
-            copy.wait()
-        held = [buffers.at[slot, i] for i in range(n)]
+            copy_out(step - 2, slot).wait()
+
         for t in range(STEP_ROWS):
-            out[step * STEP_ROWS + t] = mix_rows(held, w3, x.at[t], t)
+            y = bases[part][own * STEP_ROWS + t] + mix_rows(held, w3, x.at[t], t)
+            split = y.shape[1] // 128
+            for h in range(split):
+                lines = pl.ds(h, y.shape[0], stride=split)
+                held_out[slot, t, lines, :] = y[:, h * 128 : (h + 1) * 128]
+        copy_out(step, slot).start()
+
+    in_steps(pieces, buffers, sems, n_bases, part_steps, body)
+    for step in range(max(steps - 2, 0), steps):
+        copy_out(step, step % 2).wait()
+
+
+def in_hbm(pieces):
+    return [pltpu.with_memory_space_constraint(piece, pltpu.HBM) for piece in pieces]
+
+
+def scratch_of(pieces):
+    n, (_, _, chunk, width) = len(pieces), pieces[0].shape
+    return [
+        pltpu.VMEM((2, n, 2, STEP_ROWS, chunk, width), jnp.bfloat16),
+        pltpu.VMEM((STEP_ROWS, 2 * n * chunk, width), jnp.bfloat16),
+    ]
 
 
 def partial_b(pieces, w3):
-    _, local_a, chunk, width = pieces[0].shape
-    n = len(pieces)
+    _, local_a, _, width = pieces[0].shape
+    n, count = len(pieces), local_a // SUM_ROWS
+    vmem = pl.BlockSpec(memory_space=pltpu.VMEM)
     return pl.pallas_call(
         functools.partial(partial_kernel, n),
-        in_specs=[pl.BlockSpec(memory_space=pl.ANY)] * n
-        + [pl.BlockSpec(memory_space=pltpu.VMEM)],
-        out_specs=pl.BlockSpec(memory_space=pltpu.VMEM),
-        out_shape=jax.ShapeDtypeStruct((local_a, w3.shape[0], width), jnp.float32),
-        scratch_shapes=[
-            pltpu.VMEM((2, n, 2, STEP_ROWS, chunk, width), jnp.bfloat16),
-            pltpu.VMEM((STEP_ROWS, 2 * n * chunk, width), jnp.bfloat16),
+        in_specs=[pl.BlockSpec(memory_space=pl.ANY)] * n + [vmem],
+        out_specs=[vmem] * count,
+        out_shape=[pltpu.VMEM((SUM_ROWS, w3.shape[0], width), jnp.float32)] * count,
+        scratch_shapes=scratch_of(pieces) + [pltpu.SemaphoreType.DMA((2, n))],
+        compiler_params=pltpu.CompilerParams(vmem_limit_bytes=12 << 20),
+        name="partial",
+    )(*in_hbm(pieces), w3)
+
+
+def last_b(pieces, w3, bases, out, start, rows):
+    width = pieces[0].shape[3]
+    n, lines = len(pieces), w3.shape[0] * (width // 128)
+    vmem = pl.BlockSpec(memory_space=pltpu.VMEM)
+    any_space = pl.BlockSpec(memory_space=pl.ANY)
+    given = [] if out is None else [out]
+    return pl.pallas_call(
+        functools.partial(last_kernel, n, len(bases), start),
+        in_specs=[any_space] * n + [vmem] * (1 + len(bases)) + [any_space] * len(given),
+        out_specs=any_space,
+        out_shape=jax.ShapeDtypeStruct((rows, lines, 128), jnp.float32),
+        input_output_aliases={n + 1 + len(bases): 0} if given else {},
+        scratch_shapes=scratch_of(pieces)
+        + [
+            pltpu.VMEM((2, STEP_ROWS, lines, 128), jnp.float32),
             pltpu.SemaphoreType.DMA((2, n)),
+            pltpu.SemaphoreType.DMA((2,)),
         ],
         compiler_params=pltpu.CompilerParams(vmem_limit_bytes=12 << 20),
-        name="partial",
-    )(*pieces, w3)
-
-
-def last_kernel(n, *refs):
-    pieces, w3, base, out, x = refs[:n], *refs[n:]
-    for t in range(out.shape[0]):
-        y = base[t] + mix_rows(pieces, w3, x.at[t], t)
-        split = y.shape[1] // 128
-        for h in range(split):
-            out[t, pl.ds(h, y.shape[0], stride=split), :] = y[:, h * 128 : (h + 1) * 128]
-
-
-def last_b(pieces, w3, base):
-    _, local_a, chunk, width = pieces[0].shape
-    n = len(pieces)
-    lines = w3.shape[0] * (width // 128)
-    return pl.pallas_call(
-        functools.partial(last_kernel, n),
-        grid=(local_a // STEP_ROWS,),
-        in_specs=[pl.BlockSpec((2, STEP_ROWS, chunk, width), lambda a: (0, a, 0, 0))] * n
-        + [
-            pl.BlockSpec(w3.shape, lambda a: (0, 0)),
-            pl.BlockSpec((STEP_ROWS,) + base.shape[1:], lambda a: (a, 0, 0)),
-        ],
-        out_specs=pl.BlockSpec((STEP_ROWS, lines, 128), lambda a: (a, 0, 0)),
-        out_shape=jax.ShapeDtypeStruct((local_a, lines, 128), jnp.float32),
-        scratch_shapes=[pltpu.VMEM((STEP_ROWS, 2 * n * chunk, width), jnp.bfloat16)],
-        compiler_params=pltpu.CompilerParams(vmem_limit_bytes=20 << 20),
         name="last",
-    )(*pieces, w3, base)
+    )(
+        *in_hbm(pieces),
+        w3,
+        *[pltpu.with_memory_space_constraint(base, pltpu.VMEM) for base in bases],
+        *given,
+    )
 
 
 def on_device(stem_tensor, branch_one, branch_two, mode_order, branch_three, closing):
@@ -262,6 +314,8 @@
     if (
         local_b % (B_CHUNKS * 2 * ROWS)
         or local_a % ROWS
+        or local_a % SUM_ROWS
+        or local_a <= LAST_ROWS
         or width % 128
         or stem_tensor.shape[3] != 1
     ):
@@ -330,12 +384,19 @@
     w1, w2, w3 = lax.optimization_barrier((w1, w2, w3))
 
     returned = []
+    parts = (local_a - LAST_ROWS, LAST_ROWS)
     for j in range(B_CHUNKS):
-        pieces = front(arrived[j], w1, w2, close[:, :, j * chunk : (j + 1) * chunk])
-        returned.append([send(piece, k) for k, piece in enumerate(pieces)])
-
-    base = partial_b(returned[0], w3[0])
-    out = last_b(returned[1], w3[1], base)
+        splits = parts if j else (local_a,)
+        pieces = front(arrived[j], w1, w2, close[:, :, j * chunk : (j + 1) * chunk], splits)
+        for i in range(len(splits)):
+            returned.append([send(piece, k) for k, piece in enumerate(pieces[i :: len(splits)])])
+
+    sums = partial_b(returned[0], w3[0])
+    out, start = None, 0
+    for i, count in enumerate(parts):
+        own = sums[start // SUM_ROWS : (start + count) // SUM_ROWS]
+        out = last_b(returned[1 + i], w3[1], own, out, start, local_a)
+        start += count
     return out.reshape(local_a, size_b, 2, 1, width)
 
 

time: 778 us -> 777 us (level)
  starting transfers between devices: 354 us -> 397 us
  waiting for transfers between devices: 157 us -> 131 us
  Pallas kernels: 112 us -> 99.8 us
  local copies, waits for them, and re-layouts: 142 us -> 134 us
    ppermute x60 -> x75, starting transfers between devices: 354 us -> 397 us  [send(): return lax.ppermute(block, 'inter', pairs[k])]
    ppermute x60 -> x75, waiting for transfers between devices: 157 us -> 131 us  [send(): return lax.ppermute(block, 'inter', pairs[k])]
    pallas_call x3 -> x4, Pallas kernels: 94.8 us -> 85.1 us  [the longest x2 62.9 us: front(): pl.pallas_call(functools.partial(front_kernel, group, splits), grid=(chun...]
    unnamed x104 -> x208, local copies, waits for them, and re-layouts: 15.6 us -> 7.07 us
  transfers between devices with their start and end apart: 60 -> 75, of which waited for: 18 -> 13; matrix products, arithmetic and copies ran while one was open for 17% -> 17% of each run, Pallas kernels for 10% -> 12%
where the time goes in v2:
time: 777 us; the launch traced here: 771 us
  starting transfers between devices  397 us (51%)
  local copies, waits for them, and re-layouts  134 us (17%)
  waiting for transfers between devices  131 us (17%)
  Pallas kernels  99.8 us (13%)
  other arithmetic  7.87 us (1%)
    ppermute x75, starting transfers between devices, send(): return lax.ppermute(block, 'inter', pairs[k])  397 us
    ppermute x75, waiting for transfers between devices, send(): return lax.ppermute(block, 'inter', pairs[k])  131 us
    pallas_call x2, Pallas kernels, front(): pl.pallas_call(functools.partial(front_kernel, group, splits), grid=(chun...  62.9 us
    dynamic_slice x34, local copies, waits for them, and re-layouts, on_device(): lax.dynamic_slice(stem, (zero, zero, target[k] * jnp.uint32(local_b) + jn...  51.2 us
    gather x4, local copies, waits for them, and re-layouts, on_device(): one = one[:, where_from][:, :, :, where_to].reshape(2, size_a, size_a)  23 us
    pallas_call x2, Pallas kernels, last_b(): pl.pallas_call(functools.partial(last_kernel, n, len(bases), start), in_s...  22.1 us
    scatter x1, local copies, waits for them, and re-layouts, on_device(): permuted = jnp.zeros_like(branch_two).at[:, mode_order, :].set(branch_two)  18.2 us
  transfers between devices with their start and end apart: 75, of which 13 were waited for; matrix products, arithmetic and copies ran while one was open for 17% of the time, Pallas kernels for 12%

profile of v2, /device:TPU:1, one launch (start us, length us, event | category | flops | bytes accessed | tf_op | source)
XLA Modules:
  0.0 771.4 jit_solution(8206430540378559499)
XLA Ops:
  31.0 7.5 constant_dynamic-slice_fusion
  43.1 29.7 %collective-permute-start.7 = (bf16[2,16,32,256]{3,2,1,0:T(8,128)(2,1)}, bf16[2,16,32,256]{3,2,1,0:T(8,128)(2,1)}, u32[]{:S(2)}, u32[]{:S(2)}) collective-permute-start(bf16[2,16,32,256]{3,2,1,0:T(8,128)(2,1)} %bitcast.211), channel_id=1, source_target_pairs={{0,8},{1,9},{2,10},{3,11},{4,0},{5,1},{6,2},{7,3},{8,12},{9,13},{1... | collective-permute-start | bytes 1572872 | tf_op jit(solution)/shard_map/ppermute | solution.py:334
  72.9 31.6 %collective-permute-start.9 = (bf16[2,16,32,256]{3,2,1,0:T(8,128)(2,1)}, bf16[2,16,32,256]{3,2,1,0:T(8,128)(2,1)}, u32[]{:S(2)}, u32[]{:S(2)}) collective-permute-start(bf16[2,16,32,256]{3,2,1,0:T(8,128)(2,1)} %bitcast.209), channel_id=1, source_target_pairs={{0,10},{1,11},{2,8},{3,9},{4,2},{5,3},{6,0},{7,1},{8,14},{9,15},{1... | collective-permute-start | bytes 1572872 | tf_op jit(solution)/shard_map/ppermute | solution.py:334
  128.1 18.9 %collective-permute-start.11 = (bf16[2,16,32,256]{3,2,1,0:T(8,128)(2,1)}, bf16[2,16,32,256]{3,2,1,0:T(8,128)(2,1)S(1)}, u32[]{:S(2)}, u32[]{:S(2)}) collective-permute-start(bf16[2,16,32,256]{3,2,1,0:T(8,128)(2,1)} %bitcast.207), channel_id=1, source_target_pairs={{0,4},{1,5},{2,6},{3,7},{4,12},{5,13},{6,14},{7,15},{8,0},{9,1},{1... | collective-permute-start | bytes 1572872 | tf_op jit(solution)/shard_map/ppermute | solution.py:334
  154.2 6.5 collective-permute-done.11.refs_12_
  162.3 9.3 %collective-permute-done.43.refs_14_ = bf16[2,16,32,256]{3,2,1,0:T(8,128)(2,1)S(1)} collective-permute-done((bf16[2,16,32,256]{3,2,1,0:T(8,128)(2,1)S(1)}, bf16[2,16,32,256]{3,2,1,0:T(8,128)(2,1)S(1)}, u32[]{:S(2)}, u32[]{:S(2)}) %collective-permute-start.43) | collective-permute-done | bytes 524320 | tf_op jit(solution)/shard_map/ppermute | solution.py:334
  171.6 9.9 %collective-permute-done.12.refs_13_ = bf16[2,16,32,256]{3,2,1,0:T(8,128)(2,1)S(1)} collective-permute-done((bf16[2,16,32,256]{3,2,1,0:T(8,128)(2,1)S(1)}, bf16[2,16,32,256]{3,2,1,0:T(8,128)(2,1)S(1)}, u32[]{:S(2)}, u32[]{:S(2)}) %collective-permute-start.12) | collective-permute-done | bytes 524320 | tf_op jit(solution)/shard_map/ppermute | solution.py:334
  183.8 10.4 %collective-permute-done.13.refs_14_ = bf16[2,16,32,256]{3,2,1,0:T(8,128)(2,1)S(1)} collective-permute-done((bf16[2,16,32,256]{3,2,1,0:T(8,128)(2,1)S(1)}, bf16[2,16,32,256]{3,2,1,0:T(8,128)(2,1)S(1)}, u32[]{:S(2)}, u32[]{:S(2)}) %collective-permute-start.13) | collective-permute-done | bytes 524320 | tf_op jit(solution)/shard_map/ppermute | solution.py:334
  203.0 18.2 %scatter_fusion = bf16[2,256,256]{2,0,1:T(2,128)(2,1)S(1)} fusion(bf16[2,256,256]{2,0,1:T(2,128)(2,1)S(1)} %broadcast_in_dim.4, s32[256]{0:T(256)S(1)} %compare_select_fusion, bf16[256,2,256]{2,1,0:T(2,128)(2,1)} %copy.112), kind=kCustom, calls=%fused_computation.4 | custom fusion | bytes 787456 | tf_op jit(solution)/shard_map/scatter | solution.py:362
  272.2 7.1 copy.111
  279.2 6.8 reshape.545
  295.4 22.7 %collective-permute-start.40 = (bf16[2,16,32,256]{3,2,1,0:T(8,128)(2,1)S(1)}, bf16[2,16,32,256]{3,2,1,0:T(8,128)(2,1)S(1)}, u32[]{:S(2)}, u32[]{:S(2)}) collective-permute-start(bf16[2,16,32,256]{3,2,1,0:T(8,128)(2,1)S(1)} %bitcast.243), channel_id=1, source_target_pairs={{0,11},{1,8},{2,9},{3,10},{4,3},{5,0},{6,1},{7,2},{8,15},{9,12},{1... | collective-permute-start | bytes 1572872 | tf_op jit(solution)/shard_map/ppermute | solution.py:334
  318.1 22.0 %collective-permute-start.41 = (bf16[2,16,32,256]{3,2,1,0:T(8,128)(2,1)S(1)}, bf16[2,16,32,256]{3,2,1,0:T(8,128)(2,1)S(1)}, u32[]{:S(2)}, u32[]{:S(2)}) collective-permute-start(bf16[2,16,32,256]{3,2,1,0:T(8,128)(2,1)S(1)} %bitcast.241), channel_id=1, source_target_pairs={{0,4},{1,5},{2,6},{3,7},{4,12},{5,13},{6,14},{7,15},{8,0},{9,1},{1... | collective-permute-start | bytes 1572872 | tf_op jit(solution)/shard_map/ppermute | solution.py:334
  342.6 31.8 %front.2 = (bf16[2,24,16,256]{3,2,1,0:T(8,128)(2,1)}, bf16[2,8,16,256]{3,2,1,0:T(8,128)(2,1)}, bf16[2,24,16,256]{3,2,1,0:T(8,128)(2,1)}, bf16[2,8,16,256]{3,2,1,...) custom-call(bf16[2,16,32,256]{3,2,1,0:T(8,128)(2,1)S(1)} %bitcast.22, ...), custom_call_target="tpu_custom_call" | custom-call | tf_op jit(solution)/shard_map/front/pallas_call | solution.py:151
  390.2 11.9 %collective-permute-start.24 = (bf16[2,8,16,256]{3,2,1,0:T(8,128)(2,1)}, bf16[2,8,16,256]{3,2,1,0:T(8,128)(2,1)S(1)}, u32[]{:S(2)}, u32[]{:S(2)}) collective-permute-start(bf16[2,8,16,256]{3,2,1,0:T(8,128)(2,1)} %get-tuple-element.73), channel_id=1, source_target_pairs={{0,10},{1,11},{2,8},{3,9},{4,2},{5,3},{6,0},{7,1},{8,14},{9,15},{1... | collective-permute-start | bytes 393224 | tf_op jit(solution)/shard_map/ppermute | solution.py:334
  409.1 7.5 collective-permute-done.60.refs_1_
  421.1 15.9 %collective-permute-done.62.refs_3_ = bf16[2,24,16,256]{3,2,1,0:T(8,128)(2,1)S(1)} collective-permute-done((bf16[2,24,16,256]{3,2,1,0:T(8,128)(2,1)}, bf16[2,24,16,256]{3,2,1,0:T(8,128)(2,1)S(1)}, u32[]{:S(2)}, u32[]{:S(2)}) %collective-permute-start.62) | collective-permute-done | bytes 393248 | tf_op jit(solution)/shard_map/ppermute | solution.py:334
  436.9 39.5 %collective-permute-start.67 = (bf16[2,24,16,256]{3,2,1,0:T(8,128)(2,1)}, bf16[2,24,16,256]{3,2,1,0:T(8,128)(2,1)S(1)}, u32[]{:S(2)}, u32[]{:S(2)}) collective-permute-start(bf16[2,24,16,256]{3,2,1,0:T(8,128)(2,1)} %get-tuple-element.106), channel_id=1, source_target_pairs={{0,8},{1,9},{2,10},{3,11},{4,0},{5,1},{6,2},{7,3},{8,12},{9,13},{1... | collective-permute-start | bytes 1179656 | tf_op jit(solution)/shard_map/ppermute | solution.py:334
  481.0 29.7 %collective-permute-start.71 = (bf16[2,24,16,256]{3,2,1,0:T(8,128)(2,1)}, bf16[2,24,16,256]{3,2,1,0:T(8,128)(2,1)S(1)}, u32[]{:S(2)}, u32[]{:S(2)}) collective-permute-start(bf16[2,24,16,256]{3,2,1,0:T(8,128)(2,1)} %get-tuple-element.110), channel_id=1, source_target_pairs={{0,4},{1,5},{2,6},{3,7},{4,12},{5,13},{6,14},{7,15},{8,0},{9,1},{1... | collective-permute-start | bytes 1179656 | tf_op jit(solution)/shard_map/ppermute | solution.py:334
  514.3 31.2 %front.3 = (bf16[2,32,16,256]{3,2,1,0:T(8,128)(2,1)}, bf16[2,32,16,256]{3,2,1,0:T(8,128)(2,1)}, bf16[2,32,16,256]{3,2,1,0:T(8,128)(2,1)}, bf16[2,32,16,256]{3,2,...) custom-call(bf16[2,16,32,256]{3,2,1,0:T(8,128)(2,1)S(1)} %bitcast.22, ...), custom_call_target="tpu_custom_call" | custom-call | tf_op jit(solution)/shard_map/front/pallas_call | solution.py:151
  552.3 8.9 %collective-permute-done.45.refs_1_ = bf16[2,32,16,256]{3,2,1,0:T(8,128)(2,1)S(1)} collective-permute-done((bf16[2,32,16,256]{3,2,1,0:T(8,128)(2,1)}, bf16[2,32,16,256]{3,2,1,0:T(8,128)(2,1)S(1)}, u32[]{:S(2)}, u32[]{:S(2)}) %collective-permute-start.45) | collective-permute-done | bytes 524320 | tf_op jit(solution)/shard_map/ppermute | solution.py:334
  566.8 26.0 %collective-permute-done.47.refs_3_ = bf16[2,32,16,256]{3,2,1,0:T(8,128)(2,1)S(1)} collective-permute-done((bf16[2,32,16,256]{3,2,1,0:T(8,128)(2,1)}, bf16[2,32,16,256]{3,2,1,0:T(8,128)(2,1)S(1)}, u32[]{:S(2)}, u32[]{:S(2)}) %collective-permute-start.47) | collective-permute-done | bytes 524320 | tf_op jit(solution)/shard_map/ppermute | solution.py:334
  592.8 16.9 %collective-permute-start.52 = (bf16[2,32,16,256]{3,2,1,0:T(8,128)(2,1)}, bf16[2,32,16,256]{3,2,1,0:T(8,128)(2,1)S(1)}, u32[]{:S(2)}, u32[]{:S(2)}) collective-permute-start(bf16[2,32,16,256]{3,2,1,0:T(8,128)(2,1)} %get-tuple-element.88), channel_id=1, source_target_pairs={{0,8},{1,9},{2,10},{3,11},{4,0},{5,1},{6,2},{7,3},{8,12},{9,13},{1... | collective-permute-start | bytes 1572872 | tf_op jit(solution)/shard_map/ppermute | solution.py:334
  609.8 31.5 %collective-permute-start.54 = (bf16[2,32,16,256]{3,2,1,0:T(8,128)(2,1)}, bf16[2,32,16,256]{3,2,1,0:T(8,128)(2,1)S(1)}, u32[]{:S(2)}, u32[]{:S(2)}) collective-permute-start(bf16[2,32,16,256]{3,2,1,0:T(8,128)(2,1)} %get-tuple-element.90), channel_id=1, source_target_pairs={{0,10},{1,11},{2,8},{3,9},{4,2},{5,3},{6,0},{7,1},{8,14},{9,15},{1... | collective-permute-start | bytes 1572872 | tf_op jit(solution)/shard_map/ppermute | solution.py:334
  641.3 22.7 %collective-permute-start.55 = (bf16[2,32,16,256]{3,2,1,0:T(8,128)(2,1)}, bf16[2,32,16,256]{3,2,1,0:T(8,128)(2,1)S(1)}, u32[]{:S(2)}, u32[]{:S(2)}) collective-permute-start(bf16[2,32,16,256]{3,2,1,0:T(8,128)(2,1)} %get-tuple-element.91), channel_id=1, source_target_pairs={{0,11},{1,8},{2,9},{3,10},{4,3},{5,0},{6,1},{7,2},{8,15},{9,12},{1... | collective-permute-start | bytes 1572872 | tf_op jit(solution)/shard_map/ppermute | solution.py:334
  664.1 21.1 %collective-permute-start.56 = (bf16[2,32,16,256]{3,2,1,0:T(8,128)(2,1)}, bf16[2,32,16,256]{3,2,1,0:T(8,128)(2,1)S(1)}, u32[]{:S(2)}, u32[]{:S(2)}) collective-permute-start(bf16[2,32,16,256]{3,2,1,0:T(8,128)(2,1)} %get-tuple-element.92), channel_id=1, source_target_pairs={{0,4},{1,5},{2,6},{3,7},{4,12},{5,13},{6,14},{7,15},{8,0},{9,1},{1... | collective-permute-start | bytes 1572872 | tf_op jit(solution)/shard_map/ppermute | solution.py:334
  691.0 6.6 collective-permute-done.56.refs_12_
  699.3 10.8 %collective-permute-done.57.refs_13_ = bf16[2,32,16,256]{3,2,1,0:T(8,128)(2,1)S(1)} collective-permute-done((bf16[2,32,16,256]{3,2,1,0:T(8,128)(2,1)}, bf16[2,32,16,256]{3,2,1,0:T(8,128)(2,1)S(1)}, u32[]{:S(2)}, u32[]{:S(2)}) %collective-permute-start.57) | collective-permute-done | bytes 524320 | tf_op jit(solution)/shard_map/ppermute | solution.py:334
  711.8 9.5 %collective-permute-done.58.refs_14_ = bf16[2,32,16,256]{3,2,1,0:T(8,128)(2,1)S(1)} collective-permute-done((bf16[2,32,16,256]{3,2,1,0:T(8,128)(2,1)}, bf16[2,32,16,256]{3,2,1,0:T(8,128)(2,1)S(1)}, u32[]{:S(2)}, u32[]{:S(2)}) %collective-permute-start.58) | collective-permute-done | bytes 524320 | tf_op jit(solution)/shard_map/ppermute | solution.py:334
  722.6 9.3 %collective-permute-done.59.refs_15_ = bf16[2,32,16,256]{3,2,1,0:T(8,128)(2,1)S(1)} collective-permute-done((bf16[2,32,16,256]{3,2,1,0:T(8,128)(2,1)}, bf16[2,32,16,256]{3,2,1,0:T(8,128)(2,1)S(1)}, u32[]{:S(2)}, u32[]{:S(2)}) %collective-permute-start.59) | collective-permute-done | bytes 524320 | tf_op jit(solution)/shard_map/ppermute | solution.py:334
  733.5 14.7 %partial.1 = (f32[8,1024,256]{2,1,0:T(8,128)S(1)}, f32[8,1024,256]{2,1,0:T(8,128)S(1)}, f32[8,1024,256]{2,1,0:T(8,128)S(1)}, f32[8,1024,256]{2,1,0:T(8,128)S(1)}) custom-call(bf16[2,32,16,256]{3,2,1,0:T(8,128)(2,1)} %get-tuple-element.80.refs_0_, bf16[2,32,16,256]{3,2,1,0:T(8,128)(2,1)} %copy-done.48, bf16[2,32,16,256]{3,2,1,0:T(8,128)(2,1)} %copy-done.49, ...), custom_call_target="tpu_custom_call" | custom-call | tf_op jit(solution)/shard_map/partial/pallas_call | solution.py:267
  748.2 15.6 %last.2.refs_18_ = f32[32,2048,128]{2,1,0:T(8,128)} custom-call(bf16[2,24,16,256]{3,2,1,0:T(8,128)(2,1)} %get-tuple-element.98.refs_0_, bf16[2,24,16,256]{3,2,1,0:T(8,128)(2,1)} %copy-done.66, bf16[2,24,16,256]{3,2,1,0:T(8,128)(2,1)} %copy-done.67, bf16[2,24,16,256]{3,2,1,0:T(8,128)(2,1)} %copy-done.68, bf16[2,24,16,256]{3,2,1,0:T(8,128)(2,1)} %copy-done.69, ...), custom_call_target="tpu_custom_call" | custom-call | tf_op jit(solution)/shard_map/last/pallas_call | solution.py:284
  (402 shorter events, 208.2 us)
Async XLA Ops:
  16.0 56.9 %collective-permute-start.3 = (bf16[2,16,32,256]{3,2,1,0:T(8,128)(2,1)}, bf16[2,16,32,256]{3,2,1,0:T(8,128)(2,1)S(1)}, u32[]{:S(2)}, u32[]{:S(2)}) collective-permute-start(bf16[2,16,32,256]{3,2,1,0:T(8,128)(2,1)} %bitcast.215), channel_id=1, source_target_pairs={{0,3},{1,0},{2,1},{3,2},{4,7},{5,4},{6,5},{7,6},{8,11},{9,8},{10,9... | collective-permute-start | bytes 1572872 | tf_op jit(solution)/shard_map/ppermute | solution.py:334
  38.5 84.9 %collective-permute-start.5 = (bf16[2,16,32,256]{3,2,1,0:T(8,128)(2,1)}, bf16[2,16,32,256]{3,2,1,0:T(8,128)(2,1)S(1)}, u32[]{:S(2)}, u32[]{:S(2)}) collective-permute-start(bf16[2,16,32,256]{3,2,1,0:T(8,128)(2,1)} %bitcast.213), channel_id=1, source_target_pairs={{0,14},{1,15},{2,12},{3,13},{4,10},{5,11},{6,8},{7,9},{8,6},{9,7},... | collective-permute-start | bytes 1572872 | tf_op jit(solution)/shard_map/ppermute | solution.py:334
  43.1 85.0 %collective-permute-start.6 = (bf16[2,16,32,256]{3,2,1,0:T(8,128)(2,1)}, bf16[2,16,32,256]{3,2,1,0:T(8,128)(2,1)S(1)}, u32[]{:S(2)}, u32[]{:S(2)}) collective-permute-start(bf16[2,16,32,256]{3,2,1,0:T(8,128)(2,1)} %bitcast.212), channel_id=1, source_target_pairs={{0,15},{1,12},{2,13},{3,14},{4,11},{5,8},{6,9},{7,10},{8,7},{9,4},... | collective-permute-start | bytes 1572872 | tf_op jit(solution)/shard_map/ppermute | solution.py:334
  43.1 103.9 %collective-permute-start.7 = (bf16[2,16,32,256]{3,2,1,0:T(8,128)(2,1)}, bf16[2,16,32,256]{3,2,1,0:T(8,128)(2,1)}, u32[]{:S(2)}, u32[]{:S(2)}) collective-permute-start(bf16[2,16,32,256]{3,2,1,0:T(8,128)(2,1)} %bitcast.211), channel_id=1, source_target_pairs={{0,8},{1,9},{2,10},{3,11},{4,0},{5,1},{6,2},{7,3},{8,12},{9,13},{1... | collective-permute-start | bytes 1572872 | tf_op jit(solution)/shard_map/ppermute | solution.py:334
  72.8 74.2 %collective-permute-start.8 = (bf16[2,16,32,256]{3,2,1,0:T(8,128)(2,1)}, bf16[2,16,32,256]{3,2,1,0:T(8,128)(2,1)}, u32[]{:S(2)}, u32[]{:S(2)}) collective-permute-start(bf16[2,16,32,256]{3,2,1,0:T(8,128)(2,1)} %bitcast.210), channel_id=1, source_target_pairs={{0,9},{1,10},{2,11},{3,8},{4,1},{5,2},{6,3},{7,0},{8,13},{9,14},{1... | collective-permute-start | bytes 1572872 | tf_op jit(solution)/shard_map/ppermute | solution.py:334
  72.9 76.6 %collective-permute-start.9 = (bf16[2,16,32,256]{3,2,1,0:T(8,128)(2,1)}, bf16[2,16,32,256]{3,2,1,0:T(8,128)(2,1)}, u32[]{:S(2)}, u32[]{:S(2)}) collective-permute-start(bf16[2,16,32,256]{3,2,1,0:T(8,128)(2,1)} %bitcast.209), channel_id=1, source_target_pairs={{0,10},{1,11},{2,8},{3,9},{4,2},{5,3},{6,0},{7,1},{8,14},{9,15},{1... | collective-permute-start | bytes 1572872 | tf_op jit(solution)/shard_map/ppermute | solution.py:334
  152.4 70.0 %collective-permute-start.14 = (bf16[2,16,32,256]{3,2,1,0:T(8,128)(2,1)}, bf16[2,16,32,256]{3,2,1,0:T(8,128)(2,1)S(1)}, u32[]{:S(2)}, u32[]{:S(2)}) collective-permute-start(bf16[2,16,32,256]{3,2,1,0:T(8,128)(2,1)} %bitcast.204), channel_id=1, source_target_pairs={{0,7},{1,4},{2,5},{3,6},{4,15},{5,12},{6,13},{7,14},{8,3},{9,0},{1... | collective-permute-start | bytes 1572872 | tf_op jit(solution)/shard_map/ppermute | solution.py:334
  161.5 63.4 %collective-permute-start.30 = (bf16[2,16,32,256]{3,2,1,0:T(8,128)(2,1)}, bf16[2,16,32,256]{3,2,1,0:T(8,128)(2,1)S(1)}, u32[]{:S(2)}, u32[]{:S(2)}) collective-permute-start(bf16[2,16,32,256]{3,2,1,0:T(8,128)(2,1)} %bitcast.202), channel_id=1, source_target_pairs={{0,12},{1,13},{2,14},{3,15},{4,8},{5,9},{6,10},{7,11},{8,4},{9,5},... | collective-permute-start | bytes 1572872 | tf_op jit(solution)/shard_map/ppermute | solution.py:334
  222.4 69.0 %collective-permute-start.34 = (bf16[2,16,32,256]{3,2,1,0:T(8,128)(2,1)}, bf16[2,16,32,256]{3,2,1,0:T(8,128)(2,1)}, u32[]{:S(2)}, u32[]{:S(2)}) collective-permute-start(bf16[2,16,32,256]{3,2,1,0:T(8,128)(2,1)} %bitcast.249), channel_id=1, source_target_pairs={{0,13},{1,14},{2,15},{3,12},{4,9},{5,10},{6,11},{7,8},{8,5},{9,6},... | collective-permute-start | bytes 1572872 | tf_op jit(solution)/shard_map/ppermute | solution.py:334
  224.9 70.5 %collective-permute-start.35 = (bf16[2,16,32,256]{3,2,1,0:T(8,128)(2,1)}, bf16[2,16,32,256]{3,2,1,0:T(8,128)(2,1)}, u32[]{:S(2)}, u32[]{:S(2)}) collective-permute-start(bf16[2,16,32,256]{3,2,1,0:T(8,128)(2,1)} %bitcast.246), channel_id=1, source_target_pairs={{0,14},{1,15},{2,12},{3,13},{4,10},{5,11},{6,8},{7,9},{8,6},{9,7},... | collective-permute-start | bytes 1572872 | tf_op jit(solution)/shard_map/ppermute | solution.py:334
  227.9 90.2 %collective-permute-start.36 = (bf16[2,16,32,256]{3,2,1,0:T(8,128)(2,1)}, bf16[2,16,32,256]{3,2,1,0:T(8,128)(2,1)}, u32[]{:S(2)}, u32[]{:S(2)}) collective-permute-start(bf16[2,16,32,256]{3,2,1,0:T(8,128)(2,1)} %bitcast.244), channel_id=1, source_target_pairs={{0,15},{1,12},{2,13},{3,14},{4,11},{5,8},{6,9},{7,10},{8,7},{9,4},... | collective-permute-start | bytes 1572872 | tf_op jit(solution)/shard_map/ppermute | solution.py:334
  228.1 112.0 %collective-permute-start.37 = (bf16[2,16,32,256]{3,2,1,0:T(8,128)(2,1)}, bf16[2,16,32,256]{3,2,1,0:T(8,128)(2,1)}, u32[]{:S(2)}, u32[]{:S(2)}) collective-permute-start(bf16[2,16,32,256]{3,2,1,0:T(8,128)(2,1)} %bitcast.242), channel_id=1, source_target_pairs={{0,8},{1,9},{2,10},{3,11},{4,0},{5,1},{6,2},{7,3},{8,12},{9,13},{1... | collective-permute-start | bytes 1572872 | tf_op jit(solution)/shard_map/ppermute | solution.py:334
  230.3 110.6 %collective-permute-start.38 = (bf16[2,16,32,256]{3,2,1,0:T(8,128)(2,1)}, bf16[2,16,32,256]{3,2,1,0:T(8,128)(2,1)}, u32[]{:S(2)}, u32[]{:S(2)}) collective-permute-start(bf16[2,16,32,256]{3,2,1,0:T(8,128)(2,1)} %bitcast.240), channel_id=1, source_target_pairs={{0,9},{1,10},{2,11},{3,8},{4,1},{5,2},{6,3},{7,0},{8,13},{9,14},{1... | collective-permute-start | bytes 1572872 | tf_op jit(solution)/shard_map/ppermute | solution.py:334
  291.4 83.0 %collective-permute-start.39 = (bf16[2,16,32,256]{3,2,1,0:T(8,128)(2,1)S(1)}, bf16[2,16,32,256]{3,2,1,0:T(8,128)(2,1)S(1)}, u32[]{:S(2)}, u32[]{:S(2)}) collective-permute-start(bf16[2,16,32,256]{3,2,1,0:T(8,128)(2,1)S(1)} %bitcast.245), channel_id=1, source_target_pairs={{0,10},{1,11},{2,8},{3,9},{4,2},{5,3},{6,0},{7,1},{8,14},{9,15},{1... | collective-permute-start | bytes 1572872 | tf_op jit(solution)/shard_map/ppermute | solution.py:334
  295.4 81.3 %collective-permute-start.40 = (bf16[2,16,32,256]{3,2,1,0:T(8,128)(2,1)S(1)}, bf16[2,16,32,256]{3,2,1,0:T(8,128)(2,1)S(1)}, u32[]{:S(2)}, u32[]{:S(2)}) collective-permute-start(bf16[2,16,32,256]{3,2,1,0:T(8,128)(2,1)S(1)} %bitcast.243), channel_id=1, source_target_pairs={{0,11},{1,8},{2,9},{3,10},{4,3},{5,0},{6,1},{7,2},{8,15},{9,12},{1... | collective-permute-start | bytes 1572872 | tf_op jit(solution)/shard_map/ppermute | solution.py:334
  318.1 61.1 %collective-permute-start.41 = (bf16[2,16,32,256]{3,2,1,0:T(8,128)(2,1)S(1)}, bf16[2,16,32,256]{3,2,1,0:T(8,128)(2,1)S(1)}, u32[]{:S(2)}, u32[]{:S(2)}) collective-permute-start(bf16[2,16,32,256]{3,2,1,0:T(8,128)(2,1)S(1)} %bitcast.241), channel_id=1, source_target_pairs={{0,4},{1,5},{2,6},{3,7},{4,12},{5,13},{6,14},{7,15},{8,0},{9,1},{1... | collective-permute-start | bytes 1572872 | tf_op jit(solution)/shard_map/ppermute | solution.py:334
  405.5 70.9 %collective-permute-start.63 = (bf16[2,24,16,256]{3,2,1,0:T(8,128)(2,1)}, bf16[2,24,16,256]{3,2,1,0:T(8,128)(2,1)S(1)}, u32[]{:S(2)}, u32[]{:S(2)}) collective-permute-start(bf16[2,24,16,256]{3,2,1,0:T(8,128)(2,1)} %get-tuple-element.102), channel_id=1, source_target_pairs={{0,3},{1,0},{2,1},{3,2},{4,7},{5,4},{6,5},{7,6},{8,11},{9,8},{10,9... | collective-permute-start | bytes 1179656 | tf_op jit(solution)/shard_map/ppermute | solution.py:334
  405.7 72.1 %collective-permute-start.64 = (bf16[2,24,16,256]{3,2,1,0:T(8,128)(2,1)}, bf16[2,24,16,256]{3,2,1,0:T(8,128)(2,1)S(1)}, u32[]{:S(2)}, u32[]{:S(2)}) collective-permute-start(bf16[2,24,16,256]{3,2,1,0:T(8,128)(2,1)} %get-tuple-element.103), channel_id=1, source_target_pairs={{0,13},{1,14},{2,15},{3,12},{4,9},{5,10},{6,11},{7,8},{8,5},{9,6},... | collective-permute-start | bytes 1179656 | tf_op jit(solution)/shard_map/ppermute | solution.py:334
  416.6 61.3 %collective-permute-start.65 = (bf16[2,24,16,256]{3,2,1,0:T(8,128)(2,1)}, bf16[2,24,16,256]{3,2,1,0:T(8,128)(2,1)S(1)}, u32[]{:S(2)}, u32[]{:S(2)}) collective-permute-start(bf16[2,24,16,256]{3,2,1,0:T(8,128)(2,1)} %get-tuple-element.104), channel_id=1, source_target_pairs={{0,14},{1,15},{2,12},{3,13},{4,10},{5,11},{6,8},{7,9},{8,6},{9,7},... | collective-permute-start | bytes 1179656 | tf_op jit(solution)/shard_map/ppermute | solution.py:334
  419.1 61.9 %collective-permute-start.66 = (bf16[2,24,16,256]{3,2,1,0:T(8,128)(2,1)}, bf16[2,24,16,256]{3,2,1,0:T(8,128)(2,1)S(1)}, u32[]{:S(2)}, u32[]{:S(2)}) collective-permute-start(bf16[2,24,16,256]{3,2,1,0:T(8,128)(2,1)} %get-tuple-element.105), channel_id=1, source_target_pairs={{0,15},{1,12},{2,13},{3,14},{4,11},{5,8},{6,9},{7,10},{8,7},{9,4},... | collective-permute-start | bytes 1179656 | tf_op jit(solution)/shard_map/ppermute | solution.py:334
  436.9 73.8 %collective-permute-start.67 = (bf16[2,24,16,256]{3,2,1,0:T(8,128)(2,1)}, bf16[2,24,16,256]{3,2,1,0:T(8,128)(2,1)S(1)}, u32[]{:S(2)}, u32[]{:S(2)}) collective-permute-start(bf16[2,24,16,256]{3,2,1,0:T(8,128)(2,1)} %get-tuple-element.106), channel_id=1, source_target_pairs={{0,8},{1,9},{2,10},{3,11},{4,0},{5,1},{6,2},{7,3},{8,12},{9,13},{1... | collective-permute-start | bytes 1179656 | tf_op jit(solution)/shard_map/ppermute | solution.py:334
  477.9 67.8 %collective-permute-start.70 = (bf16[2,24,16,256]{3,2,1,0:T(8,128)(2,1)}, bf16[2,24,16,256]{3,2,1,0:T(8,128)(2,1)S(1)}, u32[]{:S(2)}, u32[]{:S(2)}) collective-permute-start(bf16[2,24,16,256]{3,2,1,0:T(8,128)(2,1)} %get-tuple-element.109), channel_id=1, source_target_pairs={{0,11},{1,8},{2,9},{3,10},{4,3},{5,0},{6,1},{7,2},{8,15},{9,12},{1... | collective-permute-start | bytes 1179656 | tf_op jit(solution)/shard_map/ppermute | solution.py:334
  481.0 66.0 %collective-permute-start.71 = (bf16[2,24,16,256]{3,2,1,0:T(8,128)(2,1)}, bf16[2,24,16,256]{3,2,1,0:T(8,128)(2,1)S(1)}, u32[]{:S(2)}, u32[]{:S(2)}) collective-permute-start(bf16[2,24,16,256]{3,2,1,0:T(8,128)(2,1)} %get-tuple-element.110), channel_id=1, source_target_pairs={{0,4},{1,5},{2,6},{3,7},{4,12},{5,13},{6,14},{7,15},{8,0},{9,1},{1... | collective-permute-start | bytes 1179656 | tf_op jit(solution)/shard_map/ppermute | solution.py:334
  549.0 60.6 %collective-permute-start.48 = (bf16[2,32,16,256]{3,2,1,0:T(8,128)(2,1)}, bf16[2,32,16,256]{3,2,1,0:T(8,128)(2,1)S(1)}, u32[]{:S(2)}, u32[]{:S(2)}) collective-permute-start(bf16[2,32,16,256]{3,2,1,0:T(8,128)(2,1)} %get-tuple-element.84), channel_id=1, source_target_pairs={{0,3},{1,0},{2,1},{3,2},{4,7},{5,4},{6,5},{7,6},{8,11},{9,8},{10,9... | collective-permute-start | bytes 1572872 | tf_op jit(solution)/shard_map/ppermute | solution.py:334
  549.0 60.8 %collective-permute-start.49 = (bf16[2,32,16,256]{3,2,1,0:T(8,128)(2,1)}, bf16[2,32,16,256]{3,2,1,0:T(8,128)(2,1)S(1)}, u32[]{:S(2)}, u32[]{:S(2)}) collective-permute-start(bf16[2,32,16,256]{3,2,1,0:T(8,128)(2,1)} %get-tuple-element.85), channel_id=1, source_target_pairs={{0,13},{1,14},{2,15},{3,12},{4,9},{5,10},{6,11},{7,8},{8,5},{9,6},... | collective-permute-start | bytes 1572872 | tf_op jit(solution)/shard_map/ppermute | solution.py:334
  561.1 80.2 %collective-permute-start.50 = (bf16[2,32,16,256]{3,2,1,0:T(8,128)(2,1)}, bf16[2,32,16,256]{3,2,1,0:T(8,128)(2,1)S(1)}, u32[]{:S(2)}, u32[]{:S(2)}) collective-permute-start(bf16[2,32,16,256]{3,2,1,0:T(8,128)(2,1)} %get-tuple-element.86), channel_id=1, source_target_pairs={{0,14},{1,15},{2,12},{3,13},{4,10},{5,11},{6,8},{7,9},{8,6},{9,7},... | collective-permute-start | bytes 1572872 | tf_op jit(solution)/shard_map/ppermute | solution.py:334
  562.8 101.2 %collective-permute-start.51 = (bf16[2,32,16,256]{3,2,1,0:T(8,128)(2,1)}, bf16[2,32,16,256]{3,2,1,0:T(8,128)(2,1)S(1)}, u32[]{:S(2)}, u32[]{:S(2)}) collective-permute-start(bf16[2,32,16,256]{3,2,1,0:T(8,128)(2,1)} %get-tuple-element.87), channel_id=1, source_target_pairs={{0,15},{1,12},{2,13},{3,14},{4,11},{5,8},{6,9},{7,10},{8,7},{9,4},... | collective-permute-start | bytes 1572872 | tf_op jit(solution)/shard_map/ppermute | solution.py:334
  592.8 92.4 %collective-permute-start.52 = (bf16[2,32,16,256]{3,2,1,0:T(8,128)(2,1)}, bf16[2,32,16,256]{3,2,1,0:T(8,128)(2,1)S(1)}, u32[]{:S(2)}, u32[]{:S(2)}) collective-permute-start(bf16[2,32,16,256]{3,2,1,0:T(8,128)(2,1)} %get-tuple-element.88), channel_id=1, source_target_pairs={{0,8},{1,9},{2,10},{3,11},{4,0},{5,1},{6,2},{7,3},{8,12},{9,13},{1... | collective-permute-start | bytes 1572872 | tf_op jit(solution)/shard_map/ppermute | solution.py:334
  609.7 76.0 %collective-permute-start.53 = (bf16[2,32,16,256]{3,2,1,0:T(8,128)(2,1)}, bf16[2,32,16,256]{3,2,1,0:T(8,128)(2,1)S(1)}, u32[]{:S(2)}, u32[]{:S(2)}) collective-permute-start(bf16[2,32,16,256]{3,2,1,0:T(8,128)(2,1)} %get-tuple-element.89), channel_id=1, source_target_pairs={{0,9},{1,10},{2,11},{3,8},{4,1},{5,2},{6,3},{7,0},{8,13},{9,14},{1... | collective-permute-start | bytes 1572872 | tf_op jit(solution)/shard_map/ppermute | solution.py:334
  609.8 78.7 %collective-permute-start.54 = (bf16[2,32,16,256]{3,2,1,0:T(8,128)(2,1)}, bf16[2,32,16,256]{3,2,1,0:T(8,128)(2,1)S(1)}, u32[]{:S(2)}, u32[]{:S(2)}) collective-permute-start(bf16[2,32,16,256]{3,2,1,0:T(8,128)(2,1)} %get-tuple-element.90), channel_id=1, source_target_pairs={{0,10},{1,11},{2,8},{3,9},{4,2},{5,3},{6,0},{7,1},{8,14},{9,15},{1... | collective-permute-start | bytes 1572872 | tf_op jit(solution)/shard_map/ppermute | solution.py:334
  688.5 75.3 %collective-permute-start.25 = (bf16[2,8,16,256]{3,2,1,0:T(8,128)(2,1)S(1)}, bf16[2,8,16,256]{3,2,1,0:T(8,128)(2,1)S(1)}, u32[]{:S(2)}, u32[]{:S(2)}) collective-permute-start(bf16[2,8,16,256]{3,2,1,0:T(8,128)(2,1)S(1)} %copy-done.102), channel_id=1, source_target_pairs={{0,11},{1,8},{2,9},{3,10},{4,3},{5,0},{6,1},{7,2},{8,15},{9,12},{1... | collective-permute-start | bytes 393224 | tf_op jit(solution)/shard_map/ppermute | solution.py:334
  697.7 66.2 %collective-permute-start.26 = (bf16[2,8,16,256]{3,2,1,0:T(8,128)(2,1)S(1)}, bf16[2,8,16,256]{3,2,1,0:T(8,128)(2,1)S(1)}, u32[]{:S(2)}, u32[]{:S(2)}) collective-permute-start(bf16[2,8,16,256]{3,2,1,0:T(8,128)(2,1)S(1)} %copy-done.101), channel_id=1, source_target_pairs={{0,4},{1,5},{2,6},{3,7},{4,12},{5,13},{6,14},{7,15},{8,0},{9,1},{1... | collective-permute-start | bytes 393224 | tf_op jit(solution)/shard_map/ppermute | solution.py:334
  (146 other events, 9157.7 us)

commit v3 on v2

--- a/solution.py
+++ b/solution.py
@@ -181,6 +181,16 @@
     return jnp.dot(w3[...], x[...], preferred_element_type=jnp.float32)
 
 
+def in_place(pieces, parts, steps, body):
+    for part in range(parts):
+
+        @pl.loop(0, steps)
+        def _(own):
+            step = part * steps + own
+            rows = pl.ds(step * STEP_ROWS, STEP_ROWS)
+            body(part, own, step, [piece.at[:, rows] for piece in pieces])
+
+
 def in_steps(pieces, buffers, sems, parts, steps, body):
     def copies(step, slot):
         rows = pl.ds(step * STEP_ROWS, STEP_ROWS)
@@ -209,7 +219,7 @@
 
 
 def partial_kernel(n, *refs):
-    pieces, w3, outs, (buffers, x, sems) = refs[:n], refs[n], refs[n + 1 : -3], refs[-3:]
+    pieces, w3, outs, (x, buffers, sems) = refs[:n], refs[n], refs[n + 1 : -3], refs[-3:]
 
     def body(part, own, step, held):
         for t in range(STEP_ROWS):
@@ -218,9 +228,9 @@
     in_steps(pieces, buffers, sems, len(outs), outs[0].shape[0] // STEP_ROWS, body)
 
 
-def last_kernel(n, n_bases, start, *refs):
+def last_kernel(n, n_bases, start, near, *refs):
     pieces, w3, bases = refs[:n], refs[n], refs[n + 1 : n + 1 + n_bases]
-    out, buffers, x, held_out, sems, out_sems = refs[-6:]
+    out, x, held_out, out_sems = refs[-4:] if near else refs[-6:-2]
     part_steps = bases[0].shape[0] // STEP_ROWS
     steps = part_steps * n_bases
 
@@ -243,20 +253,28 @@
                 held_out[slot, t, lines, :] = y[:, h * 128 : (h + 1) * 128]
         copy_out(step, slot).start()
 
-    in_steps(pieces, buffers, sems, n_bases, part_steps, body)
+    if near:
+        in_place(pieces, n_bases, part_steps, body)
+    else:
+        in_steps(pieces, *refs[-2:], n_bases, part_steps, body)
     for step in range(max(steps - 2, 0), steps):
         copy_out(step, step % 2).wait()
 
 
-def in_hbm(pieces):
-    return [pltpu.with_memory_space_constraint(piece, pltpu.HBM) for piece in pieces]
-
-
-def scratch_of(pieces):
+def placed(pieces, space):
+    return [pltpu.with_memory_space_constraint(piece, space) for piece in pieces]
+
+
+def held_rows(pieces):
+    n, (_, _, chunk, width) = len(pieces), pieces[0].shape
+    return pltpu.VMEM((STEP_ROWS, 2 * n * chunk, width), jnp.bfloat16)
+
+
+def copied_rows(pieces):
     n, (_, _, chunk, width) = len(pieces), pieces[0].shape
     return [
         pltpu.VMEM((2, n, 2, STEP_ROWS, chunk, width), jnp.bfloat16),
-        pltpu.VMEM((STEP_ROWS, 2 * n * chunk, width), jnp.bfloat16),
+        pltpu.SemaphoreType.DMA((2, n)),
     ]
 
 
@@ -269,36 +287,38 @@
         in_specs=[pl.BlockSpec(memory_space=pl.ANY)] * n + [vmem],
         out_specs=[vmem] * count,
         out_shape=[pltpu.VMEM((SUM_ROWS, w3.shape[0], width), jnp.float32)] * count,
-        scratch_shapes=scratch_of(pieces) + [pltpu.SemaphoreType.DMA((2, n))],
+        scratch_shapes=[held_rows(pieces)] + copied_rows(pieces),
         compiler_params=pltpu.CompilerParams(vmem_limit_bytes=12 << 20),
         name="partial",
-    )(*in_hbm(pieces), w3)
-
-
-def last_b(pieces, w3, bases, out, start, rows):
+    )(*placed(pieces, pltpu.HBM), w3)
+
+
+def last_b(pieces, w3, bases, out, start, rows, near):
     width = pieces[0].shape[3]
     n, lines = len(pieces), w3.shape[0] * (width // 128)
     vmem = pl.BlockSpec(memory_space=pltpu.VMEM)
     any_space = pl.BlockSpec(memory_space=pl.ANY)
     given = [] if out is None else [out]
     return pl.pallas_call(
-        functools.partial(last_kernel, n, len(bases), start),
-        in_specs=[any_space] * n + [vmem] * (1 + len(bases)) + [any_space] * len(given),
+        functools.partial(last_kernel, n, len(bases), start, near),
+        in_specs=[vmem if near else any_space] * n
+        + [vmem] * (1 + len(bases))
+        + [any_space] * len(given),
         out_specs=any_space,
         out_shape=jax.ShapeDtypeStruct((rows, lines, 128), jnp.float32),
         input_output_aliases={n + 1 + len(bases): 0} if given else {},
-        scratch_shapes=scratch_of(pieces)
-        + [
+        scratch_shapes=[
+            held_rows(pieces),
             pltpu.VMEM((2, STEP_ROWS, lines, 128), jnp.float32),
-            pltpu.SemaphoreType.DMA((2, n)),
             pltpu.SemaphoreType.DMA((2,)),
-        ],
+        ]
+        + ([] if near else copied_rows(pieces)),
         compiler_params=pltpu.CompilerParams(vmem_limit_bytes=12 << 20),
         name="last",
     )(
-        *in_hbm(pieces),
+        *placed(pieces, pltpu.VMEM if near else pltpu.HBM),
         w3,
-        *[pltpu.with_memory_space_constraint(base, pltpu.VMEM) for base in bases],
+        *placed(bases, pltpu.VMEM),
         *given,
     )
 
@@ -333,19 +353,23 @@
             return block
         return lax.ppermute(block, "inter", pairs[k])
 
-    stem = stem_tensor[:, :, :, 0, :]
+    first = stem_tensor[:, :, :, 0, :]
+    stem = lax.optimization_barrier(first)
     arrived = []
     for j in range(B_CHUNKS):
         got = []
         for k in range(n_rounds):
+            ahead = j == 0 and k == 1
             block = lax.dynamic_slice(
-                stem,
+                first if ahead else stem,
                 (zero, zero, target[k] * jnp.uint32(local_b) + jnp.uint32(j * chunk), zero),
                 (2, local_a, chunk, width),
                 allow_negative_indices=False,
             )
-            got.append(send(jnp.transpose(block, (0, 2, 1, 3)), k))
+            block = jnp.transpose(block, (0, 2, 1, 3))
+            got.append(send(block, k))
         arrived.append(got)
+        stem, _ = lax.optimization_barrier((stem, block))
 
     where_to = jnp.stack(target).astype(jnp.int32)
     where_from = jnp.stack(partners(place, inverse_of(rounds, group), group)).astype(jnp.int32)
@@ -395,7 +419,7 @@
     out, start = None, 0
     for i, count in enumerate(parts):
         own = sums[start // SUM_ROWS : (start + count) // SUM_ROWS]
-        out = last_b(returned[1 + i], w3[1], own, out, start, local_a)
+        out = last_b(returned[1 + i], w3[1], own, out, start, local_a, i == len(parts) - 1)
         start += count
     return out.reshape(local_a, size_b, 2, 1, width)
 

time: 777 us -> 797 us (1.026)
  waiting for transfers between devices: 131 us -> 275 us
  starting transfers between devices: 397 us -> 306 us
  local copies, waits for them, and re-layouts: 134 us -> 104 us
    ppermute x75, waiting for transfers between devices: 131 us -> 275 us  [send(): return lax.ppermute(block, 'inter', pairs[k])]
    ppermute x75, starting transfers between devices: 397 us -> 306 us  [send(): return lax.ppermute(block, 'inter', pairs[k])]
    dynamic_slice x34 -> x2, local copies, waits for them, and re-layouts: 51.2 us -> 2.13 us  [on_device(): lax.dynamic_slice(first if ahead else stem, (zero, zero, target[k] * jnp....]
    unnamed x208 -> x175, local copies, waits for them, and re-layouts: 7.07 us -> 24.1 us
    transpose x0 -> x2, local copies, waits for them, and re-layouts: none -> 13.2 us  [on_device(): block = jnp.transpose(block, (0, 2, 1, 3))]
    scatter x1, local copies, waits for them, and re-layouts: 18.2 us -> 7.07 us  [on_device(): permuted = jnp.zeros_like(branch_two).at[:, mode_order, :].set(branch_two)]
  transfers between devices with their start and end apart: 75 -> 75, of which waited for: 13 -> 20; matrix products, arithmetic and copies ran while one was open for 17% -> 13% of each run, Pallas kernels for 12% -> 12%
where the time goes in v3:
time: 797 us; the launch traced here: 792 us
  starting transfers between devices  306 us (38%)
  waiting for transfers between devices  275 us (35%)
  local copies, waits for them, and re-layouts  104 us (13%)
  Pallas kernels  98.1 us (12%)
    ppermute x75, starting transfers between devices, send(): return lax.ppermute(block, 'inter', pairs[k])  306 us
    ppermute x75, waiting for transfers between devices, send(): return lax.ppermute(block, 'inter', pairs[k])  275 us
    pallas_call x2, Pallas kernels, front(): pl.pallas_call(functools.partial(front_kernel, group, splits), grid=(chun...  62.9 us
    unnamed x175, local copies, waits for them, and re-layouts  24.1 us
    gather x4, local copies, waits for them, and re-layouts, on_device(): one = one[:, where_from][:, :, :, where_to].reshape(2, size_a, size_a)  23 us
    pallas_call x2, Pallas kernels, last_b(): pl.pallas_call(functools.partial(last_kernel, n, len(bases), start, near)...  20.6 us
  transfers between devices with their start and end apart: 75, of which 20 were waited for; matrix products, arithmetic and copies ran while one was open for 13% of the time, Pallas kernels for 12%

profile of v3, /device:TPU:1, one launch (start us, length us, event | category | flops | bytes accessed | tf_op | source)
XLA Modules:
  0.0 792.2 jit_solution(12067207255352898980)
XLA Ops:
  6.3 17.9 %copy.58 = bf16[2,32,512,1,256]{4,1,2,0,3:T(8,128)(2,1)} copy(bf16[2,32,512,1,256]{4,2,3,1,0:T(8,128)(2,1)} %param.6) | data formatting | bytes 33554432 | tf_op args[0]
  30.5 6.8 dynamic-slice_bitcast_fusion.14
  53.7 11.6 %collective-permute-done.13.refs_14_ = bf16[2,16,32,256]{3,2,1,0:T(8,128)(2,1)S(1)} collective-permute-done((bf16[2,16,32,256]{3,2,1,0:T(8,128)(2,1)}, bf16[2,16,32,256]{3,2,1,0:T(8,128)(2,1)S(1)}, u32[]{:S(2)}, u32[]{:S(2)}) %collective-permute-start.13) | collective-permute-done | bytes 524320 | tf_op jit(solution)/shard_map/ppermute | solution.py:354
  65.3 11.2 %collective-permute-done.12.refs_13_ = bf16[2,16,32,256]{3,2,1,0:T(8,128)(2,1)S(1)} collective-permute-done((bf16[2,16,32,256]{3,2,1,0:T(8,128)(2,1)}, bf16[2,16,32,256]{3,2,1,0:T(8,128)(2,1)S(1)}, u32[]{:S(2)}, u32[]{:S(2)}) %collective-permute-start.12) | collective-permute-done | bytes 524320 | tf_op jit(solution)/shard_map/ppermute | solution.py:354
  76.5 55.0 %collective-permute-done.11.refs_12_ = bf16[2,16,32,256]{3,2,1,0:T(8,128)(2,1)} collective-permute-done((bf16[2,16,32,256]{3,2,1,0:T(8,128)(2,1)}, bf16[2,16,32,256]{3,2,1,0:T(8,128)(2,1)}, u32[]{:S(2)}, u32[]{:S(2)}) %collective-permute-start.11) | collective-permute-done | bytes 524320 | tf_op jit(solution)/shard_map/ppermute | solution.py:354
  142.5 6.4 collective-permute-done.6.refs_7_
  150.4 9.4 %collective-permute-done.5.refs_6_ = bf16[2,16,32,256]{3,2,1,0:T(8,128)(2,1)S(1)} collective-permute-done((bf16[2,16,32,256]{3,2,1,0:T(8,128)(2,1)S(1)}, bf16[2,16,32,256]{3,2,1,0:T(8,128)(2,1)S(1)}, u32[]{:S(2)}, u32[]{:S(2)}) %collective-permute-start.5) | collective-permute-done | bytes 524320 | tf_op jit(solution)/shard_map/ppermute | solution.py:354
  160.6 10.7 %collective-permute-done.4.refs_5_ = bf16[2,16,32,256]{3,2,1,0:T(8,128)(2,1)S(1)} collective-permute-done((bf16[2,16,32,256]{3,2,1,0:T(8,128)(2,1)S(1)}, bf16[2,16,32,256]{3,2,1,0:T(8,128)(2,1)S(1)}, u32[]{:S(2)}, u32[]{:S(2)}) %collective-permute-start.4) | collective-permute-done | bytes 524320 | tf_op jit(solution)/shard_map/ppermute | solution.py:354
  172.1 41.1 %collective-permute-start.43 = (bf16[2,16,32,256]{3,2,1,0:T(8,128)(2,1)}, bf16[2,16,32,256]{3,2,1,0:T(8,128)(2,1)S(1)}, u32[]{:S(2)}, u32[]{:S(2)}) collective-permute-start(bf16[2,16,32,256]{3,2,1,0:T(8,128)(2,1)} %get-tuple-element.121), channel_id=1, source_target_pairs={{0,6},{1,7},{2,4},{3,5},{4,14},{5,15},{6,12},{7,13},{8,2},{9,3},{1... | collective-permute-start | bytes 1572872 | tf_op jit(solution)/shard_map/ppermute | solution.py:354
  221.1 7.1 scatter_fusion
  234.6 11.0 %collective-permute-done.42.refs_13_ = bf16[2,16,32,256]{3,2,1,0:T(8,128)(2,1)S(1)} collective-permute-done((bf16[2,16,32,256]{3,2,1,0:T(8,128)(2,1)}, bf16[2,16,32,256]{3,2,1,0:T(8,128)(2,1)S(1)}, u32[]{:S(2)}, u32[]{:S(2)}) %collective-permute-start.42) | collective-permute-done | bytes 524320 | tf_op jit(solution)/shard_map/ppermute | solution.py:354
  245.6 53.9 %collective-permute-done.41.refs_12_ = bf16[2,16,32,256]{3,2,1,0:T(8,128)(2,1)S(1)} collective-permute-done((bf16[2,16,32,256]{3,2,1,0:T(8,128)(2,1)}, bf16[2,16,32,256]{3,2,1,0:T(8,128)(2,1)S(1)}, u32[]{:S(2)}, u32[]{:S(2)}) %collective-permute-start.41) | collective-permute-done | bytes 524320 | tf_op jit(solution)/shard_map/ppermute | solution.py:354
  342.1 7.1 copy.36
  349.2 6.8 reshape.514
  365.2 31.8 %front.2 = (bf16[2,24,16,256]{3,2,1,0:T(8,128)(2,1)}, bf16[2,8,16,256]{3,2,1,0:T(8,128)(2,1)}, bf16[2,24,16,256]{3,2,1,0:T(8,128)(2,1)}, bf16[2,8,16,256]{3,2,1,...) custom-call(bf16[2,16,32,256]{3,2,1,0:T(8,128)(2,1)S(1)} %copy-done., ...), custom_call_target="tpu_custom_call" | custom-call | tf_op jit(solution)/shard_map/front/pallas_call | solution.py:151
  408.2 7.2 collective-permute-start.22
  442.0 16.5 %collective-permute-done.62.refs_3_ = bf16[2,24,16,256]{3,2,1,0:T(8,128)(2,1)S(1)} collective-permute-done((bf16[2,24,16,256]{3,2,1,0:T(8,128)(2,1)}, bf16[2,24,16,256]{3,2,1,0:T(8,128)(2,1)S(1)}, u32[]{:S(2)}, u32[]{:S(2)}) %collective-permute-start.62) | collective-permute-done | bytes 393248 | tf_op jit(solution)/shard_map/ppermute | solution.py:354
  458.5 38.5 %collective-permute-start.67 = (bf16[2,24,16,256]{3,2,1,0:T(8,128)(2,1)}, bf16[2,24,16,256]{3,2,1,0:T(8,128)(2,1)S(1)}, u32[]{:S(2)}, u32[]{:S(2)}) collective-permute-start(bf16[2,24,16,256]{3,2,1,0:T(8,128)(2,1)} %get-tuple-element.108), channel_id=1, source_target_pairs={{0,8},{1,9},{2,10},{3,11},{4,0},{5,1},{6,2},{7,3},{8,12},{9,13},{1... | collective-permute-start | bytes 1179656 | tf_op jit(solution)/shard_map/ppermute | solution.py:354
  501.9 31.7 %collective-permute-start.71 = (bf16[2,24,16,256]{3,2,1,0:T(8,128)(2,1)}, bf16[2,24,16,256]{3,2,1,0:T(8,128)(2,1)S(1)}, u32[]{:S(2)}, u32[]{:S(2)}) collective-permute-start(bf16[2,24,16,256]{3,2,1,0:T(8,128)(2,1)} %get-tuple-element.112), channel_id=1, source_target_pairs={{0,4},{1,5},{2,6},{3,7},{4,12},{5,13},{6,14},{7,15},{8,0},{9,1},{1... | collective-permute-start | bytes 1179656 | tf_op jit(solution)/shard_map/ppermute | solution.py:354
  536.4 31.1 %front.3 = (bf16[2,32,16,256]{3,2,1,0:T(8,128)(2,1)}, bf16[2,32,16,256]{3,2,1,0:T(8,128)(2,1)}, bf16[2,32,16,256]{3,2,1,0:T(8,128)(2,1)}, bf16[2,32,16,256]{3,2,...) custom-call(bf16[2,16,32,256]{3,2,1,0:T(8,128)(2,1)S(1)} %copy-done., ...), custom_call_target="tpu_custom_call" | custom-call | tf_op jit(solution)/shard_map/front/pallas_call | solution.py:151
  574.7 8.0 %collective-permute-done.45.refs_1_ = bf16[2,32,16,256]{3,2,1,0:T(8,128)(2,1)S(1)} collective-permute-done((bf16[2,32,16,256]{3,2,1,0:T(8,128)(2,1)}, bf16[2,32,16,256]{3,2,1,0:T(8,128)(2,1)S(1)}, u32[]{:S(2)}, u32[]{:S(2)}) %collective-permute-start.45) | collective-permute-done | bytes 524320 | tf_op jit(solution)/shard_map/ppermute | solution.py:354
  588.9 26.8 %collective-permute-done.47.refs_3_ = bf16[2,32,16,256]{3,2,1,0:T(8,128)(2,1)S(1)} collective-permute-done((bf16[2,32,16,256]{3,2,1,0:T(8,128)(2,1)}, bf16[2,32,16,256]{3,2,1,0:T(8,128)(2,1)S(1)}, u32[]{:S(2)}, u32[]{:S(2)}) %collective-permute-start.47) | collective-permute-done | bytes 524320 | tf_op jit(solution)/shard_map/ppermute | solution.py:354
  615.6 16.3 %collective-permute-start.52 = (bf16[2,32,16,256]{3,2,1,0:T(8,128)(2,1)}, bf16[2,32,16,256]{3,2,1,0:T(8,128)(2,1)S(1)}, u32[]{:S(2)}, u32[]{:S(2)}) collective-permute-start(bf16[2,32,16,256]{3,2,1,0:T(8,128)(2,1)} %get-tuple-element.90), channel_id=1, source_target_pairs={{0,8},{1,9},{2,10},{3,11},{4,0},{5,1},{6,2},{7,3},{8,12},{9,13},{1... | collective-permute-start | bytes 1572872 | tf_op jit(solution)/shard_map/ppermute | solution.py:354
  632.6 30.7 %collective-permute-start.54 = (bf16[2,32,16,256]{3,2,1,0:T(8,128)(2,1)}, bf16[2,32,16,256]{3,2,1,0:T(8,128)(2,1)S(1)}, u32[]{:S(2)}, u32[]{:S(2)}) collective-permute-start(bf16[2,32,16,256]{3,2,1,0:T(8,128)(2,1)} %get-tuple-element.92), channel_id=1, source_target_pairs={{0,10},{1,11},{2,8},{3,9},{4,2},{5,3},{6,0},{7,1},{8,14},{9,15},{1... | collective-permute-start | bytes 1572872 | tf_op jit(solution)/shard_map/ppermute | solution.py:354
  663.3 23.0 %collective-permute-start.55 = (bf16[2,32,16,256]{3,2,1,0:T(8,128)(2,1)}, bf16[2,32,16,256]{3,2,1,0:T(8,128)(2,1)S(1)}, u32[]{:S(2)}, u32[]{:S(2)}) collective-permute-start(bf16[2,32,16,256]{3,2,1,0:T(8,128)(2,1)} %get-tuple-element.93), channel_id=1, source_target_pairs={{0,11},{1,8},{2,9},{3,10},{4,3},{5,0},{6,1},{7,2},{8,15},{9,12},{1... | collective-permute-start | bytes 1572872 | tf_op jit(solution)/shard_map/ppermute | solution.py:354
  686.3 21.3 %collective-permute-start.56 = (bf16[2,32,16,256]{3,2,1,0:T(8,128)(2,1)}, bf16[2,32,16,256]{3,2,1,0:T(8,128)(2,1)S(1)}, u32[]{:S(2)}, u32[]{:S(2)}) collective-permute-start(bf16[2,32,16,256]{3,2,1,0:T(8,128)(2,1)} %get-tuple-element.94), channel_id=1, source_target_pairs={{0,4},{1,5},{2,6},{3,7},{4,12},{5,13},{6,14},{7,15},{8,0},{9,1},{1... | collective-permute-start | bytes 1572872 | tf_op jit(solution)/shard_map/ppermute | solution.py:354
  714.1 6.9 collective-permute-done.56.refs_12_
  721.5 10.1 %collective-permute-done.57.refs_13_ = bf16[2,32,16,256]{3,2,1,0:T(8,128)(2,1)S(1)} collective-permute-done((bf16[2,32,16,256]{3,2,1,0:T(8,128)(2,1)}, bf16[2,32,16,256]{3,2,1,0:T(8,128)(2,1)S(1)}, u32[]{:S(2)}, u32[]{:S(2)}) %collective-permute-start.57) | collective-permute-done | bytes 524320 | tf_op jit(solution)/shard_map/ppermute | solution.py:354
  733.9 8.9 %collective-permute-done.58.refs_14_ = bf16[2,32,16,256]{3,2,1,0:T(8,128)(2,1)S(1)} collective-permute-done((bf16[2,32,16,256]{3,2,1,0:T(8,128)(2,1)}, bf16[2,32,16,256]{3,2,1,0:T(8,128)(2,1)S(1)}, u32[]{:S(2)}, u32[]{:S(2)}) %collective-permute-start.58) | collective-permute-done | bytes 524320 | tf_op jit(solution)/shard_map/ppermute | solution.py:354
  744.9 10.8 %collective-permute-done.59.refs_15_ = bf16[2,32,16,256]{3,2,1,0:T(8,128)(2,1)S(1)} collective-permute-done((bf16[2,32,16,256]{3,2,1,0:T(8,128)(2,1)}, bf16[2,32,16,256]{3,2,1,0:T(8,128)(2,1)S(1)}, u32[]{:S(2)}, u32[]{:S(2)}) %collective-permute-start.59) | collective-permute-done | bytes 524320 | tf_op jit(solution)/shard_map/ppermute | solution.py:354
  756.5 14.7 %partial.1 = (f32[8,1024,256]{2,1,0:T(8,128)S(1)}, f32[8,1024,256]{2,1,0:T(8,128)S(1)}, f32[8,1024,256]{2,1,0:T(8,128)S(1)}, f32[8,1024,256]{2,1,0:T(8,128)S(1)}) custom-call(bf16[2,32,16,256]{3,2,1,0:T(8,128)(2,1)} %get-tuple-element.82.refs_0_, bf16[2,32,16,256]{3,2,1,0:T(8,128)(2,1)} %copy-done.49, bf16[2,32,16,256]{3,2,1,0:T(8,128)(2,1)} %copy-done.50, ...), custom_call_target="tpu_custom_call" | custom-call | tf_op jit(solution)/shard_map/partial/pallas_call | solution.py:285
  771.3 15.8 %last.2.refs_18_ = f32[32,2048,128]{2,1,0:T(8,128)} custom-call(bf16[2,24,16,256]{3,2,1,0:T(8,128)(2,1)} %get-tuple-element.100.refs_0_, bf16[2,24,16,256]{3,2,1,0:T(8,128)(2,1)} %copy-done.70, bf16[2,24,16,256]{3,2,1,0:T(8,128)(2,1)} %copy-done.71, bf16[2,24,16,256]{3,2,1,0:T(8,128)(2,1)} %copy-done.72, bf16[2,24,16,256]{3,2,1,0:T(8,128)(2,1)} %copy-done.73, ...), custom_call_target="tpu_custom_call" | custom-call | tf_op jit(solution)/shard_map/last/pallas_call | solution.py:302
  (339 shorter events, 184.8 us)
Async XLA Ops:
  40.4 91.0 %collective-permute-start.11 = (bf16[2,16,32,256]{3,2,1,0:T(8,128)(2,1)}, bf16[2,16,32,256]{3,2,1,0:T(8,128)(2,1)}, u32[]{:S(2)}, u32[]{:S(2)}) collective-permute-start(bf16[2,16,32,256]{3,2,1,0:T(8,128)(2,1)} %get-tuple-element.139), channel_id=1, source_target_pairs={{0,4},{1,5},{2,6},{3,7},{4,12},{5,13},{6,14},{7,15},{8,0},{9,1},{1... | collective-permute-start | bytes 1572872 | tf_op jit(solution)/shard_map/ppermute | solution.py:354
  47.5 88.7 %collective-permute-start.10 = (bf16[2,16,32,256]{3,2,1,0:T(8,128)(2,1)}, bf16[2,16,32,256]{3,2,1,0:T(8,128)(2,1)S(1)}, u32[]{:S(2)}, u32[]{:S(2)}) collective-permute-start(bf16[2,16,32,256]{3,2,1,0:T(8,128)(2,1)} %get-tuple-element.140), channel_id=1, source_target_pairs={{0,11},{1,8},{2,9},{3,10},{4,3},{5,0},{6,1},{7,2},{8,15},{9,12},{1... | collective-permute-start | bytes 1572872 | tf_op jit(solution)/shard_map/ppermute | solution.py:354
  53.5 87.3 %collective-permute-start.9 = (bf16[2,16,32,256]{3,2,1,0:T(8,128)(2,1)}, bf16[2,16,32,256]{3,2,1,0:T(8,128)(2,1)S(1)}, u32[]{:S(2)}, u32[]{:S(2)}) collective-permute-start(bf16[2,16,32,256]{3,2,1,0:T(8,128)(2,1)} %get-tuple-element.141), channel_id=1, source_target_pairs={{0,10},{1,11},{2,8},{3,9},{4,2},{5,3},{6,0},{7,1},{8,14},{9,15},{1... | collective-permute-start | bytes 1572872 | tf_op jit(solution)/shard_map/ppermute | solution.py:354
  65.3 76.4 %collective-permute-start.8 = (bf16[2,16,32,256]{3,2,1,0:T(8,128)(2,1)}, bf16[2,16,32,256]{3,2,1,0:T(8,128)(2,1)}, u32[]{:S(2)}, u32[]{:S(2)}) collective-permute-start(bf16[2,16,32,256]{3,2,1,0:T(8,128)(2,1)} %get-tuple-element.142), channel_id=1, source_target_pairs={{0,9},{1,10},{2,11},{3,8},{4,1},{5,2},{6,3},{7,0},{8,13},{9,14},{1... | collective-permute-start | bytes 1572872 | tf_op jit(solution)/shard_map/ppermute | solution.py:354
  76.5 65.2 %collective-permute-start.7 = (bf16[2,16,32,256]{3,2,1,0:T(8,128)(2,1)}, bf16[2,16,32,256]{3,2,1,0:T(8,128)(2,1)}, u32[]{:S(2)}, u32[]{:S(2)}) collective-permute-start(bf16[2,16,32,256]{3,2,1,0:T(8,128)(2,1)} %get-tuple-element.143), channel_id=1, source_target_pairs={{0,8},{1,9},{2,10},{3,11},{4,0},{5,1},{6,2},{7,3},{8,12},{9,13},{1... | collective-permute-start | bytes 1572872 | tf_op jit(solution)/shard_map/ppermute | solution.py:354
  141.7 71.5 %collective-permute-start.3 = (bf16[2,16,32,256]{3,2,1,0:T(8,128)(2,1)S(1)}, bf16[2,16,32,256]{3,2,1,0:T(8,128)(2,1)S(1)}, u32[]{:S(2)}, u32[]{:S(2)}) collective-permute-start(bf16[2,16,32,256]{3,2,1,0:T(8,128)(2,1)S(1)} %copy-done.67), channel_id=1, source_target_pairs={{0,3},{1,0},{2,1},{3,2},{4,7},{5,4},{6,5},{7,6},{8,11},{9,8},{10,9... | collective-permute-start | bytes 1572872 | tf_op jit(solution)/shard_map/ppermute | solution.py:354
  141.7 72.3 %collective-permute-start.2 = (bf16[2,16,32,256]{3,2,1,0:T(8,128)(2,1)S(1)}, bf16[2,16,32,256]{3,2,1,0:T(8,128)(2,1)S(1)}, u32[]{:S(2)}, u32[]{:S(2)}) collective-permute-start(bf16[2,16,32,256]{3,2,1,0:T(8,128)(2,1)S(1)} %copy-done.66), channel_id=1, source_target_pairs={{0,2},{1,3},{2,0},{3,1},{4,6},{5,7},{6,4},{7,5},{8,10},{9,11},{10,... | collective-permute-start | bytes 1572872 | tf_op jit(solution)/shard_map/ppermute | solution.py:354
  148.9 69.8 %collective-permute-start.1 = (bf16[2,16,32,256]{3,2,1,0:T(8,128)(2,1)S(1)}, bf16[2,16,32,256]{3,2,1,0:T(8,128)(2,1)S(1)}, u32[]{:S(2)}, u32[]{:S(2)}) collective-permute-start(bf16[2,16,32,256]{3,2,1,0:T(8,128)(2,1)S(1)} %copy-done.65), channel_id=1, source_target_pairs={{0,1},{1,2},{2,3},{3,0},{4,5},{5,6},{6,7},{7,4},{8,9},{9,10},{10,1... | collective-permute-start | bytes 1572872 | tf_op jit(solution)/shard_map/ppermute | solution.py:354
  160.6 69.4 %collective-permute-start = (bf16[2,16,32,256]{3,2,1,0:T(8,128)(2,1)}, bf16[2,16,32,256]{3,2,1,0:T(8,128)(2,1)S(1)}, u32[]{:S(2)}, u32[]{:S(2)}) collective-permute-start(bf16[2,16,32,256]{3,2,1,0:T(8,128)(2,1)} %get-tuple-element.150), channel_id=1, source_target_pairs={{0,12},{1,13},{2,14},{3,15},{4,8},{5,9},{6,10},{7,11},{8,4},{9,5},... | collective-permute-start | bytes 1572872 | tf_op jit(solution)/shard_map/ppermute | solution.py:354
  172.1 62.3 %collective-permute-start.43 = (bf16[2,16,32,256]{3,2,1,0:T(8,128)(2,1)}, bf16[2,16,32,256]{3,2,1,0:T(8,128)(2,1)S(1)}, u32[]{:S(2)}, u32[]{:S(2)}) collective-permute-start(bf16[2,16,32,256]{3,2,1,0:T(8,128)(2,1)} %get-tuple-element.121), channel_id=1, source_target_pairs={{0,6},{1,7},{2,4},{3,5},{4,14},{5,15},{6,12},{7,13},{8,2},{9,3},{1... | collective-permute-start | bytes 1572872 | tf_op jit(solution)/shard_map/ppermute | solution.py:354
  214.8 84.7 %collective-permute-start.41 = (bf16[2,16,32,256]{3,2,1,0:T(8,128)(2,1)}, bf16[2,16,32,256]{3,2,1,0:T(8,128)(2,1)S(1)}, u32[]{:S(2)}, u32[]{:S(2)}) collective-permute-start(bf16[2,16,32,256]{3,2,1,0:T(8,128)(2,1)} %get-tuple-element.123), channel_id=1, source_target_pairs={{0,4},{1,5},{2,6},{3,7},{4,12},{5,13},{6,14},{7,15},{8,0},{9,1},{1... | collective-permute-start | bytes 1572872 | tf_op jit(solution)/shard_map/ppermute | solution.py:354
  219.6 84.8 %collective-permute-start.40 = (bf16[2,16,32,256]{3,2,1,0:T(8,128)(2,1)}, bf16[2,16,32,256]{3,2,1,0:T(8,128)(2,1)S(1)}, u32[]{:S(2)}, u32[]{:S(2)}) collective-permute-start(bf16[2,16,32,256]{3,2,1,0:T(8,128)(2,1)} %get-tuple-element.124), channel_id=1, source_target_pairs={{0,11},{1,8},{2,9},{3,10},{4,3},{5,0},{6,1},{7,2},{8,15},{9,12},{1... | collective-permute-start | bytes 1572872 | tf_op jit(solution)/shard_map/ppermute | solution.py:354
  229.9 128.8 %collective-permute-start.39 = (bf16[2,16,32,256]{3,2,1,0:T(8,128)(2,1)}, bf16[2,16,32,256]{3,2,1,0:T(8,128)(2,1)}, u32[]{:S(2)}, u32[]{:S(2)}) collective-permute-start(bf16[2,16,32,256]{3,2,1,0:T(8,128)(2,1)} %get-tuple-element.125), channel_id=1, source_target_pairs={{0,10},{1,11},{2,8},{3,9},{4,2},{5,3},{6,0},{7,1},{8,14},{9,15},{1... | collective-permute-start | bytes 1572872 | tf_op jit(solution)/shard_map/ppermute | solution.py:354
  234.4 124.4 %collective-permute-start.38 = (bf16[2,16,32,256]{3,2,1,0:T(8,128)(2,1)}, bf16[2,16,32,256]{3,2,1,0:T(8,128)(2,1)}, u32[]{:S(2)}, u32[]{:S(2)}) collective-permute-start(bf16[2,16,32,256]{3,2,1,0:T(8,128)(2,1)} %get-tuple-element.126), channel_id=1, source_target_pairs={{0,9},{1,10},{2,11},{3,8},{4,1},{5,2},{6,3},{7,0},{8,13},{9,14},{1... | collective-permute-start | bytes 1572872 | tf_op jit(solution)/shard_map/ppermute | solution.py:354
  245.6 116.5 %collective-permute-start.37 = (bf16[2,16,32,256]{3,2,1,0:T(8,128)(2,1)}, bf16[2,16,32,256]{3,2,1,0:T(8,128)(2,1)}, u32[]{:S(2)}, u32[]{:S(2)}) collective-permute-start(bf16[2,16,32,256]{3,2,1,0:T(8,128)(2,1)} %get-tuple-element.127), channel_id=1, source_target_pairs={{0,8},{1,9},{2,10},{3,11},{4,0},{5,1},{6,2},{7,3},{8,12},{9,13},{1... | collective-permute-start | bytes 1572872 | tf_op jit(solution)/shard_map/ppermute | solution.py:354
  299.5 62.6 %collective-permute-start.36 = (bf16[2,16,32,256]{3,2,1,0:T(8,128)(2,1)}, bf16[2,16,32,256]{3,2,1,0:T(8,128)(2,1)}, u32[]{:S(2)}, u32[]{:S(2)}) collective-permute-start(bf16[2,16,32,256]{3,2,1,0:T(8,128)(2,1)} %get-tuple-element.128), channel_id=1, source_target_pairs={{0,15},{1,12},{2,13},{3,14},{4,11},{5,8},{6,9},{7,10},{8,7},{9,4},... | collective-permute-start | bytes 1572872 | tf_op jit(solution)/shard_map/ppermute | solution.py:354
  424.1 72.8 %collective-permute-start.63 = (bf16[2,24,16,256]{3,2,1,0:T(8,128)(2,1)}, bf16[2,24,16,256]{3,2,1,0:T(8,128)(2,1)S(1)}, u32[]{:S(2)}, u32[]{:S(2)}) collective-permute-start(bf16[2,24,16,256]{3,2,1,0:T(8,128)(2,1)} %get-tuple-element.104), channel_id=1, source_target_pairs={{0,3},{1,0},{2,1},{3,2},{4,7},{5,4},{6,5},{7,6},{8,11},{9,8},{10,9... | collective-permute-start | bytes 1179656 | tf_op jit(solution)/shard_map/ppermute | solution.py:354
  427.4 71.7 %collective-permute-start.64 = (bf16[2,24,16,256]{3,2,1,0:T(8,128)(2,1)}, bf16[2,24,16,256]{3,2,1,0:T(8,128)(2,1)S(1)}, u32[]{:S(2)}, u32[]{:S(2)}) collective-permute-start(bf16[2,24,16,256]{3,2,1,0:T(8,128)(2,1)} %get-tuple-element.105), channel_id=1, source_target_pairs={{0,13},{1,14},{2,15},{3,12},{4,9},{5,10},{6,11},{7,8},{8,5},{9,6},... | collective-permute-start | bytes 1179656 | tf_op jit(solution)/shard_map/ppermute | solution.py:354
  435.3 63.8 %collective-permute-start.65 = (bf16[2,24,16,256]{3,2,1,0:T(8,128)(2,1)}, bf16[2,24,16,256]{3,2,1,0:T(8,128)(2,1)S(1)}, u32[]{:S(2)}, u32[]{:S(2)}) collective-permute-start(bf16[2,24,16,256]{3,2,1,0:T(8,128)(2,1)} %get-tuple-element.106), channel_id=1, source_target_pairs={{0,14},{1,15},{2,12},{3,13},{4,10},{5,11},{6,8},{7,9},{8,6},{9,7},... | collective-permute-start | bytes 1179656 | tf_op jit(solution)/shard_map/ppermute | solution.py:354
  439.2 62.7 %collective-permute-start.66 = (bf16[2,24,16,256]{3,2,1,0:T(8,128)(2,1)}, bf16[2,24,16,256]{3,2,1,0:T(8,128)(2,1)S(1)}, u32[]{:S(2)}, u32[]{:S(2)}) collective-permute-start(bf16[2,24,16,256]{3,2,1,0:T(8,128)(2,1)} %get-tuple-element.107), channel_id=1, source_target_pairs={{0,15},{1,12},{2,13},{3,14},{4,11},{5,8},{6,9},{7,10},{8,7},{9,4},... | collective-permute-start | bytes 1179656 | tf_op jit(solution)/shard_map/ppermute | solution.py:354
  458.5 75.1 %collective-permute-start.67 = (bf16[2,24,16,256]{3,2,1,0:T(8,128)(2,1)}, bf16[2,24,16,256]{3,2,1,0:T(8,128)(2,1)S(1)}, u32[]{:S(2)}, u32[]{:S(2)}) collective-permute-start(bf16[2,24,16,256]{3,2,1,0:T(8,128)(2,1)} %get-tuple-element.108), channel_id=1, source_target_pairs={{0,8},{1,9},{2,10},{3,11},{4,0},{5,1},{6,2},{7,3},{8,12},{9,13},{1... | collective-permute-start | bytes 1179656 | tf_op jit(solution)/shard_map/ppermute | solution.py:354
  499.1 68.5 %collective-permute-start.70 = (bf16[2,24,16,256]{3,2,1,0:T(8,128)(2,1)}, bf16[2,24,16,256]{3,2,1,0:T(8,128)(2,1)S(1)}, u32[]{:S(2)}, u32[]{:S(2)}) collective-permute-start(bf16[2,24,16,256]{3,2,1,0:T(8,128)(2,1)} %get-tuple-element.111), channel_id=1, source_target_pairs={{0,11},{1,8},{2,9},{3,10},{4,3},{5,0},{6,1},{7,2},{8,15},{9,12},{1... | collective-permute-start | bytes 1179656 | tf_op jit(solution)/shard_map/ppermute | solution.py:354
  501.9 67.5 %collective-permute-start.71 = (bf16[2,24,16,256]{3,2,1,0:T(8,128)(2,1)}, bf16[2,24,16,256]{3,2,1,0:T(8,128)(2,1)S(1)}, u32[]{:S(2)}, u32[]{:S(2)}) collective-permute-start(bf16[2,24,16,256]{3,2,1,0:T(8,128)(2,1)} %get-tuple-element.112), channel_id=1, source_target_pairs={{0,4},{1,5},{2,6},{3,7},{4,12},{5,13},{6,14},{7,15},{8,0},{9,1},{1... | collective-permute-start | bytes 1179656 | tf_op jit(solution)/shard_map/ppermute | solution.py:354
  571.5 60.4 %collective-permute-start.48 = (bf16[2,32,16,256]{3,2,1,0:T(8,128)(2,1)}, bf16[2,32,16,256]{3,2,1,0:T(8,128)(2,1)S(1)}, u32[]{:S(2)}, u32[]{:S(2)}) collective-permute-start(bf16[2,32,16,256]{3,2,1,0:T(8,128)(2,1)} %get-tuple-element.86), channel_id=1, source_target_pairs={{0,3},{1,0},{2,1},{3,2},{4,7},{5,4},{6,5},{7,6},{8,11},{9,8},{10,9... | collective-permute-start | bytes 1572872 | tf_op jit(solution)/shard_map/ppermute | solution.py:354
  571.5 61.0 %collective-permute-start.49 = (bf16[2,32,16,256]{3,2,1,0:T(8,128)(2,1)}, bf16[2,32,16,256]{3,2,1,0:T(8,128)(2,1)S(1)}, u32[]{:S(2)}, u32[]{:S(2)}) collective-permute-start(bf16[2,32,16,256]{3,2,1,0:T(8,128)(2,1)} %get-tuple-element.87), channel_id=1, source_target_pairs={{0,13},{1,14},{2,15},{3,12},{4,9},{5,10},{6,11},{7,8},{8,5},{9,6},... | collective-permute-start | bytes 1572872 | tf_op jit(solution)/shard_map/ppermute | solution.py:354
  582.7 80.6 %collective-permute-start.50 = (bf16[2,32,16,256]{3,2,1,0:T(8,128)(2,1)}, bf16[2,32,16,256]{3,2,1,0:T(8,128)(2,1)S(1)}, u32[]{:S(2)}, u32[]{:S(2)}) collective-permute-start(bf16[2,32,16,256]{3,2,1,0:T(8,128)(2,1)} %get-tuple-element.88), channel_id=1, source_target_pairs={{0,14},{1,15},{2,12},{3,13},{4,10},{5,11},{6,8},{7,9},{8,6},{9,7},... | collective-permute-start | bytes 1572872 | tf_op jit(solution)/shard_map/ppermute | solution.py:354
  585.4 100.9 %collective-permute-start.51 = (bf16[2,32,16,256]{3,2,1,0:T(8,128)(2,1)}, bf16[2,32,16,256]{3,2,1,0:T(8,128)(2,1)S(1)}, u32[]{:S(2)}, u32[]{:S(2)}) collective-permute-start(bf16[2,32,16,256]{3,2,1,0:T(8,128)(2,1)} %get-tuple-element.89), channel_id=1, source_target_pairs={{0,15},{1,12},{2,13},{3,14},{4,11},{5,8},{6,9},{7,10},{8,7},{9,4},... | collective-permute-start | bytes 1572872 | tf_op jit(solution)/shard_map/ppermute | solution.py:354
  615.6 92.0 %collective-permute-start.52 = (bf16[2,32,16,256]{3,2,1,0:T(8,128)(2,1)}, bf16[2,32,16,256]{3,2,1,0:T(8,128)(2,1)S(1)}, u32[]{:S(2)}, u32[]{:S(2)}) collective-permute-start(bf16[2,32,16,256]{3,2,1,0:T(8,128)(2,1)} %get-tuple-element.90), channel_id=1, source_target_pairs={{0,8},{1,9},{2,10},{3,11},{4,0},{5,1},{6,2},{7,3},{8,12},{9,13},{1... | collective-permute-start | bytes 1572872 | tf_op jit(solution)/shard_map/ppermute | solution.py:354
  631.9 76.4 %collective-permute-start.53 = (bf16[2,32,16,256]{3,2,1,0:T(8,128)(2,1)}, bf16[2,32,16,256]{3,2,1,0:T(8,128)(2,1)S(1)}, u32[]{:S(2)}, u32[]{:S(2)}) collective-permute-start(bf16[2,32,16,256]{3,2,1,0:T(8,128)(2,1)} %get-tuple-element.91), channel_id=1, source_target_pairs={{0,9},{1,10},{2,11},{3,8},{4,1},{5,2},{6,3},{7,0},{8,13},{9,14},{1... | collective-permute-start | bytes 1572872 | tf_op jit(solution)/shard_map/ppermute | solution.py:354
  632.6 77.7 %collective-permute-start.54 = (bf16[2,32,16,256]{3,2,1,0:T(8,128)(2,1)}, bf16[2,32,16,256]{3,2,1,0:T(8,128)(2,1)S(1)}, u32[]{:S(2)}, u32[]{:S(2)}) collective-permute-start(bf16[2,32,16,256]{3,2,1,0:T(8,128)(2,1)} %get-tuple-element.92), channel_id=1, source_target_pairs={{0,10},{1,11},{2,8},{3,9},{4,2},{5,3},{6,0},{7,1},{8,14},{9,15},{1... | collective-permute-start | bytes 1572872 | tf_op jit(solution)/shard_map/ppermute | solution.py:354
  710.9 76.2 %collective-permute-start.25 = (bf16[2,8,16,256]{3,2,1,0:T(8,128)(2,1)}, bf16[2,8,16,256]{3,2,1,0:T(8,128)(2,1)S(1)}, u32[]{:S(2)}, u32[]{:S(2)}) collective-permute-start(bf16[2,8,16,256]{3,2,1,0:T(8,128)(2,1)} %get-tuple-element.76), channel_id=1, source_target_pairs={{0,11},{1,8},{2,9},{3,10},{4,3},{5,0},{6,1},{7,2},{8,15},{9,12},{1... | collective-permute-start | bytes 393224 | tf_op jit(solution)/shard_map/ppermute | solution.py:354
  720.9 66.1 %collective-permute-start.26 = (bf16[2,8,16,256]{3,2,1,0:T(8,128)(2,1)}, bf16[2,8,16,256]{3,2,1,0:T(8,128)(2,1)S(1)}, u32[]{:S(2)}, u32[]{:S(2)}) collective-permute-start(bf16[2,8,16,256]{3,2,1,0:T(8,128)(2,1)} %get-tuple-element.77), channel_id=1, source_target_pairs={{0,4},{1,5},{2,6},{3,7},{4,12},{5,13},{6,14},{7,15},{8,0},{9,1},{1... | collective-permute-start | bytes 393224 | tf_op jit(solution)/shard_map/ppermute | solution.py:354
  (129 other events, 6849.5 us)

commit v4 on v3

--- a/solution.py
+++ b/solution.py
@@ -101,6 +101,37 @@
         if turn not in turned:
             turned[turn] = (place + jnp.uint32(turn)) % inner
     return [moved[move] + turned[turn] for move, turn in rounds]
+
+
+def first_block_kernel(index, piece, out, turned):
+    _, rows, chunk, width = piece.shape
+    for c in range(2):
+        for h in range(width // 128):
+            lanes = slice(h * 128, (h + 1) * 128)
+            for a in range(rows):
+                turned[c, h, pl.ds(a, chunk, stride=rows), :] = piece[c, a, :, lanes].astype(
+                    jnp.float32
+                )
+            out[c, :, :, lanes] = (
+                turned[c, h].reshape(chunk, rows, 128).astype(jnp.bfloat16)
+            )
+
+
+def first_block(stem, index, chunk):
+    _, local_a, _, width = stem.shape
+    return pl.pallas_call(
+        first_block_kernel,
+        grid_spec=pltpu.PrefetchScalarGridSpec(
+            num_scalar_prefetch=1,
+            grid=(local_a // ROWS,),
+            in_specs=[pl.BlockSpec((2, ROWS, chunk, width), lambda a, index: (0, a, index[0], 0))],
+            out_specs=pl.BlockSpec((2, chunk, ROWS, width), lambda a, index: (0, 0, a, 0)),
+            scratch_shapes=[pltpu.VMEM((2, width // 128, chunk * ROWS, 128), jnp.float32)],
+        ),
+        out_shape=pltpu.HBM((2, chunk, local_a, width), jnp.bfloat16),
+        compiler_params=pltpu.CompilerParams(vmem_limit_bytes=4 << 20),
+        name="first_block",
+    )(index.astype(jnp.int32).reshape(1), stem)
 
 
 def front_kernel(group, splits, *refs):
@@ -353,23 +384,25 @@
             return block
         return lax.ppermute(block, "inter", pairs[k])
 
-    first = stem_tensor[:, :, :, 0, :]
-    stem = lax.optimization_barrier(first)
+    stem = stem_tensor[:, :, :, 0, :]
     arrived = []
     for j in range(B_CHUNKS):
         got = []
         for k in range(n_rounds):
+            start = target[k] * jnp.uint32(B_CHUNKS) + jnp.uint32(j)
             ahead = j == 0 and k == 1
-            block = lax.dynamic_slice(
-                first if ahead else stem,
-                (zero, zero, target[k] * jnp.uint32(local_b) + jnp.uint32(j * chunk), zero),
-                (2, local_a, chunk, width),
-                allow_negative_indices=False,
-            )
-            block = jnp.transpose(block, (0, 2, 1, 3))
+            if ahead:
+                block = first_block(stem, start, chunk)
+            else:
+                block = lax.dynamic_slice(
+                    stem,
+                    (zero, zero, start * jnp.uint32(chunk), zero),
+                    (2, local_a, chunk, width),
+                    allow_negative_indices=False,
+                )
+                block = jnp.transpose(block, (0, 2, 1, 3))
             got.append(send(block, k))
         arrived.append(got)
-        stem, _ = lax.optimization_barrier((stem, block))
 
     where_to = jnp.stack(target).astype(jnp.int32)
     where_from = jnp.stack(partners(place, inverse_of(rounds, group), group)).astype(jnp.int32)

time: 797 us -> 787 us (0.987)
  waiting for transfers between devices: 275 us -> 120 us
  starting transfers between devices: 306 us -> 412 us
  local copies, waits for them, and re-layouts: 104 us -> 139 us
    ppermute x75, waiting for transfers between devices: 275 us -> 120 us  [send(): return lax.ppermute(block, 'inter', pairs[k])]
    ppermute x75, starting transfers between devices: 306 us -> 412 us  [send(): return lax.ppermute(block, 'inter', pairs[k])]
    dynamic_slice x2 -> x33, local copies, waits for them, and re-layouts: 2.13 us -> 49.1 us  [on_device(): lax.dynamic_slice(stem, (zero, zero, start * jnp.uint32(chunk), zero), (2...]
    transpose x2 -> x0, local copies, waits for them, and re-layouts: 13.2 us -> none  [on_device(): block = jnp.transpose(block, (0, 2, 1, 3))]
    scatter x1, local copies, waits for them, and re-layouts: 7.07 us -> 18.2 us  [on_device(): permuted = jnp.zeros_like(branch_two).at[:, mode_order, :].set(branch_two)]
    unnamed x175 -> x188, local copies, waits for them, and re-layouts: 24.1 us -> 14.3 us
  transfers between devices with their start and end apart: 75 -> 75, of which waited for: 20 -> 12; matrix products, arithmetic and copies ran while one was open for 13% -> 17% of each run, Pallas kernels for 12% -> 12%
where the time goes in v4:
time: 787 us; the launch traced here: 781 us
  starting transfers between devices  412 us (52%)
  local copies, waits for them, and re-layouts  139 us (18%)
  waiting for transfers between devices  120 us (15%)
  Pallas kernels  99.7 us (13%)
    ppermute x75, starting transfers between devices, send(): return lax.ppermute(block, 'inter', pairs[k])  412 us
    ppermute x75, waiting for transfers between devices, send(): return lax.ppermute(block, 'inter', pairs[k])  120 us
    pallas_call x2, Pallas kernels, front(): pl.pallas_call(functools.partial(front_kernel, group, splits), grid=(chun...  62.9 us
    dynamic_slice x33, local copies, waits for them, and re-layouts, on_device(): lax.dynamic_slice(stem, (zero, zero, start * jnp.uint32(chunk), zero), (2...  49.1 us
    gather x4, local copies, waits for them, and re-layouts, on_device(): one = one[:, where_from][:, :, :, where_to].reshape(2, size_a, size_a)  23 us
    pallas_call x2, Pallas kernels, last_b(): pl.pallas_call(functools.partial(last_kernel, n, len(bases), start, near)...  20.5 us
    scatter x1, local copies, waits for them, and re-layouts, on_device(): permuted = jnp.zeros_like(branch_two).at[:, mode_order, :].set(branch_two)  18.2 us
  transfers between devices with their start and end apart: 75, of which 12 were waited for; matrix products, arithmetic and copies ran while one was open for 17% of the time, Pallas kernels for 12%

profile of v4, /device:TPU:1, one launch (start us, length us, event | category | flops | bytes accessed | tf_op | source)
XLA Modules:
  0.0 780.7 jit_solution(3143284995101339768)
XLA Ops:
  36.4 7.5 constant_dynamic-slice_fusion
  51.8 44.5 %collective-permute-start.7 = (bf16[2,16,32,256]{3,2,1,0:T(8,128)(2,1)}, bf16[2,16,32,256]{3,2,1,0:T(8,128)(2,1)}, u32[]{:S(2)}, u32[]{:S(2)}) collective-permute-start(bf16[2,16,32,256]{3,2,1,0:T(8,128)(2,1)} %bitcast.208), channel_id=1, source_target_pairs={{0,8},{1,9},{2,10},{3,11},{4,0},{5,1},{6,2},{7,3},{8,12},{9,13},{1... | collective-permute-start | bytes 1572872 | tf_op jit(solution)/shard_map/ppermute | solution.py:385
  115.1 13.6 %collective-permute-start.9 = (bf16[2,16,32,256]{3,2,1,0:T(8,128)(2,1)S(1)}, bf16[2,16,32,256]{3,2,1,0:T(8,128)(2,1)S(1)}, u32[]{:S(2)}, u32[]{:S(2)}) collective-permute-start(bf16[2,16,32,256]{3,2,1,0:T(8,128)(2,1)S(1)} %bitcast.249), channel_id=1, source_target_pairs={{0,10},{1,11},{2,8},{3,9},{4,2},{5,3},{6,0},{7,1},{8,14},{9,15},{1... | collective-permute-start | bytes 1572872 | tf_op jit(solution)/shard_map/ppermute | solution.py:385
  128.7 21.9 %collective-permute-start.10 = (bf16[2,16,32,256]{3,2,1,0:T(8,128)(2,1)S(1)}, bf16[2,16,32,256]{3,2,1,0:T(8,128)(2,1)S(1)}, u32[]{:S(2)}, u32[]{:S(2)}) collective-permute-start(bf16[2,16,32,256]{3,2,1,0:T(8,128)(2,1)S(1)} %bitcast.248), channel_id=1, source_target_pairs={{0,11},{1,8},{2,9},{3,10},{4,3},{5,0},{6,1},{7,2},{8,15},{9,12},{1... | collective-permute-start | bytes 1572872 | tf_op jit(solution)/shard_map/ppermute | solution.py:385
  150.7 19.8 %collective-permute-start.43 = (bf16[2,16,32,256]{3,2,1,0:T(8,128)(2,1)S(1)}, bf16[2,16,32,256]{3,2,1,0:T(8,128)(2,1)S(1)}, u32[]{:S(2)}, u32[]{:S(2)}) collective-permute-start(bf16[2,16,32,256]{3,2,1,0:T(8,128)(2,1)S(1)} %bitcast.245), channel_id=1, source_target_pairs={{0,6},{1,7},{2,4},{3,5},{4,14},{5,15},{6,12},{7,13},{8,2},{9,3},{1... | collective-permute-start | bytes 1572872 | tf_op jit(solution)/shard_map/ppermute | solution.py:385
  183.7 11.5 %collective-permute-done.11.refs_12_ = bf16[2,16,32,256]{3,2,1,0:T(8,128)(2,1)S(1)} collective-permute-done((bf16[2,16,32,256]{3,2,1,0:T(8,128)(2,1)}, bf16[2,16,32,256]{3,2,1,0:T(8,128)(2,1)S(1)}, u32[]{:S(2)}, u32[]{:S(2)}) %collective-permute-start.11) | collective-permute-done | bytes 524320 | tf_op jit(solution)/shard_map/ppermute | solution.py:385
  196.0 8.4 %collective-permute-done.12.refs_13_ = bf16[2,16,32,256]{3,2,1,0:T(8,128)(2,1)S(1)} collective-permute-done((bf16[2,16,32,256]{3,2,1,0:T(8,128)(2,1)S(1)}, bf16[2,16,32,256]{3,2,1,0:T(8,128)(2,1)S(1)}, u32[]{:S(2)}, u32[]{:S(2)}) %collective-permute-start.12) | collective-permute-done | bytes 524320 | tf_op jit(solution)/shard_map/ppermute | solution.py:385
  215.6 18.2 %scatter_fusion = bf16[2,256,256]{2,0,1:T(2,128)(2,1)S(1)} fusion(bf16[2,256,256]{2,0,1:T(2,128)(2,1)S(1)} %broadcast_in_dim.4, s32[256]{0:T(256)S(1)} %compare_select_fusion, bf16[256,2,256]{2,1,0:T(2,128)(2,1)} %copy.110), kind=kCustom, calls=%fused_computation.4 | custom fusion | bytes 787456 | tf_op jit(solution)/shard_map/scatter | solution.py:419
  261.5 5.9 reshape.546
  283.3 7.1 copy.109
  290.4 6.8 reshape.547
  307.7 22.9 %collective-permute-start.40 = (bf16[2,16,32,256]{3,2,1,0:T(8,128)(2,1)S(1)}, bf16[2,16,32,256]{3,2,1,0:T(8,128)(2,1)S(1)}, u32[]{:S(2)}, u32[]{:S(2)}) collective-permute-start(bf16[2,16,32,256]{3,2,1,0:T(8,128)(2,1)S(1)} %bitcast.241), channel_id=1, source_target_pairs={{0,11},{1,8},{2,9},{3,10},{4,3},{5,0},{6,1},{7,2},{8,15},{9,12},{1... | collective-permute-start | bytes 1572872 | tf_op jit(solution)/shard_map/ppermute | solution.py:385
  330.6 20.5 %collective-permute-start.41 = (bf16[2,16,32,256]{3,2,1,0:T(8,128)(2,1)S(1)}, bf16[2,16,32,256]{3,2,1,0:T(8,128)(2,1)S(1)}, u32[]{:S(2)}, u32[]{:S(2)}) collective-permute-start(bf16[2,16,32,256]{3,2,1,0:T(8,128)(2,1)S(1)} %bitcast.239), channel_id=1, source_target_pairs={{0,4},{1,5},{2,6},{3,7},{4,12},{5,13},{6,14},{7,15},{8,0},{9,1},{1... | collective-permute-start | bytes 1572872 | tf_op jit(solution)/shard_map/ppermute | solution.py:385
  355.2 31.9 %front.2 = (bf16[2,24,16,256]{3,2,1,0:T(8,128)(2,1)}, bf16[2,8,16,256]{3,2,1,0:T(8,128)(2,1)}, bf16[2,24,16,256]{3,2,1,0:T(8,128)(2,1)}, bf16[2,8,16,256]{3,2,1,...) custom-call(bf16[2,16,32,256]{3,2,1,0:T(8,128)(2,1)S(1)} %bitcast.22, ...), custom_call_target="tpu_custom_call" | custom-call | tf_op jit(solution)/shard_map/front/pallas_call | solution.py:182
  401.6 13.0 %collective-permute-start.24 = (bf16[2,8,16,256]{3,2,1,0:T(8,128)(2,1)}, bf16[2,8,16,256]{3,2,1,0:T(8,128)(2,1)S(1)}, u32[]{:S(2)}, u32[]{:S(2)}) collective-permute-start(bf16[2,8,16,256]{3,2,1,0:T(8,128)(2,1)} %get-tuple-element.73), channel_id=1, source_target_pairs={{0,10},{1,11},{2,8},{3,9},{4,2},{5,3},{6,0},{7,1},{8,14},{9,15},{1... | collective-permute-start | bytes 393224 | tf_op jit(solution)/shard_map/ppermute | solution.py:385
  420.9 8.2 %collective-permute-done.60.refs_1_ = bf16[2,24,16,256]{3,2,1,0:T(8,128)(2,1)S(1)} collective-permute-done((bf16[2,24,16,256]{3,2,1,0:T(8,128)(2,1)}, bf16[2,24,16,256]{3,2,1,0:T(8,128)(2,1)S(1)}, u32[]{:S(2)}, u32[]{:S(2)}) %collective-permute-start.60) | collective-permute-done | bytes 393248 | tf_op jit(solution)/shard_map/ppermute | solution.py:385
  433.5 15.9 %collective-permute-done.62.refs_3_ = bf16[2,24,16,256]{3,2,1,0:T(8,128)(2,1)S(1)} collective-permute-done((bf16[2,24,16,256]{3,2,1,0:T(8,128)(2,1)}, bf16[2,24,16,256]{3,2,1,0:T(8,128)(2,1)S(1)}, u32[]{:S(2)}, u32[]{:S(2)}) %collective-permute-start.62) | collective-permute-done | bytes 393248 | tf_op jit(solution)/shard_map/ppermute | solution.py:385
  449.5 37.3 %collective-permute-start.67 = (bf16[2,24,16,256]{3,2,1,0:T(8,128)(2,1)}, bf16[2,24,16,256]{3,2,1,0:T(8,128)(2,1)S(1)}, u32[]{:S(2)}, u32[]{:S(2)}) collective-permute-start(bf16[2,24,16,256]{3,2,1,0:T(8,128)(2,1)} %get-tuple-element.106), channel_id=1, source_target_pairs={{0,8},{1,9},{2,10},{3,11},{4,0},{5,1},{6,2},{7,3},{8,12},{9,13},{1... | collective-permute-start | bytes 1179656 | tf_op jit(solution)/shard_map/ppermute | solution.py:385
  493.4 29.8 %collective-permute-start.71 = (bf16[2,24,16,256]{3,2,1,0:T(8,128)(2,1)}, bf16[2,24,16,256]{3,2,1,0:T(8,128)(2,1)S(1)}, u32[]{:S(2)}, u32[]{:S(2)}) collective-permute-start(bf16[2,24,16,256]{3,2,1,0:T(8,128)(2,1)} %get-tuple-element.110), channel_id=1, source_target_pairs={{0,4},{1,5},{2,6},{3,7},{4,12},{5,13},{6,14},{7,15},{8,0},{9,1},{1... | collective-permute-start | bytes 1179656 | tf_op jit(solution)/shard_map/ppermute | solution.py:385
  525.7 31.1 %front.3 = (bf16[2,32,16,256]{3,2,1,0:T(8,128)(2,1)}, bf16[2,32,16,256]{3,2,1,0:T(8,128)(2,1)}, bf16[2,32,16,256]{3,2,1,0:T(8,128)(2,1)}, bf16[2,32,16,256]{3,2,...) custom-call(bf16[2,16,32,256]{3,2,1,0:T(8,128)(2,1)S(1)} %bitcast.22, ...), custom_call_target="tpu_custom_call" | custom-call | tf_op jit(solution)/shard_map/front/pallas_call | solution.py:182
  565.5 6.5 collective-permute-done.45.refs_1_
  578.3 29.1 %collective-permute-done.47.refs_3_ = bf16[2,32,16,256]{3,2,1,0:T(8,128)(2,1)S(1)} collective-permute-done((bf16[2,32,16,256]{3,2,1,0:T(8,128)(2,1)}, bf16[2,32,16,256]{3,2,1,0:T(8,128)(2,1)S(1)}, u32[]{:S(2)}, u32[]{:S(2)}) %collective-permute-start.47) | collective-permute-done | bytes 524320 | tf_op jit(solution)/shard_map/ppermute | solution.py:385
  607.4 14.4 %collective-permute-start.52 = (bf16[2,32,16,256]{3,2,1,0:T(8,128)(2,1)}, bf16[2,32,16,256]{3,2,1,0:T(8,128)(2,1)S(1)}, u32[]{:S(2)}, u32[]{:S(2)}) collective-permute-start(bf16[2,32,16,256]{3,2,1,0:T(8,128)(2,1)} %get-tuple-element.88), channel_id=1, source_target_pairs={{0,8},{1,9},{2,10},{3,11},{4,0},{5,1},{6,2},{7,3},{8,12},{9,13},{1... | collective-permute-start | bytes 1572872 | tf_op jit(solution)/shard_map/ppermute | solution.py:385
  621.9 31.3 %collective-permute-start.54 = (bf16[2,32,16,256]{3,2,1,0:T(8,128)(2,1)}, bf16[2,32,16,256]{3,2,1,0:T(8,128)(2,1)S(1)}, u32[]{:S(2)}, u32[]{:S(2)}) collective-permute-start(bf16[2,32,16,256]{3,2,1,0:T(8,128)(2,1)} %get-tuple-element.90), channel_id=1, source_target_pairs={{0,10},{1,11},{2,8},{3,9},{4,2},{5,3},{6,0},{7,1},{8,14},{9,15},{1... | collective-permute-start | bytes 1572872 | tf_op jit(solution)/shard_map/ppermute | solution.py:385
  653.3 23.0 %collective-permute-start.55 = (bf16[2,32,16,256]{3,2,1,0:T(8,128)(2,1)}, bf16[2,32,16,256]{3,2,1,0:T(8,128)(2,1)S(1)}, u32[]{:S(2)}, u32[]{:S(2)}) collective-permute-start(bf16[2,32,16,256]{3,2,1,0:T(8,128)(2,1)} %get-tuple-element.91), channel_id=1, source_target_pairs={{0,11},{1,8},{2,9},{3,10},{4,3},{5,0},{6,1},{7,2},{8,15},{9,12},{1... | collective-permute-start | bytes 1572872 | tf_op jit(solution)/shard_map/ppermute | solution.py:385
  676.3 21.0 %collective-permute-start.56 = (bf16[2,32,16,256]{3,2,1,0:T(8,128)(2,1)}, bf16[2,32,16,256]{3,2,1,0:T(8,128)(2,1)S(1)}, u32[]{:S(2)}, u32[]{:S(2)}) collective-permute-start(bf16[2,32,16,256]{3,2,1,0:T(8,128)(2,1)} %get-tuple-element.92), channel_id=1, source_target_pairs={{0,4},{1,5},{2,6},{3,7},{4,12},{5,13},{6,14},{7,15},{8,0},{9,1},{1... | collective-permute-start | bytes 1572872 | tf_op jit(solution)/shard_map/ppermute | solution.py:385
  702.7 7.3 collective-permute-done.56.refs_12_
  711.1 9.1 %collective-permute-done.57.refs_13_ = bf16[2,32,16,256]{3,2,1,0:T(8,128)(2,1)S(1)} collective-permute-done((bf16[2,32,16,256]{3,2,1,0:T(8,128)(2,1)}, bf16[2,32,16,256]{3,2,1,0:T(8,128)(2,1)S(1)}, u32[]{:S(2)}, u32[]{:S(2)}) %collective-permute-start.57) | collective-permute-done | bytes 524320 | tf_op jit(solution)/shard_map/ppermute | solution.py:385
  723.5 9.3 %collective-permute-done.58.refs_14_ = bf16[2,32,16,256]{3,2,1,0:T(8,128)(2,1)S(1)} collective-permute-done((bf16[2,32,16,256]{3,2,1,0:T(8,128)(2,1)}, bf16[2,32,16,256]{3,2,1,0:T(8,128)(2,1)S(1)}, u32[]{:S(2)}, u32[]{:S(2)}) %collective-permute-start.58) | collective-permute-done | bytes 524320 | tf_op jit(solution)/shard_map/ppermute | solution.py:385
  734.5 9.4 %collective-permute-done.59.refs_15_ = bf16[2,32,16,256]{3,2,1,0:T(8,128)(2,1)S(1)} collective-permute-done((bf16[2,32,16,256]{3,2,1,0:T(8,128)(2,1)}, bf16[2,32,16,256]{3,2,1,0:T(8,128)(2,1)S(1)}, u32[]{:S(2)}, u32[]{:S(2)}) %collective-permute-start.59) | collective-permute-done | bytes 524320 | tf_op jit(solution)/shard_map/ppermute | solution.py:385
  745.2 14.7 %partial.1 = (f32[8,1024,256]{2,1,0:T(8,128)S(1)}, f32[8,1024,256]{2,1,0:T(8,128)S(1)}, f32[8,1024,256]{2,1,0:T(8,128)S(1)}, f32[8,1024,256]{2,1,0:T(8,128)S(1)}) custom-call(bf16[2,32,16,256]{3,2,1,0:T(8,128)(2,1)} %get-tuple-element.80.refs_0_, bf16[2,32,16,256]{3,2,1,0:T(8,128)(2,1)} %copy-done.56, bf16[2,32,16,256]{3,2,1,0:T(8,128)(2,1)} %copy-done.57, ...), custom_call_target="tpu_custom_call" | custom-call | tf_op jit(solution)/shard_map/partial/pallas_call | solution.py:316
  759.9 15.7 %last.2.refs_18_ = f32[32,2048,128]{2,1,0:T(8,128)} custom-call(bf16[2,24,16,256]{3,2,1,0:T(8,128)(2,1)} %get-tuple-element.98.refs_0_, bf16[2,24,16,256]{3,2,1,0:T(8,128)(2,1)} %copy-done.74, bf16[2,24,16,256]{3,2,1,0:T(8,128)(2,1)} %copy-done.75, bf16[2,24,16,256]{3,2,1,0:T(8,128)(2,1)} %copy-done.76, bf16[2,24,16,256]{3,2,1,0:T(8,128)(2,1)} %copy-done.77, ...), custom_call_target="tpu_custom_call" | custom-call | tf_op jit(solution)/shard_map/last/pallas_call | solution.py:333
  (382 shorter events, 212.8 us)
Async XLA Ops:
  23.1 73.1 %collective-permute-start.3 = (bf16[2,16,32,256]{3,2,1,0:T(8,128)(2,1)}, bf16[2,16,32,256]{3,2,1,0:T(8,128)(2,1)}, u32[]{:S(2)}, u32[]{:S(2)}) collective-permute-start(bf16[2,16,32,256]{3,2,1,0:T(8,128)(2,1)} %bitcast.212), channel_id=1, source_target_pairs={{0,3},{1,0},{2,1},{3,2},{4,7},{5,4},{6,5},{7,6},{8,11},{9,8},{10,9... | collective-permute-start | bytes 1572872 | tf_op jit(solution)/shard_map/ppermute | solution.py:385
  43.9 70.4 %collective-permute-start.4 = (bf16[2,16,32,256]{3,2,1,0:T(8,128)(2,1)}, bf16[2,16,32,256]{3,2,1,0:T(8,128)(2,1)S(1)}, u32[]{:S(2)}, u32[]{:S(2)}) collective-permute-start(bf16[2,16,32,256]{3,2,1,0:T(8,128)(2,1)} %bitcast.211), channel_id=1, source_target_pairs={{0,13},{1,14},{2,15},{3,12},{4,9},{5,10},{6,11},{7,8},{8,5},{9,6},... | collective-permute-start | bytes 1572872 | tf_op jit(solution)/shard_map/ppermute | solution.py:385
  48.5 80.2 %collective-permute-start.5 = (bf16[2,16,32,256]{3,2,1,0:T(8,128)(2,1)}, bf16[2,16,32,256]{3,2,1,0:T(8,128)(2,1)S(1)}, u32[]{:S(2)}, u32[]{:S(2)}) collective-permute-start(bf16[2,16,32,256]{3,2,1,0:T(8,128)(2,1)} %bitcast.210), channel_id=1, source_target_pairs={{0,14},{1,15},{2,12},{3,13},{4,10},{5,11},{6,8},{7,9},{8,6},{9,7},... | collective-permute-start | bytes 1572872 | tf_op jit(solution)/shard_map/ppermute | solution.py:385
  49.5 101.2 %collective-permute-start.6 = (bf16[2,16,32,256]{3,2,1,0:T(8,128)(2,1)}, bf16[2,16,32,256]{3,2,1,0:T(8,128)(2,1)}, u32[]{:S(2)}, u32[]{:S(2)}) collective-permute-start(bf16[2,16,32,256]{3,2,1,0:T(8,128)(2,1)} %bitcast.209), channel_id=1, source_target_pairs={{0,15},{1,12},{2,13},{3,14},{4,11},{5,8},{6,9},{7,10},{8,7},{9,4},... | collective-permute-start | bytes 1572872 | tf_op jit(solution)/shard_map/ppermute | solution.py:385
  51.8 118.7 %collective-permute-start.7 = (bf16[2,16,32,256]{3,2,1,0:T(8,128)(2,1)}, bf16[2,16,32,256]{3,2,1,0:T(8,128)(2,1)}, u32[]{:S(2)}, u32[]{:S(2)}) collective-permute-start(bf16[2,16,32,256]{3,2,1,0:T(8,128)(2,1)} %bitcast.208), channel_id=1, source_target_pairs={{0,8},{1,9},{2,10},{3,11},{4,0},{5,1},{6,2},{7,3},{8,12},{9,13},{1... | collective-permute-start | bytes 1572872 | tf_op jit(solution)/shard_map/ppermute | solution.py:385
  96.2 74.3 %collective-permute-start.8 = (bf16[2,16,32,256]{3,2,1,0:T(8,128)(2,1)}, bf16[2,16,32,256]{3,2,1,0:T(8,128)(2,1)}, u32[]{:S(2)}, u32[]{:S(2)}) collective-permute-start(bf16[2,16,32,256]{3,2,1,0:T(8,128)(2,1)} %bitcast.207), channel_id=1, source_target_pairs={{0,9},{1,10},{2,11},{3,8},{4,1},{5,2},{6,3},{7,0},{8,13},{9,14},{1... | collective-permute-start | bytes 1572872 | tf_op jit(solution)/shard_map/ppermute | solution.py:385
  115.1 58.9 %collective-permute-start.9 = (bf16[2,16,32,256]{3,2,1,0:T(8,128)(2,1)S(1)}, bf16[2,16,32,256]{3,2,1,0:T(8,128)(2,1)S(1)}, u32[]{:S(2)}, u32[]{:S(2)}) collective-permute-start(bf16[2,16,32,256]{3,2,1,0:T(8,128)(2,1)S(1)} %bitcast.249), channel_id=1, source_target_pairs={{0,10},{1,11},{2,8},{3,9},{4,2},{5,3},{6,0},{7,1},{8,14},{9,15},{1... | collective-permute-start | bytes 1572872 | tf_op jit(solution)/shard_map/ppermute | solution.py:385
  174.8 60.1 %collective-permute-start.13 = (bf16[2,16,32,256]{3,2,1,0:T(8,128)(2,1)}, bf16[2,16,32,256]{3,2,1,0:T(8,128)(2,1)S(1)}, u32[]{:S(2)}, u32[]{:S(2)}) collective-permute-start(bf16[2,16,32,256]{3,2,1,0:T(8,128)(2,1)} %bitcast.202), channel_id=1, source_target_pairs={{0,6},{1,7},{2,4},{3,5},{4,14},{5,15},{6,12},{7,13},{8,2},{9,3},{1... | collective-permute-start | bytes 1572872 | tf_op jit(solution)/shard_map/ppermute | solution.py:385
  176.6 60.3 %collective-permute-start.14 = (bf16[2,16,32,256]{3,2,1,0:T(8,128)(2,1)}, bf16[2,16,32,256]{3,2,1,0:T(8,128)(2,1)S(1)}, u32[]{:S(2)}, u32[]{:S(2)}) collective-permute-start(bf16[2,16,32,256]{3,2,1,0:T(8,128)(2,1)} %bitcast.201), channel_id=1, source_target_pairs={{0,7},{1,4},{2,5},{3,6},{4,15},{5,12},{6,13},{7,14},{8,3},{9,0},{1... | collective-permute-start | bytes 1572872 | tf_op jit(solution)/shard_map/ppermute | solution.py:385
  234.9 67.6 %collective-permute-start.34 = (bf16[2,16,32,256]{3,2,1,0:T(8,128)(2,1)}, bf16[2,16,32,256]{3,2,1,0:T(8,128)(2,1)S(1)}, u32[]{:S(2)}, u32[]{:S(2)}) collective-permute-start(bf16[2,16,32,256]{3,2,1,0:T(8,128)(2,1)} %bitcast.247), channel_id=1, source_target_pairs={{0,13},{1,14},{2,15},{3,12},{4,9},{5,10},{6,11},{7,8},{8,5},{9,6},... | collective-permute-start | bytes 1572872 | tf_op jit(solution)/shard_map/ppermute | solution.py:385
  236.9 70.9 %collective-permute-start.35 = (bf16[2,16,32,256]{3,2,1,0:T(8,128)(2,1)}, bf16[2,16,32,256]{3,2,1,0:T(8,128)(2,1)}, u32[]{:S(2)}, u32[]{:S(2)}) collective-permute-start(bf16[2,16,32,256]{3,2,1,0:T(8,128)(2,1)} %bitcast.244), channel_id=1, source_target_pairs={{0,14},{1,15},{2,12},{3,13},{4,10},{5,11},{6,8},{7,9},{8,6},{9,7},... | collective-permute-start | bytes 1572872 | tf_op jit(solution)/shard_map/ppermute | solution.py:385
  239.0 91.5 %collective-permute-start.36 = (bf16[2,16,32,256]{3,2,1,0:T(8,128)(2,1)}, bf16[2,16,32,256]{3,2,1,0:T(8,128)(2,1)}, u32[]{:S(2)}, u32[]{:S(2)}) collective-permute-start(bf16[2,16,32,256]{3,2,1,0:T(8,128)(2,1)} %bitcast.242), channel_id=1, source_target_pairs={{0,15},{1,12},{2,13},{3,14},{4,11},{5,8},{6,9},{7,10},{8,7},{9,4},... | collective-permute-start | bytes 1572872 | tf_op jit(solution)/shard_map/ppermute | solution.py:385
  240.8 110.3 %collective-permute-start.37 = (bf16[2,16,32,256]{3,2,1,0:T(8,128)(2,1)}, bf16[2,16,32,256]{3,2,1,0:T(8,128)(2,1)}, u32[]{:S(2)}, u32[]{:S(2)}) collective-permute-start(bf16[2,16,32,256]{3,2,1,0:T(8,128)(2,1)} %bitcast.240), channel_id=1, source_target_pairs={{0,8},{1,9},{2,10},{3,11},{4,0},{5,1},{6,2},{7,3},{8,12},{9,13},{1... | collective-permute-start | bytes 1572872 | tf_op jit(solution)/shard_map/ppermute | solution.py:385
  240.8 111.4 %collective-permute-start.38 = (bf16[2,16,32,256]{3,2,1,0:T(8,128)(2,1)}, bf16[2,16,32,256]{3,2,1,0:T(8,128)(2,1)}, u32[]{:S(2)}, u32[]{:S(2)}) collective-permute-start(bf16[2,16,32,256]{3,2,1,0:T(8,128)(2,1)} %bitcast.238), channel_id=1, source_target_pairs={{0,9},{1,10},{2,11},{3,8},{4,1},{5,2},{6,3},{7,0},{8,13},{9,14},{1... | collective-permute-start | bytes 1572872 | tf_op jit(solution)/shard_map/ppermute | solution.py:385
  302.6 84.5 %collective-permute-start.39 = (bf16[2,16,32,256]{3,2,1,0:T(8,128)(2,1)S(1)}, bf16[2,16,32,256]{3,2,1,0:T(8,128)(2,1)S(1)}, u32[]{:S(2)}, u32[]{:S(2)}) collective-permute-start(bf16[2,16,32,256]{3,2,1,0:T(8,128)(2,1)S(1)} %bitcast.243), channel_id=1, source_target_pairs={{0,10},{1,11},{2,8},{3,9},{4,2},{5,3},{6,0},{7,1},{8,14},{9,15},{1... | collective-permute-start | bytes 1572872 | tf_op jit(solution)/shard_map/ppermute | solution.py:385
  307.7 80.0 %collective-permute-start.40 = (bf16[2,16,32,256]{3,2,1,0:T(8,128)(2,1)S(1)}, bf16[2,16,32,256]{3,2,1,0:T(8,128)(2,1)S(1)}, u32[]{:S(2)}, u32[]{:S(2)}) collective-permute-start(bf16[2,16,32,256]{3,2,1,0:T(8,128)(2,1)S(1)} %bitcast.241), channel_id=1, source_target_pairs={{0,11},{1,8},{2,9},{3,10},{4,3},{5,0},{6,1},{7,2},{8,15},{9,12},{1... | collective-permute-start | bytes 1572872 | tf_op jit(solution)/shard_map/ppermute | solution.py:385
  330.6 60.1 %collective-permute-start.41 = (bf16[2,16,32,256]{3,2,1,0:T(8,128)(2,1)S(1)}, bf16[2,16,32,256]{3,2,1,0:T(8,128)(2,1)S(1)}, u32[]{:S(2)}, u32[]{:S(2)}) collective-permute-start(bf16[2,16,32,256]{3,2,1,0:T(8,128)(2,1)S(1)} %bitcast.239), channel_id=1, source_target_pairs={{0,4},{1,5},{2,6},{3,7},{4,12},{5,13},{6,14},{7,15},{8,0},{9,1},{1... | collective-permute-start | bytes 1572872 | tf_op jit(solution)/shard_map/ppermute | solution.py:385
  418.0 68.8 %collective-permute-start.63 = (bf16[2,24,16,256]{3,2,1,0:T(8,128)(2,1)}, bf16[2,24,16,256]{3,2,1,0:T(8,128)(2,1)S(1)}, u32[]{:S(2)}, u32[]{:S(2)}) collective-permute-start(bf16[2,24,16,256]{3,2,1,0:T(8,128)(2,1)} %get-tuple-element.102), channel_id=1, source_target_pairs={{0,3},{1,0},{2,1},{3,2},{4,7},{5,4},{6,5},{7,6},{8,11},{9,8},{10,9... | collective-permute-start | bytes 1179656 | tf_op jit(solution)/shard_map/ppermute | solution.py:385
  418.3 70.9 %collective-permute-start.64 = (bf16[2,24,16,256]{3,2,1,0:T(8,128)(2,1)}, bf16[2,24,16,256]{3,2,1,0:T(8,128)(2,1)S(1)}, u32[]{:S(2)}, u32[]{:S(2)}) collective-permute-start(bf16[2,24,16,256]{3,2,1,0:T(8,128)(2,1)} %get-tuple-element.103), channel_id=1, source_target_pairs={{0,13},{1,14},{2,15},{3,12},{4,9},{5,10},{6,11},{7,8},{8,5},{9,6},... | collective-permute-start | bytes 1179656 | tf_op jit(solution)/shard_map/ppermute | solution.py:385
  429.1 62.1 %collective-permute-start.65 = (bf16[2,24,16,256]{3,2,1,0:T(8,128)(2,1)}, bf16[2,24,16,256]{3,2,1,0:T(8,128)(2,1)S(1)}, u32[]{:S(2)}, u32[]{:S(2)}) collective-permute-start(bf16[2,24,16,256]{3,2,1,0:T(8,128)(2,1)} %get-tuple-element.104), channel_id=1, source_target_pairs={{0,14},{1,15},{2,12},{3,13},{4,10},{5,11},{6,8},{7,9},{8,6},{9,7},... | collective-permute-start | bytes 1179656 | tf_op jit(solution)/shard_map/ppermute | solution.py:385
  430.1 63.3 %collective-permute-start.66 = (bf16[2,24,16,256]{3,2,1,0:T(8,128)(2,1)}, bf16[2,24,16,256]{3,2,1,0:T(8,128)(2,1)S(1)}, u32[]{:S(2)}, u32[]{:S(2)}) collective-permute-start(bf16[2,24,16,256]{3,2,1,0:T(8,128)(2,1)} %get-tuple-element.105), channel_id=1, source_target_pairs={{0,15},{1,12},{2,13},{3,14},{4,11},{5,8},{6,9},{7,10},{8,7},{9,4},... | collective-permute-start | bytes 1179656 | tf_op jit(solution)/shard_map/ppermute | solution.py:385
  449.5 73.7 %collective-permute-start.67 = (bf16[2,24,16,256]{3,2,1,0:T(8,128)(2,1)}, bf16[2,24,16,256]{3,2,1,0:T(8,128)(2,1)S(1)}, u32[]{:S(2)}, u32[]{:S(2)}) collective-permute-start(bf16[2,24,16,256]{3,2,1,0:T(8,128)(2,1)} %get-tuple-element.106), channel_id=1, source_target_pairs={{0,8},{1,9},{2,10},{3,11},{4,0},{5,1},{6,2},{7,3},{8,12},{9,13},{1... | collective-permute-start | bytes 1179656 | tf_op jit(solution)/shard_map/ppermute | solution.py:385
  491.2 65.7 %collective-permute-start.70 = (bf16[2,24,16,256]{3,2,1,0:T(8,128)(2,1)}, bf16[2,24,16,256]{3,2,1,0:T(8,128)(2,1)S(1)}, u32[]{:S(2)}, u32[]{:S(2)}) collective-permute-start(bf16[2,24,16,256]{3,2,1,0:T(8,128)(2,1)} %get-tuple-element.109), channel_id=1, source_target_pairs={{0,11},{1,8},{2,9},{3,10},{4,3},{5,0},{6,1},{7,2},{8,15},{9,12},{1... | collective-permute-start | bytes 1179656 | tf_op jit(solution)/shard_map/ppermute | solution.py:385
  493.4 66.0 %collective-permute-start.71 = (bf16[2,24,16,256]{3,2,1,0:T(8,128)(2,1)}, bf16[2,24,16,256]{3,2,1,0:T(8,128)(2,1)S(1)}, u32[]{:S(2)}, u32[]{:S(2)}) collective-permute-start(bf16[2,24,16,256]{3,2,1,0:T(8,128)(2,1)} %get-tuple-element.110), channel_id=1, source_target_pairs={{0,4},{1,5},{2,6},{3,7},{4,12},{5,13},{6,14},{7,15},{8,0},{9,1},{1... | collective-permute-start | bytes 1179656 | tf_op jit(solution)/shard_map/ppermute | solution.py:385
  562.0 59.9 %collective-permute-start.48 = (bf16[2,32,16,256]{3,2,1,0:T(8,128)(2,1)}, bf16[2,32,16,256]{3,2,1,0:T(8,128)(2,1)S(1)}, u32[]{:S(2)}, u32[]{:S(2)}) collective-permute-start(bf16[2,32,16,256]{3,2,1,0:T(8,128)(2,1)} %get-tuple-element.84), channel_id=1, source_target_pairs={{0,3},{1,0},{2,1},{3,2},{4,7},{5,4},{6,5},{7,6},{8,11},{9,8},{10,9... | collective-permute-start | bytes 1572872 | tf_op jit(solution)/shard_map/ppermute | solution.py:385
  571.9 81.3 %collective-permute-start.50 = (bf16[2,32,16,256]{3,2,1,0:T(8,128)(2,1)}, bf16[2,32,16,256]{3,2,1,0:T(8,128)(2,1)S(1)}, u32[]{:S(2)}, u32[]{:S(2)}) collective-permute-start(bf16[2,32,16,256]{3,2,1,0:T(8,128)(2,1)} %get-tuple-element.86), channel_id=1, source_target_pairs={{0,14},{1,15},{2,12},{3,13},{4,10},{5,11},{6,8},{7,9},{8,6},{9,7},... | collective-permute-start | bytes 1572872 | tf_op jit(solution)/shard_map/ppermute | solution.py:385
  575.0 101.4 %collective-permute-start.51 = (bf16[2,32,16,256]{3,2,1,0:T(8,128)(2,1)}, bf16[2,32,16,256]{3,2,1,0:T(8,128)(2,1)S(1)}, u32[]{:S(2)}, u32[]{:S(2)}) collective-permute-start(bf16[2,32,16,256]{3,2,1,0:T(8,128)(2,1)} %get-tuple-element.87), channel_id=1, source_target_pairs={{0,15},{1,12},{2,13},{3,14},{4,11},{5,8},{6,9},{7,10},{8,7},{9,4},... | collective-permute-start | bytes 1572872 | tf_op jit(solution)/shard_map/ppermute | solution.py:385
  607.4 89.8 %collective-permute-start.52 = (bf16[2,32,16,256]{3,2,1,0:T(8,128)(2,1)}, bf16[2,32,16,256]{3,2,1,0:T(8,128)(2,1)S(1)}, u32[]{:S(2)}, u32[]{:S(2)}) collective-permute-start(bf16[2,32,16,256]{3,2,1,0:T(8,128)(2,1)} %get-tuple-element.88), channel_id=1, source_target_pairs={{0,8},{1,9},{2,10},{3,11},{4,0},{5,1},{6,2},{7,3},{8,12},{9,13},{1... | collective-permute-start | bytes 1572872 | tf_op jit(solution)/shard_map/ppermute | solution.py:385
  621.9 76.0 %collective-permute-start.53 = (bf16[2,32,16,256]{3,2,1,0:T(8,128)(2,1)}, bf16[2,32,16,256]{3,2,1,0:T(8,128)(2,1)S(1)}, u32[]{:S(2)}, u32[]{:S(2)}) collective-permute-start(bf16[2,32,16,256]{3,2,1,0:T(8,128)(2,1)} %get-tuple-element.89), channel_id=1, source_target_pairs={{0,9},{1,10},{2,11},{3,8},{4,1},{5,2},{6,3},{7,0},{8,13},{9,14},{1... | collective-permute-start | bytes 1572872 | tf_op jit(solution)/shard_map/ppermute | solution.py:385
  621.9 77.0 %collective-permute-start.54 = (bf16[2,32,16,256]{3,2,1,0:T(8,128)(2,1)}, bf16[2,32,16,256]{3,2,1,0:T(8,128)(2,1)S(1)}, u32[]{:S(2)}, u32[]{:S(2)}) collective-permute-start(bf16[2,32,16,256]{3,2,1,0:T(8,128)(2,1)} %get-tuple-element.90), channel_id=1, source_target_pairs={{0,10},{1,11},{2,8},{3,9},{4,2},{5,3},{6,0},{7,1},{8,14},{9,15},{1... | collective-permute-start | bytes 1572872 | tf_op jit(solution)/shard_map/ppermute | solution.py:385
  699.8 75.9 %collective-permute-start.25 = (bf16[2,8,16,256]{3,2,1,0:T(8,128)(2,1)}, bf16[2,8,16,256]{3,2,1,0:T(8,128)(2,1)S(1)}, u32[]{:S(2)}, u32[]{:S(2)}) collective-permute-start(bf16[2,8,16,256]{3,2,1,0:T(8,128)(2,1)} %get-tuple-element.74), channel_id=1, source_target_pairs={{0,11},{1,8},{2,9},{3,10},{4,3},{5,0},{6,1},{7,2},{8,15},{9,12},{1... | collective-permute-start | bytes 393224 | tf_op jit(solution)/shard_map/ppermute | solution.py:385
  710.0 65.7 %collective-permute-start.26 = (bf16[2,8,16,256]{3,2,1,0:T(8,128)(2,1)}, bf16[2,8,16,256]{3,2,1,0:T(8,128)(2,1)S(1)}, u32[]{:S(2)}, u32[]{:S(2)}) collective-permute-start(bf16[2,8,16,256]{3,2,1,0:T(8,128)(2,1)} %get-tuple-element.75), channel_id=1, source_target_pairs={{0,4},{1,5},{2,6},{3,7},{4,12},{5,13},{6,14},{7,15},{8,0},{9,1},{1... | collective-permute-start | bytes 393224 | tf_op jit(solution)/shard_map/ppermute | solution.py:385
  (136 other events, 7299.0 us)

commit v5 on v4

--- a/solution.py
+++ b/solution.py
@@ -89,49 +89,60 @@
 def partners(index, rounds, group):
     inner = group // len(rounds[0][0])
     quarter, place = index // inner, index % inner
+    kind = jnp.uint32 if index.dtype == jnp.uint32 else jnp.int32
     moved, turned = {}, {}
     for move, turn in rounds:
         if move not in moved:
             steps = [
-                jnp.where(quarter == q, jnp.uint32(m * inner), jnp.uint32(0))
-                for q, m in enumerate(move)
-                if m
+                jnp.where(quarter == q, kind(m * inner), kind(0)) for q, m in enumerate(move) if m
             ]
-            moved[move] = functools.reduce(jnp.add, steps) if steps else jnp.uint32(0)
+            moved[move] = functools.reduce(jnp.add, steps) if steps else kind(0)
         if turn not in turned:
-            turned[turn] = (place + jnp.uint32(turn)) % inner
+            turned[turn] = (place + kind(turn)) % inner
     return [moved[move] + turned[turn] for move, turn in rounds]
 
 
-def first_block_kernel(index, piece, out, turned):
-    _, rows, chunk, width = piece.shape
-    for c in range(2):
-        for h in range(width // 128):
-            lanes = slice(h * 128, (h + 1) * 128)
-            for a in range(rows):
-                turned[c, h, pl.ds(a, chunk, stride=rows), :] = piece[c, a, :, lanes].astype(
-                    jnp.float32
+def first_block_kernel(move_turn, group, stem, out, held, turned, sems):
+    local_a, width = stem.shape[1], stem.shape[3]
+    chunk = out.shape[1]
+    (target,) = partners(lax.axis_index("inter"), [move_turn], group)
+    columns = pl.ds(pl.multiple_of(target * (stem.shape[2] // group), chunk), chunk)
+    copies = []
+    for i in range(local_a // ROWS):
+        rows = slice(i * ROWS, (i + 1) * ROWS)
+        copies.append(
+            pltpu.make_async_copy(stem.at[:, rows, columns], held.at[:, rows], sems.at[i])
+        )
+        copies[-1].start()
+    for i, copy in enumerate(copies):
+        copy.wait()
+        for c in range(2):
+            for h in range(width // 128):
+                lanes = slice(h * 128, (h + 1) * 128)
+                for a in range(ROWS):
+                    turned[c, h, pl.ds(a, chunk, stride=ROWS), :] = held[
+                        c, i * ROWS + a, :, lanes
+                    ].astype(jnp.float32)
+                out[c, :, i * ROWS : (i + 1) * ROWS, lanes] = (
+                    turned[c, h].reshape(chunk, ROWS, 128).astype(jnp.bfloat16)
                 )
-            out[c, :, :, lanes] = (
-                turned[c, h].reshape(chunk, rows, 128).astype(jnp.bfloat16)
-            )
-
-
-def first_block(stem, index, chunk):
+
+
+def first_block(stem, move_turn, group, chunk):
     _, local_a, _, width = stem.shape
     return pl.pallas_call(
-        first_block_kernel,
-        grid_spec=pltpu.PrefetchScalarGridSpec(
-            num_scalar_prefetch=1,
-            grid=(local_a // ROWS,),
-            in_specs=[pl.BlockSpec((2, ROWS, chunk, width), lambda a, index: (0, a, index[0], 0))],
-            out_specs=pl.BlockSpec((2, chunk, ROWS, width), lambda a, index: (0, 0, a, 0)),
-            scratch_shapes=[pltpu.VMEM((2, width // 128, chunk * ROWS, 128), jnp.float32)],
-        ),
-        out_shape=pltpu.HBM((2, chunk, local_a, width), jnp.bfloat16),
+        functools.partial(first_block_kernel, move_turn, group),
+        in_specs=[pl.BlockSpec(memory_space=pl.ANY)],
+        out_specs=pl.BlockSpec(memory_space=pltpu.VMEM),
+        out_shape=pltpu.VMEM((2, chunk, local_a, width), jnp.bfloat16),
+        scratch_shapes=[
+            pltpu.VMEM((2, local_a, chunk, width), jnp.bfloat16),
+            pltpu.VMEM((2, width // 128, chunk * ROWS, 128), jnp.float32),
+            pltpu.SemaphoreType.DMA((local_a // ROWS,)),
+        ],
         compiler_params=pltpu.CompilerParams(vmem_limit_bytes=4 << 20),
         name="first_block",
-    )(index.astype(jnp.int32).reshape(1), stem)
+    )(*placed([stem], pltpu.HBM))
 
 
 def front_kernel(group, splits, *refs):
@@ -392,7 +403,7 @@
             start = target[k] * jnp.uint32(B_CHUNKS) + jnp.uint32(j)
             ahead = j == 0 and k == 1
             if ahead:
-                block = first_block(stem, start, chunk)
+                block = first_block(stem, rounds[k], group, chunk)
             else:
                 block = lax.dynamic_slice(
                     stem,

time: 787 us -> 782 us (level)
    unnamed x188 -> x196, local copies, waits for them, and re-layouts: 14.3 us -> 6.26 us
where the time goes in v5:
time: 782 us; the launch traced here: 775 us
  starting transfers between devices  414 us (53%)
  local copies, waits for them, and re-layouts  132 us (17%)
  waiting for transfers between devices  120 us (15%)
  Pallas kernels  100 us (13%)
  other arithmetic  7.83 us (1%)
    ppermute x75, starting transfers between devices, send(): return lax.ppermute(block, 'inter', pairs[k])  414 us
    ppermute x75, waiting for transfers between devices, send(): return lax.ppermute(block, 'inter', pairs[k])  120 us
    pallas_call x2, Pallas kernels, front(): pl.pallas_call(functools.partial(front_kernel, group, splits), grid=(chun...  62.8 us
    dynamic_slice x33, local copies, waits for them, and re-layouts, on_device(): lax.dynamic_slice(stem, (zero, zero, start * jnp.uint32(chunk), zero), (2...  49.7 us
    gather x4, local copies, waits for them, and re-layouts, on_device(): one = one[:, where_from][:, :, :, where_to].reshape(2, size_a, size_a)  23 us
    pallas_call x2, Pallas kernels, last_b(): pl.pallas_call(functools.partial(last_kernel, n, len(bases), start, near)...  20.6 us
    scatter x1, local copies, waits for them, and re-layouts, on_device(): permuted = jnp.zeros_like(branch_two).at[:, mode_order, :].set(branch_two)  18.2 us
  transfers between devices with their start and end apart: 75, of which 12 were waited for; matrix products, arithmetic and copies ran while one was open for 17% of the time, Pallas kernels for 12%

profile of v5, /device:TPU:1, one launch (start us, length us, event | category | flops | bytes accessed | tf_op | source)
XLA Modules:
  0.0 775.5 jit_solution(7357391337664839911)
XLA Ops:
  31.0 7.5 constant_dynamic-slice_fusion
  46.4 44.6 %collective-permute-start.7 = (bf16[2,16,32,256]{3,2,1,0:T(8,128)(2,1)}, bf16[2,16,32,256]{3,2,1,0:T(8,128)(2,1)}, u32[]{:S(2)}, u32[]{:S(2)}) collective-permute-start(bf16[2,16,32,256]{3,2,1,0:T(8,128)(2,1)} %bitcast.207), channel_id=1, source_target_pairs={{0,8},{1,9},{2,10},{3,11},{4,0},{5,1},{6,2},{7,3},{8,12},{9,13},{1... | collective-permute-start | bytes 1572872 | tf_op jit(solution)/shard_map/ppermute | solution.py:396
  110.5 12.9 %collective-permute-start.9 = (bf16[2,16,32,256]{3,2,1,0:T(8,128)(2,1)}, bf16[2,16,32,256]{3,2,1,0:T(8,128)(2,1)S(1)}, u32[]{:S(2)}, u32[]{:S(2)}) collective-permute-start(bf16[2,16,32,256]{3,2,1,0:T(8,128)(2,1)} %bitcast.205), channel_id=1, source_target_pairs={{0,10},{1,11},{2,8},{3,9},{4,2},{5,3},{6,0},{7,1},{8,14},{9,15},{1... | collective-permute-start | bytes 1572872 | tf_op jit(solution)/shard_map/ppermute | solution.py:396
  123.4 22.0 %collective-permute-start.10 = (bf16[2,16,32,256]{3,2,1,0:T(8,128)(2,1)}, bf16[2,16,32,256]{3,2,1,0:T(8,128)(2,1)S(1)}, u32[]{:S(2)}, u32[]{:S(2)}) collective-permute-start(bf16[2,16,32,256]{3,2,1,0:T(8,128)(2,1)} %bitcast.204), channel_id=1, source_target_pairs={{0,11},{1,8},{2,9},{3,10},{4,3},{5,0},{6,1},{7,2},{8,15},{9,12},{1... | collective-permute-start | bytes 1572872 | tf_op jit(solution)/shard_map/ppermute | solution.py:396
  145.4 19.8 %collective-permute-start.43 = (bf16[2,16,32,256]{3,2,1,0:T(8,128)(2,1)S(1)}, bf16[2,16,32,256]{3,2,1,0:T(8,128)(2,1)S(1)}, u32[]{:S(2)}, u32[]{:S(2)}) collective-permute-start(bf16[2,16,32,256]{3,2,1,0:T(8,128)(2,1)S(1)} %bitcast.244), channel_id=1, source_target_pairs={{0,6},{1,7},{2,4},{3,5},{4,14},{5,15},{6,12},{7,13},{8,2},{9,3},{1... | collective-permute-start | bytes 1572872 | tf_op jit(solution)/shard_map/ppermute | solution.py:396
  178.4 11.6 %collective-permute-done.11.refs_12_ = bf16[2,16,32,256]{3,2,1,0:T(8,128)(2,1)S(1)} collective-permute-done((bf16[2,16,32,256]{3,2,1,0:T(8,128)(2,1)}, bf16[2,16,32,256]{3,2,1,0:T(8,128)(2,1)S(1)}, u32[]{:S(2)}, u32[]{:S(2)}) %collective-permute-start.11) | collective-permute-done | bytes 524320 | tf_op jit(solution)/shard_map/ppermute | solution.py:396
  190.7 8.4 %collective-permute-done.12.refs_13_ = bf16[2,16,32,256]{3,2,1,0:T(8,128)(2,1)S(1)} collective-permute-done((bf16[2,16,32,256]{3,2,1,0:T(8,128)(2,1)S(1)}, bf16[2,16,32,256]{3,2,1,0:T(8,128)(2,1)S(1)}, u32[]{:S(2)}, u32[]{:S(2)}) %collective-permute-start.12) | collective-permute-done | bytes 524320 | tf_op jit(solution)/shard_map/ppermute | solution.py:396
  210.2 18.2 %scatter_fusion = bf16[2,256,256]{2,0,1:T(2,128)(2,1)S(1)} fusion(bf16[2,256,256]{2,0,1:T(2,128)(2,1)S(1)} %broadcast_in_dim.4, s32[256]{0:T(256)S(1)} %compare_select_fusion, bf16[256,2,256]{2,1,0:T(2,128)(2,1)} %copy.110), kind=kCustom, calls=%fused_computation.4 | custom fusion | bytes 787456 | tf_op jit(solution)/shard_map/scatter | solution.py:430
  256.1 5.9 reshape.543
  278.0 7.1 copy.109
  285.0 6.8 reshape.544
  302.4 22.7 %collective-permute-start.40 = (bf16[2,16,32,256]{3,2,1,0:T(8,128)(2,1)S(1)}, bf16[2,16,32,256]{3,2,1,0:T(8,128)(2,1)S(1)}, u32[]{:S(2)}, u32[]{:S(2)}) collective-permute-start(bf16[2,16,32,256]{3,2,1,0:T(8,128)(2,1)S(1)} %bitcast.240), channel_id=1, source_target_pairs={{0,11},{1,8},{2,9},{3,10},{4,3},{5,0},{6,1},{7,2},{8,15},{9,12},{1... | collective-permute-start | bytes 1572872 | tf_op jit(solution)/shard_map/ppermute | solution.py:396
  325.2 20.5 %collective-permute-start.41 = (bf16[2,16,32,256]{3,2,1,0:T(8,128)(2,1)S(1)}, bf16[2,16,32,256]{3,2,1,0:T(8,128)(2,1)S(1)}, u32[]{:S(2)}, u32[]{:S(2)}) collective-permute-start(bf16[2,16,32,256]{3,2,1,0:T(8,128)(2,1)S(1)} %bitcast.238), channel_id=1, source_target_pairs={{0,4},{1,5},{2,6},{3,7},{4,12},{5,13},{6,14},{7,15},{8,0},{9,1},{1... | collective-permute-start | bytes 1572872 | tf_op jit(solution)/shard_map/ppermute | solution.py:396
  349.7 31.8 %front.2 = (bf16[2,24,16,256]{3,2,1,0:T(8,128)(2,1)}, bf16[2,8,16,256]{3,2,1,0:T(8,128)(2,1)}, bf16[2,24,16,256]{3,2,1,0:T(8,128)(2,1)}, bf16[2,8,16,256]{3,2,1,...) custom-call(bf16[2,16,32,256]{3,2,1,0:T(8,128)(2,1)S(1)} %bitcast.21, ...), custom_call_target="tpu_custom_call" | custom-call | tf_op jit(solution)/shard_map/front/pallas_call | solution.py:193
  396.1 13.0 %collective-permute-start.24 = (bf16[2,8,16,256]{3,2,1,0:T(8,128)(2,1)}, bf16[2,8,16,256]{3,2,1,0:T(8,128)(2,1)S(1)}, u32[]{:S(2)}, u32[]{:S(2)}) collective-permute-start(bf16[2,8,16,256]{3,2,1,0:T(8,128)(2,1)} %get-tuple-element.73), channel_id=1, source_target_pairs={{0,10},{1,11},{2,8},{3,9},{4,2},{5,3},{6,0},{7,1},{8,14},{9,15},{1... | collective-permute-start | bytes 393224 | tf_op jit(solution)/shard_map/ppermute | solution.py:396
  415.3 8.2 %collective-permute-done.60.refs_1_ = bf16[2,24,16,256]{3,2,1,0:T(8,128)(2,1)S(1)} collective-permute-done((bf16[2,24,16,256]{3,2,1,0:T(8,128)(2,1)}, bf16[2,24,16,256]{3,2,1,0:T(8,128)(2,1)S(1)}, u32[]{:S(2)}, u32[]{:S(2)}) %collective-permute-start.60) | collective-permute-done | bytes 393248 | tf_op jit(solution)/shard_map/ppermute | solution.py:396
  428.0 15.9 %collective-permute-done.62.refs_3_ = bf16[2,24,16,256]{3,2,1,0:T(8,128)(2,1)S(1)} collective-permute-done((bf16[2,24,16,256]{3,2,1,0:T(8,128)(2,1)}, bf16[2,24,16,256]{3,2,1,0:T(8,128)(2,1)S(1)}, u32[]{:S(2)}, u32[]{:S(2)}) %collective-permute-start.62) | collective-permute-done | bytes 393248 | tf_op jit(solution)/shard_map/ppermute | solution.py:396
  443.9 37.4 %collective-permute-start.67 = (bf16[2,24,16,256]{3,2,1,0:T(8,128)(2,1)}, bf16[2,24,16,256]{3,2,1,0:T(8,128)(2,1)S(1)}, u32[]{:S(2)}, u32[]{:S(2)}) collective-permute-start(bf16[2,24,16,256]{3,2,1,0:T(8,128)(2,1)} %get-tuple-element.106), channel_id=1, source_target_pairs={{0,8},{1,9},{2,10},{3,11},{4,0},{5,1},{6,2},{7,3},{8,12},{9,13},{1... | collective-permute-start | bytes 1179656 | tf_op jit(solution)/shard_map/ppermute | solution.py:396
  487.9 29.7 %collective-permute-start.71 = (bf16[2,24,16,256]{3,2,1,0:T(8,128)(2,1)}, bf16[2,24,16,256]{3,2,1,0:T(8,128)(2,1)S(1)}, u32[]{:S(2)}, u32[]{:S(2)}) collective-permute-start(bf16[2,24,16,256]{3,2,1,0:T(8,128)(2,1)} %get-tuple-element.110), channel_id=1, source_target_pairs={{0,4},{1,5},{2,6},{3,7},{4,12},{5,13},{6,14},{7,15},{8,0},{9,1},{1... | collective-permute-start | bytes 1179656 | tf_op jit(solution)/shard_map/ppermute | solution.py:396
  520.2 31.1 %front.3 = (bf16[2,32,16,256]{3,2,1,0:T(8,128)(2,1)}, bf16[2,32,16,256]{3,2,1,0:T(8,128)(2,1)}, bf16[2,32,16,256]{3,2,1,0:T(8,128)(2,1)}, bf16[2,32,16,256]{3,2,...) custom-call(bf16[2,16,32,256]{3,2,1,0:T(8,128)(2,1)S(1)} %bitcast.22, ...), custom_call_target="tpu_custom_call" | custom-call | tf_op jit(solution)/shard_map/front/pallas_call | solution.py:193
  558.5 8.0 %collective-permute-done.45.refs_1_ = bf16[2,32,16,256]{3,2,1,0:T(8,128)(2,1)S(1)} collective-permute-done((bf16[2,32,16,256]{3,2,1,0:T(8,128)(2,1)}, bf16[2,32,16,256]{3,2,1,0:T(8,128)(2,1)S(1)}, u32[]{:S(2)}, u32[]{:S(2)}) %collective-permute-start.45) | collective-permute-done | bytes 524320 | tf_op jit(solution)/shard_map/ppermute | solution.py:396
  572.9 27.3 %collective-permute-done.47.refs_3_ = bf16[2,32,16,256]{3,2,1,0:T(8,128)(2,1)S(1)} collective-permute-done((bf16[2,32,16,256]{3,2,1,0:T(8,128)(2,1)}, bf16[2,32,16,256]{3,2,1,0:T(8,128)(2,1)S(1)}, u32[]{:S(2)}, u32[]{:S(2)}) %collective-permute-start.47) | collective-permute-done | bytes 524320 | tf_op jit(solution)/shard_map/ppermute | solution.py:396
  600.1 16.3 %collective-permute-start.52 = (bf16[2,32,16,256]{3,2,1,0:T(8,128)(2,1)}, bf16[2,32,16,256]{3,2,1,0:T(8,128)(2,1)S(1)}, u32[]{:S(2)}, u32[]{:S(2)}) collective-permute-start(bf16[2,32,16,256]{3,2,1,0:T(8,128)(2,1)} %get-tuple-element.88), channel_id=1, source_target_pairs={{0,8},{1,9},{2,10},{3,11},{4,0},{5,1},{6,2},{7,3},{8,12},{9,13},{1... | collective-permute-start | bytes 1572872 | tf_op jit(solution)/shard_map/ppermute | solution.py:396
  616.5 31.2 %collective-permute-start.54 = (bf16[2,32,16,256]{3,2,1,0:T(8,128)(2,1)}, bf16[2,32,16,256]{3,2,1,0:T(8,128)(2,1)S(1)}, u32[]{:S(2)}, u32[]{:S(2)}) collective-permute-start(bf16[2,32,16,256]{3,2,1,0:T(8,128)(2,1)} %get-tuple-element.90), channel_id=1, source_target_pairs={{0,10},{1,11},{2,8},{3,9},{4,2},{5,3},{6,0},{7,1},{8,14},{9,15},{1... | collective-permute-start | bytes 1572872 | tf_op jit(solution)/shard_map/ppermute | solution.py:396
  647.8 23.0 %collective-permute-start.55 = (bf16[2,32,16,256]{3,2,1,0:T(8,128)(2,1)}, bf16[2,32,16,256]{3,2,1,0:T(8,128)(2,1)S(1)}, u32[]{:S(2)}, u32[]{:S(2)}) collective-permute-start(bf16[2,32,16,256]{3,2,1,0:T(8,128)(2,1)} %get-tuple-element.91), channel_id=1, source_target_pairs={{0,11},{1,8},{2,9},{3,10},{4,3},{5,0},{6,1},{7,2},{8,15},{9,12},{1... | collective-permute-start | bytes 1572872 | tf_op jit(solution)/shard_map/ppermute | solution.py:396
  670.8 21.0 %collective-permute-start.56 = (bf16[2,32,16,256]{3,2,1,0:T(8,128)(2,1)}, bf16[2,32,16,256]{3,2,1,0:T(8,128)(2,1)S(1)}, u32[]{:S(2)}, u32[]{:S(2)}) collective-permute-start(bf16[2,32,16,256]{3,2,1,0:T(8,128)(2,1)} %get-tuple-element.92), channel_id=1, source_target_pairs={{0,4},{1,5},{2,6},{3,7},{4,12},{5,13},{6,14},{7,15},{8,0},{9,1},{1... | collective-permute-start | bytes 1572872 | tf_op jit(solution)/shard_map/ppermute | solution.py:396
  697.2 7.3 collective-permute-done.56.refs_12_
  705.6 9.1 %collective-permute-done.57.refs_13_ = bf16[2,32,16,256]{3,2,1,0:T(8,128)(2,1)S(1)} collective-permute-done((bf16[2,32,16,256]{3,2,1,0:T(8,128)(2,1)}, bf16[2,32,16,256]{3,2,1,0:T(8,128)(2,1)S(1)}, u32[]{:S(2)}, u32[]{:S(2)}) %collective-permute-start.57) | collective-permute-done | bytes 524320 | tf_op jit(solution)/shard_map/ppermute | solution.py:396
  718.0 9.3 %collective-permute-done.58.refs_14_ = bf16[2,32,16,256]{3,2,1,0:T(8,128)(2,1)S(1)} collective-permute-done((bf16[2,32,16,256]{3,2,1,0:T(8,128)(2,1)}, bf16[2,32,16,256]{3,2,1,0:T(8,128)(2,1)S(1)}, u32[]{:S(2)}, u32[]{:S(2)}) %collective-permute-start.58) | collective-permute-done | bytes 524320 | tf_op jit(solution)/shard_map/ppermute | solution.py:396
  729.0 9.4 %collective-permute-done.59.refs_15_ = bf16[2,32,16,256]{3,2,1,0:T(8,128)(2,1)S(1)} collective-permute-done((bf16[2,32,16,256]{3,2,1,0:T(8,128)(2,1)}, bf16[2,32,16,256]{3,2,1,0:T(8,128)(2,1)S(1)}, u32[]{:S(2)}, u32[]{:S(2)}) %collective-permute-start.59) | collective-permute-done | bytes 524320 | tf_op jit(solution)/shard_map/ppermute | solution.py:396
  739.8 14.7 %partial.1 = (f32[8,1024,256]{2,1,0:T(8,128)S(1)}, f32[8,1024,256]{2,1,0:T(8,128)S(1)}, f32[8,1024,256]{2,1,0:T(8,128)S(1)}, f32[8,1024,256]{2,1,0:T(8,128)S(1)}) custom-call(bf16[2,32,16,256]{3,2,1,0:T(8,128)(2,1)} %get-tuple-element.80.refs_0_, bf16[2,32,16,256]{3,2,1,0:T(8,128)(2,1)} %copy-done.63, bf16[2,32,16,256]{3,2,1,0:T(8,128)(2,1)} %copy-done.64, ...), custom_call_target="tpu_custom_call" | custom-call | tf_op jit(solution)/shard_map/partial/pallas_call | solution.py:327
  754.5 15.8 %last.2.refs_18_ = f32[32,2048,128]{2,1,0:T(8,128)} custom-call(bf16[2,24,16,256]{3,2,1,0:T(8,128)(2,1)} %get-tuple-element.98.refs_0_, bf16[2,24,16,256]{3,2,1,0:T(8,128)(2,1)} %copy-done.80, bf16[2,24,16,256]{3,2,1,0:T(8,128)(2,1)} %copy-done.81, bf16[2,24,16,256]{3,2,1,0:T(8,128)(2,1)} %copy-done.82, bf16[2,24,16,256]{3,2,1,0:T(8,128)(2,1)} %copy-done.83, ...), custom_call_target="tpu_custom_call" | custom-call | tf_op jit(solution)/shard_map/last/pallas_call | solution.py:344
  (390 shorter events, 206.7 us)
Async XLA Ops:
  18.0 73.0 %collective-permute-start.3 = (bf16[2,16,32,256]{3,2,1,0:T(8,128)(2,1)}, bf16[2,16,32,256]{3,2,1,0:T(8,128)(2,1)}, u32[]{:S(2)}, u32[]{:S(2)}) collective-permute-start(bf16[2,16,32,256]{3,2,1,0:T(8,128)(2,1)} %bitcast.211), channel_id=1, source_target_pairs={{0,3},{1,0},{2,1},{3,2},{4,7},{5,4},{6,5},{7,6},{8,11},{9,8},{10,9... | collective-permute-start | bytes 1572872 | tf_op jit(solution)/shard_map/ppermute | solution.py:396
  38.5 71.2 %collective-permute-start.4 = (bf16[2,16,32,256]{3,2,1,0:T(8,128)(2,1)}, bf16[2,16,32,256]{3,2,1,0:T(8,128)(2,1)S(1)}, u32[]{:S(2)}, u32[]{:S(2)}) collective-permute-start(bf16[2,16,32,256]{3,2,1,0:T(8,128)(2,1)} %bitcast.210), channel_id=1, source_target_pairs={{0,13},{1,14},{2,15},{3,12},{4,9},{5,10},{6,11},{7,8},{8,5},{9,6},... | collective-permute-start | bytes 1572872 | tf_op jit(solution)/shard_map/ppermute | solution.py:396
  43.1 80.3 %collective-permute-start.5 = (bf16[2,16,32,256]{3,2,1,0:T(8,128)(2,1)}, bf16[2,16,32,256]{3,2,1,0:T(8,128)(2,1)S(1)}, u32[]{:S(2)}, u32[]{:S(2)}) collective-permute-start(bf16[2,16,32,256]{3,2,1,0:T(8,128)(2,1)} %bitcast.209), channel_id=1, source_target_pairs={{0,14},{1,15},{2,12},{3,13},{4,10},{5,11},{6,8},{7,9},{8,6},{9,7},... | collective-permute-start | bytes 1572872 | tf_op jit(solution)/shard_map/ppermute | solution.py:396
  44.1 101.3 %collective-permute-start.6 = (bf16[2,16,32,256]{3,2,1,0:T(8,128)(2,1)}, bf16[2,16,32,256]{3,2,1,0:T(8,128)(2,1)}, u32[]{:S(2)}, u32[]{:S(2)}) collective-permute-start(bf16[2,16,32,256]{3,2,1,0:T(8,128)(2,1)} %bitcast.208), channel_id=1, source_target_pairs={{0,15},{1,12},{2,13},{3,14},{4,11},{5,8},{6,9},{7,10},{8,7},{9,4},... | collective-permute-start | bytes 1572872 | tf_op jit(solution)/shard_map/ppermute | solution.py:396
  46.4 118.8 %collective-permute-start.7 = (bf16[2,16,32,256]{3,2,1,0:T(8,128)(2,1)}, bf16[2,16,32,256]{3,2,1,0:T(8,128)(2,1)}, u32[]{:S(2)}, u32[]{:S(2)}) collective-permute-start(bf16[2,16,32,256]{3,2,1,0:T(8,128)(2,1)} %bitcast.207), channel_id=1, source_target_pairs={{0,8},{1,9},{2,10},{3,11},{4,0},{5,1},{6,2},{7,3},{8,12},{9,13},{1... | collective-permute-start | bytes 1572872 | tf_op jit(solution)/shard_map/ppermute | solution.py:396
  91.0 74.3 %collective-permute-start.8 = (bf16[2,16,32,256]{3,2,1,0:T(8,128)(2,1)}, bf16[2,16,32,256]{3,2,1,0:T(8,128)(2,1)}, u32[]{:S(2)}, u32[]{:S(2)}) collective-permute-start(bf16[2,16,32,256]{3,2,1,0:T(8,128)(2,1)} %bitcast.206), channel_id=1, source_target_pairs={{0,9},{1,10},{2,11},{3,8},{4,1},{5,2},{6,3},{7,0},{8,13},{9,14},{1... | collective-permute-start | bytes 1572872 | tf_op jit(solution)/shard_map/ppermute | solution.py:396
  169.6 60.0 %collective-permute-start.13 = (bf16[2,16,32,256]{3,2,1,0:T(8,128)(2,1)}, bf16[2,16,32,256]{3,2,1,0:T(8,128)(2,1)S(1)}, u32[]{:S(2)}, u32[]{:S(2)}) collective-permute-start(bf16[2,16,32,256]{3,2,1,0:T(8,128)(2,1)} %bitcast.201), channel_id=1, source_target_pairs={{0,6},{1,7},{2,4},{3,5},{4,14},{5,15},{6,12},{7,13},{8,2},{9,3},{1... | collective-permute-start | bytes 1572872 | tf_op jit(solution)/shard_map/ppermute | solution.py:396
  171.3 60.2 %collective-permute-start.14 = (bf16[2,16,32,256]{3,2,1,0:T(8,128)(2,1)}, bf16[2,16,32,256]{3,2,1,0:T(8,128)(2,1)S(1)}, u32[]{:S(2)}, u32[]{:S(2)}) collective-permute-start(bf16[2,16,32,256]{3,2,1,0:T(8,128)(2,1)} %bitcast.200), channel_id=1, source_target_pairs={{0,7},{1,4},{2,5},{3,6},{4,15},{5,12},{6,13},{7,14},{8,3},{9,0},{1... | collective-permute-start | bytes 1572872 | tf_op jit(solution)/shard_map/ppermute | solution.py:396
  229.5 67.6 %collective-permute-start.34 = (bf16[2,16,32,256]{3,2,1,0:T(8,128)(2,1)}, bf16[2,16,32,256]{3,2,1,0:T(8,128)(2,1)}, u32[]{:S(2)}, u32[]{:S(2)}) collective-permute-start(bf16[2,16,32,256]{3,2,1,0:T(8,128)(2,1)} %bitcast.246), channel_id=1, source_target_pairs={{0,13},{1,14},{2,15},{3,12},{4,9},{5,10},{6,11},{7,8},{8,5},{9,6},... | collective-permute-start | bytes 1572872 | tf_op jit(solution)/shard_map/ppermute | solution.py:396
  231.5 71.0 %collective-permute-start.35 = (bf16[2,16,32,256]{3,2,1,0:T(8,128)(2,1)}, bf16[2,16,32,256]{3,2,1,0:T(8,128)(2,1)}, u32[]{:S(2)}, u32[]{:S(2)}) collective-permute-start(bf16[2,16,32,256]{3,2,1,0:T(8,128)(2,1)} %bitcast.243), channel_id=1, source_target_pairs={{0,14},{1,15},{2,12},{3,13},{4,10},{5,11},{6,8},{7,9},{8,6},{9,7},... | collective-permute-start | bytes 1572872 | tf_op jit(solution)/shard_map/ppermute | solution.py:396
  233.7 91.5 %collective-permute-start.36 = (bf16[2,16,32,256]{3,2,1,0:T(8,128)(2,1)}, bf16[2,16,32,256]{3,2,1,0:T(8,128)(2,1)}, u32[]{:S(2)}, u32[]{:S(2)}) collective-permute-start(bf16[2,16,32,256]{3,2,1,0:T(8,128)(2,1)} %bitcast.241), channel_id=1, source_target_pairs={{0,15},{1,12},{2,13},{3,14},{4,11},{5,8},{6,9},{7,10},{8,7},{9,4},... | collective-permute-start | bytes 1572872 | tf_op jit(solution)/shard_map/ppermute | solution.py:396
  235.4 110.3 %collective-permute-start.37 = (bf16[2,16,32,256]{3,2,1,0:T(8,128)(2,1)}, bf16[2,16,32,256]{3,2,1,0:T(8,128)(2,1)}, u32[]{:S(2)}, u32[]{:S(2)}) collective-permute-start(bf16[2,16,32,256]{3,2,1,0:T(8,128)(2,1)} %bitcast.239), channel_id=1, source_target_pairs={{0,8},{1,9},{2,10},{3,11},{4,0},{5,1},{6,2},{7,3},{8,12},{9,13},{1... | collective-permute-start | bytes 1572872 | tf_op jit(solution)/shard_map/ppermute | solution.py:396
  235.5 111.4 %collective-permute-start.38 = (bf16[2,16,32,256]{3,2,1,0:T(8,128)(2,1)}, bf16[2,16,32,256]{3,2,1,0:T(8,128)(2,1)}, u32[]{:S(2)}, u32[]{:S(2)}) collective-permute-start(bf16[2,16,32,256]{3,2,1,0:T(8,128)(2,1)} %bitcast.237), channel_id=1, source_target_pairs={{0,9},{1,10},{2,11},{3,8},{4,1},{5,2},{6,3},{7,0},{8,13},{9,14},{1... | collective-permute-start | bytes 1572872 | tf_op jit(solution)/shard_map/ppermute | solution.py:396
  297.2 84.3 %collective-permute-start.39 = (bf16[2,16,32,256]{3,2,1,0:T(8,128)(2,1)S(1)}, bf16[2,16,32,256]{3,2,1,0:T(8,128)(2,1)S(1)}, u32[]{:S(2)}, u32[]{:S(2)}) collective-permute-start(bf16[2,16,32,256]{3,2,1,0:T(8,128)(2,1)S(1)} %bitcast.242), channel_id=1, source_target_pairs={{0,10},{1,11},{2,8},{3,9},{4,2},{5,3},{6,0},{7,1},{8,14},{9,15},{1... | collective-permute-start | bytes 1572872 | tf_op jit(solution)/shard_map/ppermute | solution.py:396
  302.4 79.8 %collective-permute-start.40 = (bf16[2,16,32,256]{3,2,1,0:T(8,128)(2,1)S(1)}, bf16[2,16,32,256]{3,2,1,0:T(8,128)(2,1)S(1)}, u32[]{:S(2)}, u32[]{:S(2)}) collective-permute-start(bf16[2,16,32,256]{3,2,1,0:T(8,128)(2,1)S(1)} %bitcast.240), channel_id=1, source_target_pairs={{0,11},{1,8},{2,9},{3,10},{4,3},{5,0},{6,1},{7,2},{8,15},{9,12},{1... | collective-permute-start | bytes 1572872 | tf_op jit(solution)/shard_map/ppermute | solution.py:396
  325.2 60.0 %collective-permute-start.41 = (bf16[2,16,32,256]{3,2,1,0:T(8,128)(2,1)S(1)}, bf16[2,16,32,256]{3,2,1,0:T(8,128)(2,1)S(1)}, u32[]{:S(2)}, u32[]{:S(2)}) collective-permute-start(bf16[2,16,32,256]{3,2,1,0:T(8,128)(2,1)S(1)} %bitcast.238), channel_id=1, source_target_pairs={{0,4},{1,5},{2,6},{3,7},{4,12},{5,13},{6,14},{7,15},{8,0},{9,1},{1... | collective-permute-start | bytes 1572872 | tf_op jit(solution)/shard_map/ppermute | solution.py:396
  412.5 68.8 %collective-permute-start.63 = (bf16[2,24,16,256]{3,2,1,0:T(8,128)(2,1)}, bf16[2,24,16,256]{3,2,1,0:T(8,128)(2,1)S(1)}, u32[]{:S(2)}, u32[]{:S(2)}) collective-permute-start(bf16[2,24,16,256]{3,2,1,0:T(8,128)(2,1)} %get-tuple-element.102), channel_id=1, source_target_pairs={{0,3},{1,0},{2,1},{3,2},{4,7},{5,4},{6,5},{7,6},{8,11},{9,8},{10,9... | collective-permute-start | bytes 1179656 | tf_op jit(solution)/shard_map/ppermute | solution.py:396
  412.8 70.9 %collective-permute-start.64 = (bf16[2,24,16,256]{3,2,1,0:T(8,128)(2,1)}, bf16[2,24,16,256]{3,2,1,0:T(8,128)(2,1)S(1)}, u32[]{:S(2)}, u32[]{:S(2)}) collective-permute-start(bf16[2,24,16,256]{3,2,1,0:T(8,128)(2,1)} %get-tuple-element.103), channel_id=1, source_target_pairs={{0,13},{1,14},{2,15},{3,12},{4,9},{5,10},{6,11},{7,8},{8,5},{9,6},... | collective-permute-start | bytes 1179656 | tf_op jit(solution)/shard_map/ppermute | solution.py:396
  423.6 62.1 %collective-permute-start.65 = (bf16[2,24,16,256]{3,2,1,0:T(8,128)(2,1)}, bf16[2,24,16,256]{3,2,1,0:T(8,128)(2,1)S(1)}, u32[]{:S(2)}, u32[]{:S(2)}) collective-permute-start(bf16[2,24,16,256]{3,2,1,0:T(8,128)(2,1)} %get-tuple-element.104), channel_id=1, source_target_pairs={{0,14},{1,15},{2,12},{3,13},{4,10},{5,11},{6,8},{7,9},{8,6},{9,7},... | collective-permute-start | bytes 1179656 | tf_op jit(solution)/shard_map/ppermute | solution.py:396
  424.6 63.3 %collective-permute-start.66 = (bf16[2,24,16,256]{3,2,1,0:T(8,128)(2,1)}, bf16[2,24,16,256]{3,2,1,0:T(8,128)(2,1)S(1)}, u32[]{:S(2)}, u32[]{:S(2)}) collective-permute-start(bf16[2,24,16,256]{3,2,1,0:T(8,128)(2,1)} %get-tuple-element.105), channel_id=1, source_target_pairs={{0,15},{1,12},{2,13},{3,14},{4,11},{5,8},{6,9},{7,10},{8,7},{9,4},... | collective-permute-start | bytes 1179656 | tf_op jit(solution)/shard_map/ppermute | solution.py:396
  443.9 73.7 %collective-permute-start.67 = (bf16[2,24,16,256]{3,2,1,0:T(8,128)(2,1)}, bf16[2,24,16,256]{3,2,1,0:T(8,128)(2,1)S(1)}, u32[]{:S(2)}, u32[]{:S(2)}) collective-permute-start(bf16[2,24,16,256]{3,2,1,0:T(8,128)(2,1)} %get-tuple-element.106), channel_id=1, source_target_pairs={{0,8},{1,9},{2,10},{3,11},{4,0},{5,1},{6,2},{7,3},{8,12},{9,13},{1... | collective-permute-start | bytes 1179656 | tf_op jit(solution)/shard_map/ppermute | solution.py:396
  485.7 65.7 %collective-permute-start.70 = (bf16[2,24,16,256]{3,2,1,0:T(8,128)(2,1)}, bf16[2,24,16,256]{3,2,1,0:T(8,128)(2,1)S(1)}, u32[]{:S(2)}, u32[]{:S(2)}) collective-permute-start(bf16[2,24,16,256]{3,2,1,0:T(8,128)(2,1)} %get-tuple-element.109), channel_id=1, source_target_pairs={{0,11},{1,8},{2,9},{3,10},{4,3},{5,0},{6,1},{7,2},{8,15},{9,12},{1... | collective-permute-start | bytes 1179656 | tf_op jit(solution)/shard_map/ppermute | solution.py:396
  487.9 66.0 %collective-permute-start.71 = (bf16[2,24,16,256]{3,2,1,0:T(8,128)(2,1)}, bf16[2,24,16,256]{3,2,1,0:T(8,128)(2,1)S(1)}, u32[]{:S(2)}, u32[]{:S(2)}) collective-permute-start(bf16[2,24,16,256]{3,2,1,0:T(8,128)(2,1)} %get-tuple-element.110), channel_id=1, source_target_pairs={{0,4},{1,5},{2,6},{3,7},{4,12},{5,13},{6,14},{7,15},{8,0},{9,1},{1... | collective-permute-start | bytes 1179656 | tf_op jit(solution)/shard_map/ppermute | solution.py:396
  555.8 60.7 %collective-permute-start.48 = (bf16[2,32,16,256]{3,2,1,0:T(8,128)(2,1)}, bf16[2,32,16,256]{3,2,1,0:T(8,128)(2,1)S(1)}, u32[]{:S(2)}, u32[]{:S(2)}) collective-permute-start(bf16[2,32,16,256]{3,2,1,0:T(8,128)(2,1)} %get-tuple-element.84), channel_id=1, source_target_pairs={{0,3},{1,0},{2,1},{3,2},{4,7},{5,4},{6,5},{7,6},{8,11},{9,8},{10,9... | collective-permute-start | bytes 1572872 | tf_op jit(solution)/shard_map/ppermute | solution.py:396
  555.8 60.7 %collective-permute-start.49 = (bf16[2,32,16,256]{3,2,1,0:T(8,128)(2,1)}, bf16[2,32,16,256]{3,2,1,0:T(8,128)(2,1)S(1)}, u32[]{:S(2)}, u32[]{:S(2)}) collective-permute-start(bf16[2,32,16,256]{3,2,1,0:T(8,128)(2,1)} %get-tuple-element.85), channel_id=1, source_target_pairs={{0,13},{1,14},{2,15},{3,12},{4,9},{5,10},{6,11},{7,8},{8,5},{9,6},... | collective-permute-start | bytes 1572872 | tf_op jit(solution)/shard_map/ppermute | solution.py:396
  566.4 81.3 %collective-permute-start.50 = (bf16[2,32,16,256]{3,2,1,0:T(8,128)(2,1)}, bf16[2,32,16,256]{3,2,1,0:T(8,128)(2,1)S(1)}, u32[]{:S(2)}, u32[]{:S(2)}) collective-permute-start(bf16[2,32,16,256]{3,2,1,0:T(8,128)(2,1)} %get-tuple-element.86), channel_id=1, source_target_pairs={{0,14},{1,15},{2,12},{3,13},{4,10},{5,11},{6,8},{7,9},{8,6},{9,7},... | collective-permute-start | bytes 1572872 | tf_op jit(solution)/shard_map/ppermute | solution.py:396
  569.5 101.3 %collective-permute-start.51 = (bf16[2,32,16,256]{3,2,1,0:T(8,128)(2,1)}, bf16[2,32,16,256]{3,2,1,0:T(8,128)(2,1)S(1)}, u32[]{:S(2)}, u32[]{:S(2)}) collective-permute-start(bf16[2,32,16,256]{3,2,1,0:T(8,128)(2,1)} %get-tuple-element.87), channel_id=1, source_target_pairs={{0,15},{1,12},{2,13},{3,14},{4,11},{5,8},{6,9},{7,10},{8,7},{9,4},... | collective-permute-start | bytes 1572872 | tf_op jit(solution)/shard_map/ppermute | solution.py:396
  600.1 91.6 %collective-permute-start.52 = (bf16[2,32,16,256]{3,2,1,0:T(8,128)(2,1)}, bf16[2,32,16,256]{3,2,1,0:T(8,128)(2,1)S(1)}, u32[]{:S(2)}, u32[]{:S(2)}) collective-permute-start(bf16[2,32,16,256]{3,2,1,0:T(8,128)(2,1)} %get-tuple-element.88), channel_id=1, source_target_pairs={{0,8},{1,9},{2,10},{3,11},{4,0},{5,1},{6,2},{7,3},{8,12},{9,13},{1... | collective-permute-start | bytes 1572872 | tf_op jit(solution)/shard_map/ppermute | solution.py:396
  616.5 75.9 %collective-permute-start.53 = (bf16[2,32,16,256]{3,2,1,0:T(8,128)(2,1)}, bf16[2,32,16,256]{3,2,1,0:T(8,128)(2,1)S(1)}, u32[]{:S(2)}, u32[]{:S(2)}) collective-permute-start(bf16[2,32,16,256]{3,2,1,0:T(8,128)(2,1)} %get-tuple-element.89), channel_id=1, source_target_pairs={{0,9},{1,10},{2,11},{3,8},{4,1},{5,2},{6,3},{7,0},{8,13},{9,14},{1... | collective-permute-start | bytes 1572872 | tf_op jit(solution)/shard_map/ppermute | solution.py:396
  616.5 76.9 %collective-permute-start.54 = (bf16[2,32,16,256]{3,2,1,0:T(8,128)(2,1)}, bf16[2,32,16,256]{3,2,1,0:T(8,128)(2,1)S(1)}, u32[]{:S(2)}, u32[]{:S(2)}) collective-permute-start(bf16[2,32,16,256]{3,2,1,0:T(8,128)(2,1)} %get-tuple-element.90), channel_id=1, source_target_pairs={{0,10},{1,11},{2,8},{3,9},{4,2},{5,3},{6,0},{7,1},{8,14},{9,15},{1... | collective-permute-start | bytes 1572872 | tf_op jit(solution)/shard_map/ppermute | solution.py:396
  694.3 76.1 %collective-permute-start.25 = (bf16[2,8,16,256]{3,2,1,0:T(8,128)(2,1)}, bf16[2,8,16,256]{3,2,1,0:T(8,128)(2,1)S(1)}, u32[]{:S(2)}, u32[]{:S(2)}) collective-permute-start(bf16[2,8,16,256]{3,2,1,0:T(8,128)(2,1)} %get-tuple-element.74), channel_id=1, source_target_pairs={{0,11},{1,8},{2,9},{3,10},{4,3},{5,0},{6,1},{7,2},{8,15},{9,12},{1... | collective-permute-start | bytes 393224 | tf_op jit(solution)/shard_map/ppermute | solution.py:396
  704.5 65.8 %collective-permute-start.26 = (bf16[2,8,16,256]{3,2,1,0:T(8,128)(2,1)}, bf16[2,8,16,256]{3,2,1,0:T(8,128)(2,1)S(1)}, u32[]{:S(2)}, u32[]{:S(2)}) collective-permute-start(bf16[2,8,16,256]{3,2,1,0:T(8,128)(2,1)} %get-tuple-element.75), channel_id=1, source_target_pairs={{0,4},{1,5},{2,6},{3,7},{4,12},{5,13},{6,14},{7,15},{8,0},{9,1},{1... | collective-permute-start | bytes 393224 | tf_op jit(solution)/shard_map/ppermute | solution.py:396
  (140 other events, 7646.2 us)
